TPU v7x, 32 devices: a whole 2x2x4 slice. The times are simulated.
32 devices in a mesh: fsdp: 4 (over z), lat: 8 (over y, x, core).
Axes of the slice: x: 2, y: 2, z: 4, core: 2. Of those that a mesh axis runs over, the one named last changes fastest.
Arguments:
- fields: bfloat16 [4, 128, 360, 192], P('fsdp', 'lat'), may hold values from -6 to 6
- cotangent: bfloat16 [4, 128, 360, 192], P('fsdp', 'lat'), may hold values from -6 to 6
- kernel_one: bfloat16 [3, 3, 192, 192], P(None, None, None, 'fsdp'), may hold values from -0.15625 to 0.15625
- kernel_two: bfloat16 [3, 3, 192, 192], P(None, None, None, 'fsdp'), may hold values from -0.15625 to 0.15625
Outputs:
- block_out: bfloat16 [4, 128, 360, 192], P('fsdp', 'lat')
- field_grad: bfloat16 [4, 128, 360, 192], P('fsdp', 'lat')
- grad_one: float32 [3, 3, 192, 192], P(None, None, None, 'fsdp')
- grad_two: float32 [3, 3, 192, 192], P(None, None, None, 'fsdp')
All inputs are finite; a program needn't handle non-finite values.
Results may differ from a plain program's by a relative error of at most 0.0033.
Values may be sent and summed in bfloat16 or wider, within the bound.
No kernel may reach another device: no remote copies, remote signals or barrier semaphores. Data moves between devices by JAX's collectives and lax.ppermute only.
A program may use at most 128 MiB of HBM per device.

v0:
```python
import jax
import jax.numpy as jnp
from jax import lax
from jax.sharding import PartitionSpec as P


def extended(cells, sides, width):
    for axis, dim in sides:
        count = lax.axis_size(axis)
        ends = count - 1
        head = lax.slice_in_dim(cells, 0, width, axis=dim)
        tail = lax.slice_in_dim(cells, cells.shape[dim] - width, cells.shape[dim], axis=dim)
        cells = jnp.concatenate(
            [
                lax.ppermute(tail, axis, [(i, (i + 1) % count) for i in range(ends)]),
                cells,
                lax.ppermute(head, axis, [((i + 1) % count, i) for i in range(ends)]),
            ],
            axis=dim,
        )
    return cells


def wrap_longitude(values):
    return jnp.concatenate([values[:, :, -2:], values, values[:, :, :2]], axis=2)


def padded_rows(values):
    return wrap_longitude(extended(values, (("lat", 1),), 2))


def correlate(padded, kernel):
    return lax.conv_general_dilated(
        padded,
        kernel,
        (1, 1),
        "VALID",
        rhs_dilation=(2, 2),
        dimension_numbers=("NHWC", "HWIO", "NHWC"),
        preferred_element_type=jnp.float32,
    )


def adjoint_kernel(kernel):
    return jnp.transpose(kernel[::-1, ::-1], (0, 1, 3, 2))


def normal_cdf(values):
    return 0.5 * (1.0 + jax.scipy.special.erf(values * 0.7071067811865476))


def kernel_terms(padded, grad_field, height, width_cells):
    return jnp.stack(
        [
            jnp.stack(
                [
                    jnp.einsum(
                        "nhwc,nhwd->cd",
                        padded[:, 2 * a : 2 * a + height, 2 * b : 2 * b + width_cells],
                        grad_field,
                        preferred_element_type=jnp.float32,
                    )
                    for b in range(3)
                ]
            )
            for a in range(3)
        ]
    )


def per_device(fields, cotangent, kernel_one, kernel_two):
    height = fields.shape[1]
    width_cells = fields.shape[2]
    cell_count = (
        lax.axis_size("fsdp") * fields.shape[0] * lax.axis_size("lat") * height * width_cells
    )
    factor = 1.0 / jnp.sqrt(jnp.float32(cell_count))
    full_one, full_two = (
        lax.all_gather(kernel_one, "fsdp", axis=3, tiled=True),
        lax.all_gather(kernel_two, "fsdp", axis=3, tiled=True),
    )
    source_pad = padded_rows(fields)
    preact = correlate(source_pad, full_one)
    hidden = (preact * normal_cdf(preact)).astype(jnp.bfloat16)
    hidden_pad = padded_rows(hidden)
    block_out = (fields.astype(jnp.float32) + correlate(hidden_pad, full_two)).astype(jnp.bfloat16)
    back = correlate(padded_rows(cotangent), adjoint_kernel(full_two))
    slope = normal_cdf(preact) + preact * jnp.exp(-0.5 * preact * preact) * 0.3989422804014327
    inner_grad = (back * slope).astype(jnp.bfloat16)
    field_grad = (
        cotangent.astype(jnp.float32) + correlate(padded_rows(inner_grad), adjoint_kernel(full_one))
    ).astype(jnp.bfloat16)
    terms_two = kernel_terms(hidden_pad, cotangent, height, width_cells) * factor
    terms_one = kernel_terms(source_pad, inner_grad, height, width_cells) * factor
    share_one, share_two = (
        lax.psum_scatter(terms_one, "fsdp", scatter_dimension=3, tiled=True),
        lax.psum_scatter(terms_two, "fsdp", scatter_dimension=3, tiled=True),
    )
    grad_one, grad_two = lax.psum((share_one, share_two), "lat")
    return (block_out, field_grad, grad_one, grad_two)


def solution(mesh):
    placed = (
        P("fsdp", "lat", None, None),
        P("fsdp", "lat", None, None),
        P(None, None, None, "fsdp"),
        P(None, None, None, "fsdp"),
    )
    return jax.shard_map(
        per_device,
        mesh=mesh,
        in_specs=placed,
        out_specs=(
            P("fsdp", "lat", None, None),
            P("fsdp", "lat", None, None),
            P(None, None, None, "fsdp"),
            P(None, None, None, "fsdp"),
        ),
        check_vma=False,
    )
```

profile of v0, /device:TPU:0, one launch (start us, length us, event | category | flops | bytes accessed | tf_op | source)
XLA Modules:
  0.0 520.9 jit_solution(12465785678488781029)
XLA Ops:
  7.2 1.9 fusion.228
  10.4 3.0 collective-permute-start
  13.5 1.9 fusion.227
  16.7 5.2 %collective-permute-start.4 = (bf16[1,2,360,192]{2,3,1,0:T(8,128)(2,1)}, bf16[1,2,360,192]{2,3,1,0:T(8,128)(2,1)S(1)}, u32[]{:S(2)}, u32[]{:S(2)}) collective-permute-start(bf16[1,2,360,192]{2,3,1,0:T(8,128)(2,1)} %get-tuple-element.33), channel_id=1, source_target_pairs={{0,1},{1,2},{2,3},{3,4},{4,5},{5,6},{6,7},{8,9},{9,10},{10,11},{11... | collective-permute-start | bytes 829448 | tf_op jit(solution)/shard_map/ppermute | solution.py:15
  21.9 21.1 %all_gather.6 = bf16[3,3,192,192]{2,3,1,0:T(8,128)(2,1)} all-gather(bf16[3,3,192,48]{2,3,1,0:T(8,128)(2,1)} %param.6), channel_id=1, replica_groups=mesh['fsdp'=4,'lat'=8] {'fsdp'}, dimensions={3}, use_global_device_ids=true | all-gather | bytes 829440 | tf_op jit(solution)/shard_map/all_gather | solution.py:79
  43.0 4.9 copy.44
  47.9 3.5 copy.58
  52.7 20.2 %all_gather.7 = bf16[3,3,192,192]{2,3,1,0:T(8,128)(2,1)} all-gather(bf16[3,3,192,48]{2,3,1,0:T(8,128)(2,1)} %param.7), channel_id=1, replica_groups=mesh['fsdp'=4,'lat'=8] {'fsdp'}, dimensions={3}, use_global_device_ids=true | all-gather | bytes 829440 | tf_op jit(solution)/shard_map/all_gather | solution.py:80
  76.6 2.0 maximum_bitcast_fusion.2
  79.0 2.0 maximum_bitcast_fusion
  81.0 2.0 pad
  83.0 11.4 %reshape.194 = bf16[20,1,8,46,192]{3,2,4,0,1:T(8,128)(2,1)} reshape(bf16[20,1,368,192]{2,3,0,1:T(8,128)(2,1)} %pad) | data formatting | bytes 5652480 | tf_op jit(solution)/shard_map/conv_general_dilated | solution.py:33
  94.4 11.8 %copy.47 = bf16[20,1,8,46,192]{4,2,3,0,1:T(8,128)(2,1)} copy(bf16[20,1,8,46,192]{3,2,4,0,1:T(8,128)(2,1)} %reshape.194) | data formatting | bytes 5652480 | tf_op jit(solution)/shard_map/conv_general_dilated | solution.py:33
  107.3 8.6 %reshape.196 = bf16[20,1,8,46,192]{3,2,4,0,1:T(8,128)(2,1)} reshape(bf16[20,1,368,192]{2,3,0,1:T(8,128)(2,1)S(1)} %pad.4) | data formatting | bytes 5652480 | tf_op jit(solution)/shard_map/conv_general_dilated | solution.py:33
  115.9 11.8 %copy.61 = bf16[20,1,8,46,192]{4,2,3,0,1:T(8,128)(2,1)} copy(bf16[20,1,8,46,192]{3,2,4,0,1:T(8,128)(2,1)} %reshape.196) | data formatting | bytes 5652480 | tf_op jit(solution)/shard_map/conv_general_dilated | solution.py:33
  128.8 12.3 %multiply_convert_fusion = (bf16[16,8,46,192]{3,1,2,0:T(8,128)(2,1)}, f32[16,8,46,192]{3,1,2,0:T(8,128)S(1)}) fusion(pred[8,46]{0,1:T(8,128)(4,1)S(1)} %copy-done.35, bf16[3,3,192,192]{2,3,1,0:T(8,128)(2,1)S(1)} %copy-done.20, bf16[20,1,7,4,192]{4,2,3,0,1:T(8,128)(2,1)S(1)} %slice.162, bf16[20,1,8,46,192]{4,2,3,0,1:T(8,128)(2,1)} %copy.47), kind=kOutput, calls=%fused_computation.12 | convolution fusion | flops 3922993152 | bytes 10488176 | tf_op jit(solution)/shard_map/conv_general_dilated | solution.py:33
  141.1 10.2 %fusion.9 = bf16[16,8,46,192]{3,1,2,0:T(8,128)(2,1)S(1)} fusion(f32[16,8,46,192]{3,1,2,0:T(8,128)S(1)} %get-tuple-element.37, pred[8,46]{0,1:T(8,128)(4,1)S(1)} %copy-done.35, bf16[3,3,192,192]{2,3,1,0:T(8,128)(2,1)S(1)} %copy-done.22, bf16[20,1,7,4,192]{4,2,3,0,1:T(8,128)(2,1)S(1)} %slice.172, bf16[20,1,8,46,192]{4,2,3,0,1:T(8,128)(2,1)S(1)} %copy-done.15), kind=kOutput, calls=%fused_computation.11 | convolution fusion | flops 3929776128 | bytes 10488176 | tf_op jit(solution)/shard_map/conv_general_dilated | solution.py:33
  153.4 1.8 slice.175
  155.2 4.3 copy.98
  159.6 4.5 fusion.191
  164.0 1.8 fusion.186
  165.8 1.5 fusion.123
  167.3 1.9 fusion.196
  169.2 1.9 fusion.166
  171.1 1.8 fusion.156
  172.9 1.8 fusion.181
  175.6 2.6 copy.50
  178.2 1.6 copy.82
  181.1 1.7 slice_bitcast_fusion.27
  182.8 2.3 collective-permute-start.6
  185.1 2.5 fusion.161
  190.5 4.4 copy.73
  194.9 1.8 slice.165
  196.7 3.7 copy.97
  202.3 4.2 collective-permute-start.2
  206.6 1.6 copy.81
  209.4 1.7 slice_bitcast_fusion.28
  212.4 1.6 copy.83
  217.5 2.5 fusion.128
  221.5 4.7 maximum_maximum_fusion
  232.5 5.0 fusion.43
  237.5 2.0 pad.6
  239.5 3.8 maximum_bitcast_fusion.1
  243.3 2.0 pad.2
  245.2 1.8 fusion.176
  249.4 4.2 copy.74
  253.6 8.6 %reshape.195 = bf16[20,1,8,46,192]{3,2,4,0,1:T(8,128)(2,1)} reshape(bf16[20,1,368,192]{2,3,0,1:T(8,128)(2,1)S(1)} %copy-done.11) | data formatting | bytes 5652480 | tf_op jit(solution)/shard_map/conv_general_dilated | solution.py:33
  262.1 11.8 %copy.56 = bf16[20,1,8,46,192]{4,2,3,0,1:T(8,128)(2,1)} copy(bf16[20,1,8,46,192]{3,2,4,0,1:T(8,128)(2,1)} %reshape.195) | data formatting | bytes 5652480 | tf_op jit(solution)/shard_map/conv_general_dilated | solution.py:33
  275.5 9.8 %broadcast_select_fusion.1 = f32[16,8,46,192]{3,1,2,0:T(8,128)S(1)} fusion(pred[8,46]{0,1:T(8,128)(4,1)S(1)} %copy-done.35, bf16[3,3,192,192]{2,3,1,0:T(8,128)(2,1)S(1)} %copy-done.23, bf16[20,1,7,4,192]{4,2,3,0,1:T(8,128)(2,1)S(1)} %slice.168, bf16[20,1,8,46,192]{4,2,3,0,1:T(8,128)(2,1)} %copy.56), kind=kOutput, calls=%fused_computation.49 | convolution fusion | flops 3917340672 | bytes 8227184 | tf_op jit(solution)/shard_map/conv_general_dilated | solution.py:33
  285.3 3.5 copy.57
  288.8 2.6 fusion.13
  291.4 4.8 copy.75
  296.3 8.6 %reshape.197 = bf16[20,1,8,46,192]{3,2,4,0,1:T(8,128)(2,1)} reshape(bf16[20,1,368,192]{2,3,0,1:T(8,128)(2,1)S(1)} %copy-done.10) | data formatting | bytes 5652480 | tf_op jit(solution)/shard_map/conv_general_dilated | solution.py:33
  304.8 12.0 %copy.70 = bf16[20,1,8,46,192]{4,2,3,0,1:T(8,128)(2,1)} copy(bf16[20,1,8,46,192]{3,2,4,0,1:T(8,128)(2,1)} %reshape.197) | data formatting | bytes 5652480 | tf_op jit(solution)/shard_map/conv_general_dilated | solution.py:33
  317.9 9.1 %broadcast_select_fusion = f32[16,8,46,192]{3,1,2,0:T(8,128)S(1)} fusion(pred[8,46]{0,1:T(8,128)(4,1)S(1)} %copy-done.35, bf16[3,3,192,192]{2,3,1,0:T(8,128)(2,1)S(1)} %copy-done.21, bf16[20,1,7,4,192]{4,2,3,0,1:T(8,128)(2,1)S(1)} %slice.178, bf16[20,1,8,46,192]{4,2,3,0,1:T(8,128)(2,1)} %copy.70), kind=kOutput, calls=%fused_computation.48 | convolution fusion | flops 3917340672 | bytes 8227184 | tf_op jit(solution)/shard_map/conv_general_dilated | solution.py:33
  327.0 6.1 %copy.71 = f32[16,8,46,192]{3,0,2,1:T(8,128)} copy(f32[16,8,46,192]{3,1,2,0:T(8,128)S(1)} %broadcast_select_fusion) | data formatting | bytes 9043968 | tf_op jit(solution)/shard_map/conv_general_dilated | solution.py:33
  333.1 116.7 %all-reduce.9.cloned.1.call-done = (f32[3,3,192,192]{2,1,0,3:T(4,128)}, f32[3,3,192,192]{2,1,0,3:T(4,128)}) async-done(((f32[3,3,192,192]{2,1,0,3:T(4,128)}, f32[3,3,192,192]{2,1,0,3:T(4,128)}), (f32[3,3,192,192]{2,1,0,3:T(4,128)}, f32[3,3,192,192]{2,1,0,3:T(4,128)})) %all-reduce.9.cloned.1.call-update) | async-done | bytes 2654224
  449.7 2.0 constant_dynamic-slice_fusion.1
  451.7 2.0 constant_dynamic-slice_fusion
  453.8 5.3 %fusion.11 = bf16[1,16,360,192]{3,1,2,0:T(8,128)(2,1)} fusion(f32[16,1,368,192]{3,0,2,1:T(8,128)} %bitcast.330, bf16[1,16,360,192]{3,1,2,0:T(8,128)(2,1)S(1)} %copy-done.8), kind=kLoop, calls=%fused_computation.16 | loop fusion | flops 3317760 | bytes 8847360 | tf_op jit(solution)/shard_map/convert_element_type | solution.py:92
  459.1 4.7 copy.76
  463.8 46.3 %all-reduce.7.cloned.1.call-done = (f32[3,3,192,48]{2,1,0,3:T(4,128)}, f32[3,3,192,48]{2,1,0,3:T(4,128)}) async-done(((f32[3,3,192,48]{2,1,0,3:T(4,128)}, f32[3,3,192,48]{2,1,0,3:T(4,128)}), (f32[3,3,192,48]{2,1,0,3:T(4,128)}, f32[3,3,192,48]{2,1,0,3:T(4,128)})) %all-reduce.7.cloned.1.call-update) | async-done | bytes 663568 | tf_op jit(solution)/shard_map/psum | solution.py:99
  510.1 1.9 copy.77
  512.0 1.9 copy.78
  (127 shorter events, 36.9 us)
Async XLA Ops:
  7.2 442.6 %all-reduce.9.cloned.1.call-start = ((), (), s32[]{:S(2)}) async-start(), calls=%async_computation.1 | async-start | bytes 9437184
  9.1 66.7 %collective-permute-start.1 = (bf16[1,2,360,192]{2,3,1,0:T(8,128)(2,1)}, bf16[1,2,360,192]{2,3,1,0:T(8,128)(2,1)S(1)}, u32[]{:S(2)}, u32[]{:S(2)}) collective-permute-start(bf16[1,2,360,192]{2,3,1,0:T(8,128)(2,1)} %get-tuple-element.34), channel_id=1, source_target_pairs={{1,0},{2,1},{3,2},{4,3},{5,4},{6,5},{7,6},{9,8},{10,9},{11,10},{12... | collective-permute-start | bytes 829448 | tf_op jit(solution)/shard_map/ppermute | solution.py:17
  10.4 63.1 %collective-permute-start = (bf16[1,2,360,192]{2,3,1,0:T(8,128)(2,1)}, bf16[1,2,360,192]{2,3,1,0:T(8,128)(2,1)S(1)}, u32[]{:S(2)}, u32[]{:S(2)}) collective-permute-start(bf16[1,2,360,192]{2,3,1,0:T(8,128)(2,1)} %get-tuple-element.35), channel_id=1, source_target_pairs={{0,1},{1,2},{2,3},{3,4},{4,5},{5,6},{6,7},{8,9},{9,10},{10,11},{11... | collective-permute-start | bytes 829448 | tf_op jit(solution)/shard_map/ppermute | solution.py:15
  15.4 59.8 %collective-permute-start.5 = (bf16[1,2,360,192]{2,3,1,0:T(8,128)(2,1)}, bf16[1,2,360,192]{2,3,1,0:T(8,128)(2,1)S(1)}, u32[]{:S(2)}, u32[]{:S(2)}) collective-permute-start(bf16[1,2,360,192]{2,3,1,0:T(8,128)(2,1)} %get-tuple-element.32), channel_id=1, source_target_pairs={{1,0},{2,1},{3,2},{4,3},{5,4},{6,5},{7,6},{9,8},{10,9},{11,10},{12... | collective-permute-start | bytes 829448 | tf_op jit(solution)/shard_map/ppermute | solution.py:17
  16.7 31.3 %copy-start.2 = (bf16[1,16,360,192]{2,3,1,0:T(8,128)(2,1)S(1)}, bf16[1,16,360,192]{2,3,1,0:T(8,128)(2,1)}, u32[]{:S(2)}) copy-start(bf16[1,16,360,192]{2,3,1,0:T(8,128)(2,1)} %param.5) | copy-start | bytes 6635524
  16.7 56.3 %collective-permute-start.4 = (bf16[1,2,360,192]{2,3,1,0:T(8,128)(2,1)}, bf16[1,2,360,192]{2,3,1,0:T(8,128)(2,1)S(1)}, u32[]{:S(2)}, u32[]{:S(2)}) collective-permute-start(bf16[1,2,360,192]{2,3,1,0:T(8,128)(2,1)} %get-tuple-element.33), channel_id=1, source_target_pairs={{0,1},{1,2},{2,3},{3,4},{4,5},{5,6},{6,7},{8,9},{9,10},{10,11},{11... | collective-permute-start | bytes 829448 | tf_op jit(solution)/shard_map/ppermute | solution.py:15
  47.9 3.5 copy-start.34
  73.0 1.8 copy-start.4
  73.5 1.8 copy-start.25
  75.8 0.7 copy-start.27
  75.9 3.1 copy-start.12
  76.4 2.6 copy-start.16
  76.4 2.6 copy-start.18
  115.9 12.9 %copy-start.20 = (bf16[3,3,192,192]{2,3,1,0:T(8,128)(2,1)S(1)}, bf16[3,3,192,192]{2,3,1,0:T(8,128)(2,1)}, u32[]{:S(2)}) copy-start(bf16[3,3,192,192]{2,3,1,0:T(8,128)(2,1)} %all_gather.6) | copy-start | bytes 1990660
  115.9 12.9 %copy-start.35 = (pred[8,46]{0,1:T(8,128)(4,1)S(1)}, pred[8,46]{0,1:T(8,128)(4,1)}, u32[]{:S(2)}) copy-start(pred[8,46]{0,1:T(8,128)(4,1)} %constant.30) | copy-start | bytes 1108
  128.8 12.4 %copy-start.15 = (bf16[20,1,8,46,192]{4,2,3,0,1:T(8,128)(2,1)S(1)}, bf16[20,1,8,46,192]{4,2,3,0,1:T(8,128)(2,1)}, u32[]{:S(2)}) copy-start(bf16[20,1,8,46,192]{4,2,3,0,1:T(8,128)(2,1)} %copy.61) | copy-start | bytes 8478724
  128.8 12.3 %copy-start.22 = (bf16[3,3,192,192]{2,3,1,0:T(8,128)(2,1)S(1)}, bf16[3,3,192,192]{2,3,1,0:T(8,128)(2,1)}, u32[]{:S(2)}) copy-start(bf16[3,3,192,192]{2,3,1,0:T(8,128)(2,1)} %all_gather.7) | copy-start | bytes 1990660
  155.2 4.3 copy-start.19
  159.5 28.1 %copy-start = (bf16[16,1,360,192]{2,3,0,1:T(8,128)(2,1)}, bf16[16,1,360,192]{2,3,0,1:T(8,128)(2,1)S(1)}, u32[]{:S(2)}) copy-start(bf16[16,1,360,192]{2,3,0,1:T(8,128)(2,1)S(1)} %copy.98) | copy-start | bytes 6635524
  159.5 4.5 copy-start.13
  159.5 4.5 copy-start.17
  164.0 1.8 copy-start.5
  172.9 1.9 copy-start.14
  182.8 4.8 copy-start.32
  182.8 4.8 copy-start.33
  182.8 4.9 copy-start.6
  182.8 4.9 copy-start.26
  182.8 49.2 %collective-permute-start.6 = (bf16[1,2,360,192]{2,3,1,0:T(8,128)(2,1)}, bf16[1,2,360,192]{2,3,1,0:T(8,128)(2,1)}, u32[]{:S(2)}, u32[]{:S(2)}) collective-permute-start(bf16[1,2,360,192]{2,3,1,0:T(8,128)(2,1)} %slice_bitcast_fusion.27), channel_id=1, source_target_pairs={{0,1},{1,2},{2,3},{3,4},{4,5},{5,6},{6,7},{8,9},{9,10},{10,11},{11... | collective-permute-start | bytes 829448 | tf_op jit(solution)/shard_map/ppermute | solution.py:15
  187.7 0.9 copy-start.24
  187.7 1.0 copy-start.28
  187.7 1.1 copy-start.29
  187.7 1.2 copy-start.30
  187.7 1.2 copy-start.31
  190.5 4.4 copy-start.7
  202.3 17.7 %collective-permute-start.2 = (bf16[1,2,360,192]{2,3,1,0:T(8,128)(2,1)}, bf16[1,2,360,192]{2,3,1,0:T(8,128)(2,1)S(1)}, u32[]{:S(2)}, u32[]{:S(2)}) collective-permute-start(bf16[1,2,360,192]{2,3,1,0:T(8,128)(2,1)} %slice_bitcast_fusion.29), channel_id=1, source_target_pairs={{0,1},{1,2},{2,3},{3,4},{4,5},{5,6},{6,7},{8,9},{9,10},{10,11},{11... | collective-permute-start | bytes 829448 | tf_op jit(solution)/shard_map/ppermute | solution.py:15
  211.1 8.9 %collective-permute-start.3 = (bf16[1,2,360,192]{2,3,1,0:T(8,128)(2,1)}, bf16[1,2,360,192]{2,3,1,0:T(8,128)(2,1)}, u32[]{:S(2)}, u32[]{:S(2)}) collective-permute-start(bf16[1,2,360,192]{2,3,1,0:T(8,128)(2,1)} %slice_bitcast_fusion.28), channel_id=1, source_target_pairs={{1,0},{2,1},{3,2},{4,3},{5,4},{6,5},{7,6},{9,8},{10,9},{11,10},{12... | collective-permute-start | bytes 829448 | tf_op jit(solution)/shard_map/ppermute | solution.py:17
  216.2 15.7 %collective-permute-start.7 = (bf16[1,2,360,192]{2,3,1,0:T(8,128)(2,1)S(1)}, bf16[1,2,360,192]{2,3,1,0:T(8,128)(2,1)S(1)}, u32[]{:S(2)}, u32[]{:S(2)}) collective-permute-start(bf16[1,2,360,192]{2,3,1,0:T(8,128)(2,1)S(1)} %slice_bitcast_fusion.26), channel_id=1, source_target_pairs={{1,0},{2,1},{3,2},{4,3},{5,4},{6,5},{7,6},{9,8},{10,9},{11,10},{12... | collective-permute-start | bytes 829448 | tf_op jit(solution)/shard_map/ppermute | solution.py:17
  221.5 4.7 copy-start.3
  230.8 1.7 copy-start.1
  249.4 4.2 copy-start.11
  273.9 1.6 copy-start.23
  275.1 235.0 %all-reduce.7.cloned.1.call-start = ((), (), s32[]{:S(2)}) async-start(), calls=%async_computation | async-start | bytes 2359296 | tf_op jit(solution)/shard_map/psum | solution.py:99
  285.3 3.5 copy-start.9
  291.4 4.8 copy-start.10
  304.8 13.1 %copy-start.21 = (bf16[3,3,192,192]{2,3,1,0:T(8,128)(2,1)S(1)}, bf16[3,3,192,192]{2,3,1,0:T(8,128)(2,1)}, u32[]{:S(2)}) copy-start(bf16[3,3,192,192]{2,3,1,0:T(8,128)(2,1)} %all_gather.6) | copy-start | bytes 1990660
  333.1 120.7 %copy-start.8 = (bf16[1,16,360,192]{3,1,2,0:T(8,128)(2,1)S(1)}, bf16[1,16,360,192]{3,1,2,0:T(8,128)(2,1)}, u32[]{:S(2)}) copy-start(bf16[1,16,360,192]{3,1,2,0:T(8,128)(2,1)} %copy.58) | copy-start | bytes 6635524
Sparse Core Ops, SparseCore 0:
  275.2 174.4 all-reduce.8
  453.9 56.1 all-reduce.6
where the time goes:
time: 530 us; the launch traced here: 521 us
  local copies, waits for them, and re-layouts  180 us (34%)
  waiting for transfers between devices  163 us (31%)
  matrix products  70.5 us (13%)
  blocking collectives  41.3 us (8%)
  other arithmetic  30 us (6%)
  starting transfers between devices  20.4 us (4%)
  between operations  15.7 us (3%)
    unnamed x3, waiting for transfers between devices  117 us
    conv_general_dilated x14, local copies, waits for them, and re-layouts, correlate(): lax.conv_general_dilated(padded, kernel, (1, 1), 'VALID', rhs_dilation=(2...  98.3 us
    psum x1, waiting for transfers between devices, per_device(): grad_one, grad_two = lax.psum((share_one, share_two), 'lat')  46.3 us
    conv_general_dilated x4, matrix products, correlate(): lax.conv_general_dilated(padded, kernel, (1, 1), 'VALID', rhs_dilation=(2...  41.3 us
    unnamed x87, local copies, waits for them, and re-layouts  37.8 us
    dot_general x18, matrix products, kernel_terms(): jnp.einsum('nhwc,nhwd->cd', padded[:, 2 * a:2 * a + height, 2 * b:2 * b +...  29.2 us
    all_gather x1, blocking collectives, per_device(): lax.all_gather(kernel_one, 'fsdp', axis=3, tiled=True)  21.1 us
    all_gather x1, blocking collectives, per_device(): lax.all_gather(kernel_two, 'fsdp', axis=3, tiled=True)  20.2 us
  transfers between devices with their start and end apart: 10, of which 2 were waited for; matrix products, arithmetic and copies ran while one was open for 23% of the time, Pallas kernels for 0%

commit v1 on v0

v1 whole, which is shorter than its diff:
```python
import functools

import jax
import jax.numpy as jnp
from jax import lax
from jax.experimental import pallas as pl
from jax.experimental.pallas import tpu as pltpu
from jax.sharding import PartitionSpec as P

BF16 = jnp.bfloat16
F32 = jnp.float32
VMEM = pl.BlockSpec(memory_space=pltpu.VMEM)
SMEM = pl.BlockSpec(memory_space=pltpu.SMEM)
TAPS = 9
SLABS = 3 * TAPS
HALF = (SLABS + 1) // 2
LANES = 128


def call(body, name, out, specs, args, scratch=(), limit=40, flops=0, nbytes=0):
    return pl.pallas_call(
        body,
        name=name,
        out_shape=out,
        in_specs=specs,
        out_specs=jax.tree.map(lambda _: VMEM, out),
        scratch_shapes=list(scratch),
        compiler_params=pltpu.CompilerParams(vmem_limit_bytes=limit << 20),
        cost_estimate=pl.CostEstimate(flops=flops, bytes_accessed=nbytes, transcendentals=0),
    )(*args)


def padded_lanes(chan):
    return -(-chan // LANES) * LANES


def pack_body(parity, one, two, half):
    def slab(s):
        tap = s % TAPS
        if s < TAPS:
            return one[tap][:, :LANES]
        if s < 2 * TAPS:
            return two[tap][:, :LANES]
        return jnp.concatenate([one[tap][:, LANES:], two[tap][:, LANES:]], axis=1)

    for side in range(2):

        @pl.when(parity[0] == side)
        def _():
            for i in range(HALF):
                half[i] = slab(min(side * HALF + i, SLABS - 1))


def weights_body(parity, own, other, w1, w2, a1, a2):
    c = w1.shape[0]
    mine = parity[0] == 0

    def slab(s):
        side, i = divmod(s, HALF)
        first, second = (own, other) if side == 0 else (other, own)
        parts = [jnp.where(mine, first[f, i], second[f, i]) for f in range(own.shape[0])]
        return jnp.concatenate(parts, axis=0)

    for tap in range(TAPS):
        tails = slab(2 * TAPS + tap)
        rest = c - LANES
        one = jnp.concatenate([slab(tap), tails[:, :rest]], axis=1)
        two = jnp.concatenate([slab(TAPS + tap), tails[:, rest:]], axis=1)
        at = pl.ds(tap * c, c)
        back = pl.ds((TAPS - 1 - tap) * c, c)
        w1[:, at] = one
        w2[:, at] = two
        a1[:, back] = one.T
        a2[:, back] = two.T


def shifted(row, pad):
    lon = row.shape[1]
    fill = jnp.zeros((row.shape[0], pad), row.dtype)
    return (
        jnp.concatenate([row[:, lon - 2 :], row[:, : lon - 2], fill], axis=1),
        jnp.concatenate([row, fill], axis=1),
        jnp.concatenate([row[:, 2:], row[:, :2], fill], axis=1),
    )


def store_row(columns, at, row, pad):
    c = row.shape[0]
    for b, piece in enumerate(shifted(row, pad)):
        columns[at, b * c : (b + 1) * c] = piece


def taps_of(columns, at):
    return jnp.concatenate([columns[at], columns[at + 2], columns[at + 4]], axis=0)


def rows_of(columns, at, step):
    return jnp.concatenate([taps_of(columns, at + s) for s in range(step)], axis=1)


def normal_cdf(values):
    return 0.5 * (1.0 + lax.erf(values * 0.7071067811865476))


def first_body(step, fields, cot, above, below, w1, a2, fcol, ccol, hid, inn, up, down):
    height, c, lon = fields.shape
    wide = fcol.shape[2]
    pad = wide - lon
    for columns, source, base in ((fcol, fields, 0), (ccol, cot, 2)):
        for r in range(2):
            store_row(columns, r, above[base + r], pad)
            store_row(columns, height + 2 + r, below[base + r], pad)

        def fill(i, carry):
            store_row(columns, i + 2, source[i], pad)
            return carry

        lax.fori_loop(0, height, fill, 0)

    def work(t, carry):
        i = t * step
        pre = jnp.dot(w1[...], rows_of(fcol, i, step), preferred_element_type=F32)
        back = jnp.dot(a2[...], rows_of(ccol, i, step), preferred_element_type=F32)
        cdf = normal_cdf(pre)
        hidden = (pre * cdf).astype(BF16)
        slope = cdf + pre * jnp.exp(-0.5 * pre * pre) * 0.3989422804014327
        inner = (back * slope).astype(BF16)
        for s in range(step):
            hid[i + s] = hidden[:, s * wide : (s + 1) * wide]
            inn[i + s] = inner[:, s * wide : (s + 1) * wide]
        return carry

    lax.fori_loop(0, height // step, work, 0)
    for r in range(2):
        up[r] = hid[r][:, :lon]
        up[2 + r] = inn[r][:, :lon]
        down[r] = hid[height - 2 + r][:, :lon]
        down[2 + r] = inn[height - 2 + r][:, :lon]


def terms_body(step, scale, shards, fcol, ccol, hid, inn, out, g1, g2):
    height = hid.shape[0]
    c = hid.shape[1]
    g1[...] = jnp.zeros_like(g1)
    g2[...] = jnp.zeros_like(g2)
    contract = (((1,), (1,)), ((), ()))

    def work(t, carry):
        i = t * step
        for total, columns, field in ((g1, fcol, inn), (g2, ccol, hid)):
            rhs = jnp.concatenate([field[i + s] for s in range(step)], axis=1)
            total[...] += lax.dot_general(
                rows_of(columns, i, step), rhs, contract, preferred_element_type=F32
            )
        return carry

    lax.fori_loop(0, height // step, work, 0)
    share = c // shards
    depth = out.shape[3]

    def place(slab, value):
        for f in range(shards):
            start = slab * share
            while start < (slab + 1) * share:
                chunk, inside = divmod(start, depth)
                stop = min((slab + 1) * share, (chunk + 1) * depth)
                src = f * share + start - slab * share
                out[chunk % 2, chunk // 2, f, inside : inside + stop - start] = value[
                    src : src + stop - start
                ].astype(out.dtype)
                start = stop

    for tap in range(TAPS):
        one = g1[tap * c : (tap + 1) * c].T * scale
        two = g2[(TAPS - 1 - tap) * c : (TAPS - tap) * c] * scale
        place(tap, one[:, :LANES])
        place(TAPS + tap, two[:, :LANES])
        place(2 * TAPS + tap, jnp.concatenate([one[:, LANES:], two[:, LANES:]], axis=1))


def second_body(step, fields, cot, hid, inn, above, below, w2, a1, out, grad, columns):
    height, c, lon = fields.shape
    wide = columns.shape[2]
    pad = wide - lon
    for base, mid, weight, residual, result in (
        (0, hid, w2, fields, out),
        (2, inn, a1, cot, grad),
    ):
        for r in range(2):
            store_row(columns, r, above[base + r], pad)
            store_row(columns, height + 2 + r, below[base + r], pad)

        def fill(i, carry):
            store_row(columns, i + 2, mid[i][:, :lon], pad)
            return carry

        lax.fori_loop(0, height, fill, 0)

        def work(t, carry):
            i = t * step
            value = jnp.dot(weight[...], rows_of(columns, i, step), preferred_element_type=F32)
            for s in range(step):
                part = value[:, s * wide : s * wide + lon]
                result[i + s] = (residual[i + s].astype(F32) + part).astype(BF16)
            return carry

        lax.fori_loop(0, height // step, work, 0)


def unpack_body(share, chunks, one, two):
    count, depth, _ = chunks.shape
    c = one.shape[2]
    rest = c - LANES

    def rows(slab):
        parts = []
        start = slab * share
        while start < (slab + 1) * share:
            chunk, inside = divmod(start, depth)
            stop = min((slab + 1) * share, (chunk + 1) * depth)
            parts.append(chunks[chunk, inside : inside + stop - start])
            start = stop
        return parts[0] if len(parts) == 1 else jnp.concatenate(parts, axis=0)

    for tap in range(TAPS):
        tails = rows(2 * TAPS + tap)
        one[tap] = jnp.concatenate([rows(tap), tails[:, :rest]], axis=1)
        two[tap] = jnp.concatenate([rows(TAPS + tap), tails[:, rest:]], axis=1)


def shape(dims, dtype):
    return jax.ShapeDtypeStruct(dims, dtype)


def per_device(fields, cotangent, kernel_one, kernel_two):
    _, height, lon, c = fields.shape
    share = kernel_one.shape[3]
    shards = lax.axis_size("fsdp")
    bands = lax.axis_size("lat")
    wide = padded_lanes(lon)
    step = 4
    scale = 1.0 / (shards * fields.shape[0] * bands * height * lon) ** 0.5
    source = jnp.swapaxes(fields[0], 1, 2)
    upstream = jnp.swapaxes(cotangent[0], 1, 2)
    small = [
        jnp.swapaxes(k.reshape(TAPS, c, share), 1, 2) for k in (kernel_one, kernel_two)
    ]
    parity = (lax.axis_index("lat") % 2).astype(jnp.int32).reshape(1)
    forward = [(i, i + 1) for i in range(bands - 1)]
    backward = [(i + 1, i) for i in range(bands - 1)]
    swap = [(i, i ^ 1) for i in range(bands)]

    def edges(top, bottom):
        return lax.ppermute(bottom, "lat", forward), lax.ppermute(top, "lat", backward)

    above, below = edges(
        jnp.concatenate([source[:2], upstream[:2]], axis=0),
        jnp.concatenate([source[-2:], upstream[-2:]], axis=0),
    )
    half = call(
        pack_body, "pack", shape((HALF, share, LANES), BF16), [SMEM, VMEM, VMEM], (parity, *small)
    )
    own = lax.all_gather(half, "fsdp", axis=0)
    other = lax.ppermute(own, "lat", swap)
    w1, w2, a1, a2 = call(
        weights_body,
        "weights",
        [shape((c, TAPS * c), BF16)] * 4,
        [SMEM, VMEM, VMEM],
        (parity, own, other),
    )
    conv_flops = 2 * TAPS * c * c * height * lon
    columns = shape((height + 4, 3 * c, wide), BF16)
    middle = shape((height, c, wide), BF16)
    edge = shape((4, c, lon), BF16)
    fcol, ccol, hid, inn, up, down = call(
        functools.partial(first_body, step),
        "first",
        [columns, columns, middle, middle, edge, edge],
        [VMEM] * 6,
        (source, upstream, above, below, w1, a2),
        limit=20,
        flops=2 * conv_flops,
        nbytes=1 << 24,
    )
    hid_above, hid_below = edges(up, down)
    unit = 8 * bands
    rows = -(-SLABS * share // unit) * unit
    depth = rows // bands
    terms = call(
        functools.partial(terms_body, step, scale, shards),
        "terms",
        shape((2, bands // 2, shards, depth, LANES), F32),
        [VMEM] * 4,
        (fcol, ccol, hid, inn),
        scratch=[pltpu.VMEM((TAPS * c, c), F32)] * 2,
        limit=20,
        flops=2 * conv_flops,
        nbytes=1 << 24,
    )
    keep = lax.dynamic_index_in_dim(terms, parity[0], 0, keepdims=False)
    give = lax.dynamic_index_in_dim(terms, 1 - parity[0], 0, keepdims=False)
    pair = keep + lax.ppermute(give, "lat", swap)
    groups = [[i for i in range(bands) if i % 2 == p] for p in range(2)]
    got = lax.all_to_all(
        pair.astype(BF16), "lat", 0, 0, axis_index_groups=groups, tiled=True
    )
    column = jnp.sum(got.astype(F32), axis=0)
    got = lax.all_to_all(column.astype(BF16), "fsdp", 0, 0, tiled=True)
    chunk = jnp.sum(got.astype(F32), axis=0)
    chunks = lax.all_gather(chunk, "lat", axis=0)
    out, grad = call(
        functools.partial(second_body, step),
        "second",
        [shape((height, c, lon), BF16)] * 2,
        [VMEM] * 8,
        (source, upstream, hid, inn, hid_above, hid_below, w2, a1),
        scratch=[pltpu.VMEM(columns.shape, BF16)],
        limit=24,
        flops=2 * conv_flops,
        nbytes=1 << 24,
    )
    one, two = call(
        functools.partial(unpack_body, share),
        "unpack",
        [shape((TAPS, share, c), F32)] * 2,
        [VMEM],
        (chunks,),
    )
    return (
        jnp.swapaxes(out, 1, 2)[None],
        jnp.swapaxes(grad, 1, 2)[None],
        jnp.swapaxes(one, 1, 2).reshape(3, 3, c, share),
        jnp.swapaxes(two, 1, 2).reshape(3, 3, c, share),
    )


def solution(mesh):
    placed = (
        P("fsdp", "lat", None, None),
        P("fsdp", "lat", None, None),
        P(None, None, None, "fsdp"),
        P(None, None, None, "fsdp"),
    )
    return jax.shard_map(
        per_device,
        mesh=mesh,
        in_specs=placed,
        out_specs=placed,
        check_vma=False,
    )
```

time: 530 us -> 157 us (0.30); the launches traced: 521 us -> 156 us
  waiting for transfers between devices: 163 us -> 0.02 us
  local copies, waits for them, and re-layouts: 180 us -> 26.6 us
  matrix products: 70.5 us -> 0 us
  Pallas kernels: 0 us -> 51.4 us
  other arithmetic: 30 us -> 4.14 us
  between operations: 15.7 us -> 0.81 us
  blocking collectives: 41.3 us -> 55.3 us
    unnamed x3 -> x0, waiting for transfers between devices: 117 us -> none
    conv_general_dilated x14 -> x0, local copies, waits for them, and re-layouts: 98.3 us -> none  [correlate(): lax.conv_general_dilated(padded, kernel, (1, 1), 'VALID', rhs_dilation=(2...]
    pallas_call x0 -> x6, Pallas kernels: none -> 51.4 us  [call(): pl.pallas_call(body, name=name, out_shape=out, in_specs=specs, out_specs=...]
    psum x1 -> x0, waiting for transfers between devices: 46.3 us -> none  [per_device(): grad_one, grad_two = lax.psum((share_one, share_two), 'lat')]
    conv_general_dilated x4 -> x0, matrix products: 41.3 us -> none  [correlate(): lax.conv_general_dilated(padded, kernel, (1, 1), 'VALID', rhs_dilation=(2...]
    dot_general x18 -> x0, matrix products: 29.2 us -> none  [kernel_terms(): jnp.einsum('nhwc,nhwd->cd', padded[:, 2 * a:2 * a + height, 2 * b:2 * b +...]
    all_to_all x0 -> x1, blocking collectives: none -> 24.8 us  [per_device(): lax.all_to_all(pair.astype(BF16), 'lat', 0, 0, axis_index_groups=groups,...]
    convert_element_type x14 -> x0, local copies, waits for them, and re-layouts: 18.8 us -> none  [the longest x7 9.61 us: per_device(): inner_grad = (back * slope).astype(jnp.bfloat16)]
  transfers between devices with their start and end apart: 10 -> 7, of which waited for: 2 -> 0; matrix products, arithmetic and copies ran while one was open for 23% -> 3% of each run, Pallas kernels for 0% -> 14%
where the time goes in v1:
time: 157 us; the launch traced here: 156 us
  blocking collectives  55.3 us (35%)
  Pallas kernels  51.4 us (33%)
  local copies, waits for them, and re-layouts  26.6 us (17%)
  starting transfers between devices  18.1 us (12%)
  other arithmetic  4.14 us (3%)
    pallas_call x6, Pallas kernels, call(): pl.pallas_call(body, name=name, out_shape=out, in_specs=specs, out_specs=...  51.4 us
    all_to_all x1, blocking collectives, per_device(): lax.all_to_all(pair.astype(BF16), 'lat', 0, 0, axis_index_groups=groups,...  24.8 us
    unnamed x32, local copies, waits for them, and re-layouts  24.1 us
    all_gather x1, blocking collectives, per_device(): own = lax.all_gather(half, 'fsdp', axis=0)  20.2 us
    all_gather x1, blocking collectives, per_device(): chunks = lax.all_gather(chunk, 'lat', axis=0)  10.2 us
    ppermute x1, starting transfers between devices, per_device(): pair = keep + lax.ppermute(give, 'lat', swap)  6.18 us
    ppermute x2, starting transfers between devices, edges(): lax.ppermute(bottom, 'lat', forward)  5.78 us
    all_to_all x1, starting transfers between devices, per_device(): got = lax.all_to_all(column.astype(BF16), 'fsdp', 0, 0, tiled=True)  3.61 us
  transfers between devices with their start and end apart: 7, of which 0 were waited for; matrix products, arithmetic and copies ran while one was open for 3% of the time, Pallas kernels for 14%

profile of v1, /device:TPU:0, one launch (start us, length us, event | category | flops | bytes accessed | tf_op | source)
XLA Modules:
  0.0 156.3 jit_solution(2206553861957311073)
XLA Ops:
  0.6 0.0 copy-start
  0.7 0.9 copy-done
  1.6 0.0 copy-start.1
  1.6 0.9 copy-done.1
  2.5 20.2 %all-gather = bf16[56,48,128]{2,1,0:T(8,128)(2,1)S(1)} all-gather(bf16[14,48,128]{2,1,0:T(8,128)(2,1)S(1)} %pack.1), channel_id=2, replica_groups=mesh['fsdp'=4,'lat'=8] {'fsdp'}, dimensions={0}, use_global_device_ids=true | all-gather | bytes 860160 | tf_op jit(solution)/shard_map/all_gather | solution.py:263
  22.7 0.0 collective-permute-start.2
  22.8 1.3 fusion.1
  24.1 0.9 pad_maximum_fusion.1
  25.0 1.3 collective-permute-start.1
  26.3 0.9 pad_maximum_fusion
  27.2 3.1 %collective-permute-start = (bf16[4,192,360]{2,1,0:T(8,128)(2,1)}, bf16[4,192,360]{2,1,0:T(8,128)(2,1)S(1)}, u32[]{:S(2)}, u32[]{:S(2)}) collective-permute-start(bf16[4,192,360]{2,1,0:T(8,128)(2,1)} %pad_maximum_fusion), channel_id=1, source_target_pairs={{0,1},{1,2},{2,3},{3,4},{4,5},{5,6},{6,7},{8,9},{9,10},{10,11},{11... | collective-permute-start | bytes 1658888 | tf_op jit(solution)/shard_map/ppermute | solution.py:254
  30.3 0.0 collective-permute-done.2.other
  30.3 1.8 %weights.1 = (bf16[192,1728]{1,0:T(8,128)(2,1)S(1)}, bf16[192,1728]{1,0:T(8,128)(2,1)S(1)}, bf16[192,1728]{1,0:T(8,128)(2,1)S(1)}, bf16[192,1728]{1,0:T(8,128)(2,1)S(1)}) custom-call(s32[1]{0:T(128)} %bitcast.6.parity, bf16[4,14,48,128]{3,2,1,0:T(8,128)(2,1)S(1)} %bitcast.34, bf16[4,14,48,128]{3,2,1,0:T(8,128)(2,1)S(1)} %collective-permute-done.2.other), custom_call_target="tpu_custom_call" | custom-call | tf_op jit(solution)/shard_map/weights/pallas_call | solution.py:21
  32.1 0.0 copy-start.6
  32.1 0.8 copy-done.6
  32.9 0.0 collective-permute-done.1.below
  33.0 0.0 collective-permute-done.above
  33.0 0.0 copy-start.2
  33.0 1.7 %copy-done.2 = bf16[1,16,360,192]{2,3,1,0:T(8,128)(2,1)S(1)} copy-done((bf16[1,16,360,192]{2,3,1,0:T(8,128)(2,1)S(1)}, bf16[1,16,360,192]{2,3,1,0:T(8,128)(2,1)}, u32[]{:S(2)}) %copy-start.2) | copy-done | bytes 2211864
  34.6 0.0 copy-start.4
  34.6 1.7 %copy-done.4 = bf16[1,16,360,192]{2,3,1,0:T(8,128)(2,1)S(1)} copy-done((bf16[1,16,360,192]{2,3,1,0:T(8,128)(2,1)S(1)}, bf16[1,16,360,192]{2,3,1,0:T(8,128)(2,1)}, u32[]{:S(2)}) %copy-start.4) | copy-done | bytes 2211864
  36.3 16.0 %first.1 = (bf16[20,576,384]{2,1,0:T(8,128)(2,1)S(1)}, bf16[20,576,384]{2,1,0:T(8,128)(2,1)S(1)}, bf16[16,192,384]{2,1,0:T(8,128)(2,1)S(1)}, bf16[16,192,384]{2,...) custom-call(bf16[16,192,360]{2,1,0:T(8,128)(2,1)S(1)} %bitcast.39, ...), custom_call_target="tpu_custom_call" | custom-call | flops 7644119040 | bytes 16777216 | tf_op jit(solution)/shard_map/first/pallas_call | solution.py:21
  52.3 0.0 copy-start.8
  52.4 0.8 copy-done.8
  53.1 0.0 copy-start.9
  53.2 0.8 copy-done.9
  54.0 0.0 copy-start.10
  54.0 3.4 %copy-done.10 = bf16[20,576,384]{2,1,0:T(8,128)(2,1)} copy-done((bf16[20,576,384]{2,1,0:T(8,128)(2,1)}, bf16[20,576,384]{2,1,0:T(8,128)(2,1)S(1)}, u32[]{:S(2)}) %copy-start.10) | copy-done | bytes 8847384
  57.4 0.0 copy-start.12
  57.4 0.0 copy-start.14
  57.4 0.0 copy-start.11
  57.4 5.2 %copy-done.11 = bf16[20,576,384]{2,1,0:T(8,128)(2,1)S(1)} copy-done((bf16[20,576,384]{2,1,0:T(8,128)(2,1)S(1)}, bf16[20,576,384]{2,1,0:T(8,128)(2,1)}, u32[]{:S(2)}) %copy-start.11) | copy-done | bytes 8847384
  62.6 12.8 %terms.1 = f32[2,4,4,168,128]{4,3,2,1,0:T(8,128)S(1)} custom-call(bf16[20,576,384]{2,1,0:T(8,128)(2,1)S(1)} %copy-done.11, bf16[20,576,384]{2,1,0:T(8,128)(2,1)S(1)} %get-tuple-element.29.ccol, bf16[16,192,384]{2,1,0:T(8,128)(2,1)S(1)} %get-tuple-element.20.hid, bf16[16,192,384]{2,1,0:T(8,128)(2,1)S(1)} %get-tuple-element.21.inn), custom_call_target="tpu_custom_call" | custom-call | flops 7644119040 | bytes 16777216 | tf_op jit(solution)/shard_map/terms/pallas_call | solution.py:21
  75.5 0.0 copy-done.12
  75.5 0.0 copy-done.14
  75.5 1.2 dynamic-slice_bitcast_fusion
  76.7 6.2 %collective-permute-start.5 = (f32[4,4,168,128]{3,2,1,0:T(8,128)}, f32[4,4,168,128]{3,2,1,0:T(8,128)}, u32[]{:S(2)}, u32[]{:S(2)}) collective-permute-start(f32[4,4,168,128]{3,2,1,0:T(8,128)} %dynamic-slice_bitcast_fusion), channel_id=1, source_target_pairs={{0,1},{1,0},{2,3},{3,2},{4,5},{5,4},{6,7},{7,6},{8,9},{9,8},{10,11... | collective-permute-start | bytes 4128776 | tf_op jit(solution)/shard_map/ppermute | solution.py:303
  82.9 2.7 %collective-permute-start.3 = (bf16[4,192,360]{2,1,0:T(8,128)(2,1)}, bf16[4,192,360]{2,1,0:T(8,128)(2,1)}, u32[]{:S(2)}, u32[]{:S(2)}) collective-permute-start(bf16[4,192,360]{2,1,0:T(8,128)(2,1)} %copy-done.9), channel_id=1, source_target_pairs={{0,1},{1,2},{2,3},{3,4},{4,5},{5,6},{6,7},{8,9},{9,10},{10,11},{11... | collective-permute-start | bytes 1658888 | tf_op jit(solution)/shard_map/ppermute | solution.py:254
  85.6 1.3 collective-permute-start.4
  86.9 0.0 collective-permute-done.5
  86.9 1.5 fusion
  88.4 24.8 %all_to_all.10 = bf16[4,4,168,128]{3,2,1,0:T(8,128)(2,1)S(1)} all-to-all(bf16[4,4,168,128]{3,2,1,0:T(8,128)(2,1)S(1)} %fusion), channel_id=1, replica_groups={{0,2,4,6},{1,3,5,7},{8,10,12,14},{9,11,13,15},{16,18,20,22},{17,19,21,2..., dimensions={0} | all-to-all | bytes 1376256 | tf_op jit(solution)/shard_map/all_to_all | solution.py:305
  113.2 0.8 reduce_sum.21
  114.0 3.6 %all-to-all-start.1 = ((bf16[4,168,128]{2,1,0:T(8,128)(2,1)}), bf16[4,168,128]{2,1,0:T(8,128)(2,1)S(1)}, u32[]{:S(2)}, u32[]{:S(2)}) async-start(bf16[4,168,128]{2,1,0:T(8,128)(2,1)} %reduce_sum.21), calls=%async_computation.1 | async-start | bytes 344064 | tf_op jit(solution)/shard_map/all_to_all | solution.py:309
  117.6 0.0 collective-permute-done.3.above
  117.6 0.0 collective-permute-done.4.below
  117.6 0.0 copy-start.3
  117.6 1.7 %copy-done.3 = bf16[1,16,360,192]{2,3,1,0:T(8,128)(2,1)S(1)} copy-done((bf16[1,16,360,192]{2,3,1,0:T(8,128)(2,1)S(1)}, bf16[1,16,360,192]{2,3,1,0:T(8,128)(2,1)}, u32[]{:S(2)}) %copy-start.3) | copy-done | bytes 2211864
  119.3 0.0 copy-start.5
  119.3 1.7 %copy-done.5 = bf16[1,16,360,192]{2,3,1,0:T(8,128)(2,1)S(1)} copy-done((bf16[1,16,360,192]{2,3,1,0:T(8,128)(2,1)S(1)}, bf16[1,16,360,192]{2,3,1,0:T(8,128)(2,1)}, u32[]{:S(2)}) %copy-start.5) | copy-done | bytes 2211864
  120.9 0.0 copy-start.7
  120.9 1.1 copy-done.7
  122.0 0.0 copy-start.13
  122.0 1.7 %copy-done.13 = bf16[16,192,384]{2,1,0:T(8,128)(2,1)S(1)} copy-done((bf16[16,192,384]{2,1,0:T(8,128)(2,1)S(1)}, bf16[16,192,384]{2,1,0:T(8,128)(2,1)}, u32[]{:S(2)}) %copy-start.13) | copy-done | bytes 2359320
  123.7 0.0 copy-start.15
  123.7 1.7 %copy-done.15 = bf16[16,192,384]{2,1,0:T(8,128)(2,1)S(1)} copy-done((bf16[16,192,384]{2,1,0:T(8,128)(2,1)S(1)}, bf16[16,192,384]{2,1,0:T(8,128)(2,1)}, u32[]{:S(2)}) %copy-start.15) | copy-done | bytes 2359320
  125.3 19.7 %second.1 = (bf16[16,192,360]{2,1,0:T(8,128)(2,1)}, bf16[16,192,360]{2,1,0:T(8,128)(2,1)}) custom-call(bf16[16,192,360]{2,1,0:T(8,128)(2,1)S(1)} %bitcast.40, bf16[16,192,360]{2,1,0:T(8,128)(2,1)S(1)} %bitcast.43, bf16[16,192,384]{2,1,0:T(8,128)(2,1)S(1)} %copy-done.13, bf16[16,192,384]{2,1,0:T(8,128)(2,1)S(1)} %copy-done.15, ...), custom_call_target="tpu_custom_call" | custom-call | flops 7644119040 | bytes 16777216 | tf_op jit(solution)/shard_map/second/pallas_call | solution.py:21
  145.1 0.0 all-to-all-done.1
  145.1 10.2 %all-gather.1 = f32[1344,128]{1,0:T(8,128)S(1)} all-gather(f32[168,128]{1,0:T(8,128)S(1)} %convert_reduce_fusion), channel_id=3, replica_groups=mesh['fsdp'=4,'lat'=8] {'lat'}, dimensions={0}, use_global_device_ids=true | all-gather | bytes 774144 | tf_op jit(solution)/shard_map/all_gather | solution.py:311
  155.4 1.0 unpack.1
  (2 shorter events, 0.1 us)
Async XLA Ops:
  0.6 0.9 copy-start
  1.6 0.9 copy-start.1
  22.7 7.6 %collective-permute-start.2 = (bf16[4,14,48,128]{3,2,1,0:T(8,128)(2,1)S(1)}, bf16[4,14,48,128]{3,2,1,0:T(8,128)(2,1)S(1)}, u32[]{:S(2)}, u32[]{:S(2)}) collective-permute-start(bf16[4,14,48,128]{3,2,1,0:T(8,128)(2,1)S(1)} %bitcast.33), channel_id=1, source_target_pairs={{0,1},{1,0},{2,3},{3,2},{4,5},{5,4},{6,7},{7,6},{8,9},{9,8},{10,11... | collective-permute-start | bytes 2064392 | tf_op jit(solution)/shard_map/ppermute | solution.py:264
  25.0 7.9 %collective-permute-start.1 = (bf16[4,192,360]{2,1,0:T(8,128)(2,1)}, bf16[4,192,360]{2,1,0:T(8,128)(2,1)S(1)}, u32[]{:S(2)}, u32[]{:S(2)}) collective-permute-start(bf16[4,192,360]{2,1,0:T(8,128)(2,1)} %pad_maximum_fusion.1), channel_id=1, source_target_pairs={{1,0},{2,1},{3,2},{4,3},{5,4},{6,5},{7,6},{9,8},{10,9},{11,10},{12... | collective-permute-start | bytes 1658888 | tf_op jit(solution)/shard_map/ppermute | solution.py:254
  27.2 5.7 %collective-permute-start = (bf16[4,192,360]{2,1,0:T(8,128)(2,1)}, bf16[4,192,360]{2,1,0:T(8,128)(2,1)S(1)}, u32[]{:S(2)}, u32[]{:S(2)}) collective-permute-start(bf16[4,192,360]{2,1,0:T(8,128)(2,1)} %pad_maximum_fusion), channel_id=1, source_target_pairs={{0,1},{1,2},{2,3},{3,4},{4,5},{5,6},{6,7},{8,9},{9,10},{10,11},{11... | collective-permute-start | bytes 1658888 | tf_op jit(solution)/shard_map/ppermute | solution.py:254
  32.1 0.9 copy-start.6
  33.0 1.7 %copy-start.2 = (bf16[1,16,360,192]{2,3,1,0:T(8,128)(2,1)S(1)}, bf16[1,16,360,192]{2,3,1,0:T(8,128)(2,1)}, u32[]{:S(2)}) copy-start(bf16[1,16,360,192]{2,3,1,0:T(8,128)(2,1)} %param.4) | copy-start | bytes 6635524
  34.6 1.7 %copy-start.4 = (bf16[1,16,360,192]{2,3,1,0:T(8,128)(2,1)S(1)}, bf16[1,16,360,192]{2,3,1,0:T(8,128)(2,1)}, u32[]{:S(2)}) copy-start(bf16[1,16,360,192]{2,3,1,0:T(8,128)(2,1)} %param.5) | copy-start | bytes 6635524
  52.3 0.8 copy-start.8
  53.1 0.8 copy-start.9
  54.0 3.4 %copy-start.10 = (bf16[20,576,384]{2,1,0:T(8,128)(2,1)}, bf16[20,576,384]{2,1,0:T(8,128)(2,1)S(1)}, u32[]{:S(2)}) copy-start(bf16[20,576,384]{2,1,0:T(8,128)(2,1)S(1)} %get-tuple-element.28.fcol) | copy-start | bytes 26542084
  57.4 18.1 %copy-start.12 = (bf16[16,192,384]{2,1,0:T(8,128)(2,1)}, bf16[16,192,384]{2,1,0:T(8,128)(2,1)S(1)}, u32[]{:S(2)}) copy-start(bf16[16,192,384]{2,1,0:T(8,128)(2,1)S(1)} %get-tuple-element.20.hid) | copy-start | bytes 7077892
  57.4 18.1 %copy-start.14 = (bf16[16,192,384]{2,1,0:T(8,128)(2,1)}, bf16[16,192,384]{2,1,0:T(8,128)(2,1)S(1)}, u32[]{:S(2)}) copy-start(bf16[16,192,384]{2,1,0:T(8,128)(2,1)S(1)} %get-tuple-element.21.inn) | copy-start | bytes 7077892
  57.4 5.2 %copy-start.11 = (bf16[20,576,384]{2,1,0:T(8,128)(2,1)S(1)}, bf16[20,576,384]{2,1,0:T(8,128)(2,1)}, u32[]{:S(2)}) copy-start(bf16[20,576,384]{2,1,0:T(8,128)(2,1)} %copy-done.10) | copy-start | bytes 26542084
  76.7 10.2 %collective-permute-start.5 = (f32[4,4,168,128]{3,2,1,0:T(8,128)}, f32[4,4,168,128]{3,2,1,0:T(8,128)}, u32[]{:S(2)}, u32[]{:S(2)}) collective-permute-start(f32[4,4,168,128]{3,2,1,0:T(8,128)} %dynamic-slice_bitcast_fusion), channel_id=1, source_target_pairs={{0,1},{1,0},{2,3},{3,2},{4,5},{5,4},{6,7},{7,6},{8,9},{9,8},{10,11... | collective-permute-start | bytes 4128776 | tf_op jit(solution)/shard_map/ppermute | solution.py:303
  82.9 34.7 %collective-permute-start.3 = (bf16[4,192,360]{2,1,0:T(8,128)(2,1)}, bf16[4,192,360]{2,1,0:T(8,128)(2,1)}, u32[]{:S(2)}, u32[]{:S(2)}) collective-permute-start(bf16[4,192,360]{2,1,0:T(8,128)(2,1)} %copy-done.9), channel_id=1, source_target_pairs={{0,1},{1,2},{2,3},{3,4},{4,5},{5,6},{6,7},{8,9},{9,10},{10,11},{11... | collective-permute-start | bytes 1658888 | tf_op jit(solution)/shard_map/ppermute | solution.py:254
  85.6 32.0 %collective-permute-start.4 = (bf16[4,192,360]{2,1,0:T(8,128)(2,1)}, bf16[4,192,360]{2,1,0:T(8,128)(2,1)}, u32[]{:S(2)}, u32[]{:S(2)}) collective-permute-start(bf16[4,192,360]{2,1,0:T(8,128)(2,1)} %copy-done.8), channel_id=1, source_target_pairs={{1,0},{2,1},{3,2},{4,3},{5,4},{6,5},{7,6},{9,8},{10,9},{11,10},{12... | collective-permute-start | bytes 1658888 | tf_op jit(solution)/shard_map/ppermute | solution.py:254
  114.0 31.1 %all-to-all-start.1 = ((bf16[4,168,128]{2,1,0:T(8,128)(2,1)}), bf16[4,168,128]{2,1,0:T(8,128)(2,1)S(1)}, u32[]{:S(2)}, u32[]{:S(2)}) async-start(bf16[4,168,128]{2,1,0:T(8,128)(2,1)} %reduce_sum.21), calls=%async_computation.1 | async-start | bytes 344064 | tf_op jit(solution)/shard_map/all_to_all | solution.py:309
  117.6 1.7 %copy-start.3 = (bf16[1,16,360,192]{2,3,1,0:T(8,128)(2,1)S(1)}, bf16[1,16,360,192]{2,3,1,0:T(8,128)(2,1)}, u32[]{:S(2)}) copy-start(bf16[1,16,360,192]{2,3,1,0:T(8,128)(2,1)} %param.4) | copy-start | bytes 6635524
  119.3 1.7 %copy-start.5 = (bf16[1,16,360,192]{2,3,1,0:T(8,128)(2,1)S(1)}, bf16[1,16,360,192]{2,3,1,0:T(8,128)(2,1)}, u32[]{:S(2)}) copy-start(bf16[1,16,360,192]{2,3,1,0:T(8,128)(2,1)} %param.5) | copy-start | bytes 6635524
  120.9 1.1 copy-start.7
  122.0 1.7 %copy-start.13 = (bf16[16,192,384]{2,1,0:T(8,128)(2,1)S(1)}, bf16[16,192,384]{2,1,0:T(8,128)(2,1)}, u32[]{:S(2)}) copy-start(bf16[16,192,384]{2,1,0:T(8,128)(2,1)} %copy-done.12) | copy-start | bytes 7077892
  123.7 1.7 %copy-start.15 = (bf16[16,192,384]{2,1,0:T(8,128)(2,1)S(1)}, bf16[16,192,384]{2,1,0:T(8,128)(2,1)}, u32[]{:S(2)}) copy-start(bf16[16,192,384]{2,1,0:T(8,128)(2,1)} %copy-done.14) | copy-start | bytes 7077892

commit v2 on v0

v2 whole, which is shorter than its diff:
```python
import functools

import jax
import jax.numpy as jnp
from jax import lax
from jax.experimental import pallas as pl
from jax.experimental.pallas import tpu as pltpu
from jax.sharding import PartitionSpec as P

BF16 = jnp.bfloat16
F32 = jnp.float32
VMEM = pl.BlockSpec(memory_space=pltpu.VMEM)
SMEM = pl.BlockSpec(memory_space=pltpu.SMEM)
ANY = pl.BlockSpec(memory_space=pltpu.HBM)
TAPS = 9
SLABS = TAPS + (TAPS + 1) // 2
HALF = SLABS // 2
LANES = 128
GROUP = 4
SPAN = 4


def shape(*dims, dtype=BF16):
    return jax.ShapeDtypeStruct(dims, dtype)


def call(body, name, outs, specs, args, scratch=(), limit=16, flops=0, nbytes=0):
    return pl.pallas_call(
        body,
        name=name,
        out_shape=[o for o, _ in outs],
        in_specs=specs,
        out_specs=[s for _, s in outs],
        scratch_shapes=list(scratch),
        compiler_params=pltpu.CompilerParams(vmem_limit_bytes=limit << 20),
        cost_estimate=pl.CostEstimate(flops=flops, bytes_accessed=nbytes, transcendentals=0),
    )(*args)


def to_slab(tap_of, s):
    if s < TAPS:
        return tap_of(s)[:, :LANES]
    first = 2 * (s - TAPS)
    second = min(first + 1, TAPS - 1)
    return jnp.concatenate([tap_of(first)[:, LANES:], tap_of(second)[:, LANES:]], axis=1)


def from_slabs(slab_of, tap):
    tails = slab_of(TAPS + tap // 2)
    half = LANES // 2
    tail = tails[:, half:] if tap % 2 else tails[:, :half]
    return jnp.concatenate([slab_of(tap), tail], axis=1)


def pack_body(parity, one, two, source, upstream, half, top, bottom, sem):
    height = source.shape[0]
    copies = []
    for base, rows in ((0, source), (2, upstream)):
        for k, (ref, at) in enumerate(((top, 0), (bottom, height - 2))):
            copies.append(
                pltpu.make_async_copy(
                    rows.at[pl.ds(at, 2)], ref.at[pl.ds(base, 2)], sem.at[base + k]
                )
            )
    for copy in copies:
        copy.start()
    for side in range(2):

        @pl.when(parity[0] == side)
        def _():
            for k, kernel in enumerate((one, two)):
                for i in range(HALF):
                    half[k * HALF + i] = to_slab(lambda tap: kernel[tap], side * HALF + i)

    for copy in copies:
        copy.wait()


def stack_body(place, half, *refs):
    out = refs[-1]
    for d, piece in enumerate((half,) + refs[:-1]):
        out[place[1] ^ d] = piece[...]


def load_weight(place, own, other, which, weight, adjoint):
    c = weight.shape[0]
    base = which * HALF
    mine = place[0] == 0
    slabs = {}

    def slab(s):
        if s not in slabs:
            side, i = divmod(s, HALF)
            first, second = (own, other) if side == 0 else (other, own)
            parts = [
                jnp.where(mine, first[f, base + i], second[f, base + i])
                for f in range(own.shape[0])
            ]
            slabs[s] = jnp.concatenate(parts, axis=0)
        return slabs[s]

    for tap in range(TAPS):
        value = from_slabs(slab, tap)
        if adjoint:
            weight[:, pl.ds((TAPS - 1 - tap) * c, c)] = value.T
        else:
            weight[:, pl.ds(tap * c, c)] = value


def store_row(columns, at, row):
    c, lon = row.shape
    fill = jnp.zeros((c, columns.shape[2] - lon), row.dtype)
    pieces = (
        jnp.concatenate([row[:, lon - 2 :], row[:, : lon - 2], fill], axis=1),
        jnp.concatenate([row, fill], axis=1),
        jnp.concatenate([row[:, 2:], row[:, :2], fill], axis=1),
    )
    for b, piece in enumerate(pieces):
        columns[at, b * c : (b + 1) * c] = piece


def taps_of(columns, at):
    return jnp.concatenate([columns[at], columns[at + 2], columns[at + 4]], axis=0)


def rows_of(columns, at, count=None):
    return jnp.concatenate([taps_of(columns, at + s) for s in range(count or GROUP)], axis=1)


def chunked(source, target, sem):
    return [
        pltpu.make_async_copy(
            source.at[pl.ds(at, GROUP)], target.at[pl.ds(at, GROUP)], sem.at[at // GROUP]
        )
        for at in range(0, source.shape[0], GROUP)
    ]


class Columns:
    def __init__(self, ref, rows, copies, base, lon):
        self.ref, self.rows, self.copies = ref, rows, copies
        self.base, self.lon = base, lon
        self.done = 0

    def fill(self, upto):
        while self.done < min(upto, self.rows.shape[0]):
            if self.done % GROUP == 0:
                self.copies[self.done // GROUP].wait()
            store_row(self.ref, self.done + self.base, self.rows[self.done][:, : self.lon])
            self.done += 1


def place_terms(out, base, depth, total, shards, scale, flip):
    c = total.shape[1]
    share = c // shards
    values = {}

    def tap_of(tap):
        if tap not in values:
            if flip:
                values[tap] = total[tap * c : (tap + 1) * c].T * scale
            else:
                values[tap] = total[(TAPS - 1 - tap) * c : (TAPS - tap) * c] * scale
        return values[tap]

    for s in range(SLABS):
        value = to_slab(tap_of, s).astype(BF16)
        for f in range(shards):
            start = s * share
            while start < (s + 1) * share:
                chunk, inside = divmod(start, depth)
                stop = min((s + 1) * share, (chunk + 1) * depth)
                src = f * share + start - s * share
                lo = base + inside
                out[chunk, f, lo : lo + stop - start] = value[src : src + stop - start]
                start = stop


def sum_terms(total, columns, field):
    total[...] = jnp.zeros_like(total)

    def work(t, carry):
        at = t * SPAN
        rhs = jnp.concatenate([field[at + s] for s in range(SPAN)], axis=1)
        total[...] += lax.dot_general(
            rows_of(columns, at, SPAN),
            rhs,
            (((1,), (1,)), ((), ())),
            preferred_element_type=F32,
        )
        return carry

    lax.fori_loop(0, field.shape[0] // SPAN, work, 0)


def stage_body(
    scale, shards, place, source, upstream, above, below, own, other,
    hid, inn, top, bottom, terms,
    src, ups, fcol, ccol, w1, a2, hidden, inner, one, two, sem, edge_sem,
):
    height, _, lon = source.shape
    wide = fcol.shape[2]
    loads = [chunked(source, src, sem.at[0]), chunked(upstream, ups, sem.at[1])]
    for pair in zip(*loads):
        for copy in pair:
            copy.start()
    load_weight(place, own, other, 0, w1, False)
    load_weight(place, own, other, 1, a2, True)
    for columns, base in ((fcol, 0), (ccol, 2)):
        for r in range(2):
            store_row(columns, r, above[base + r])
            store_row(columns, height + 2 + r, below[base + r])
    forward = Columns(fcol, src, loads[0], 2, lon)
    reverse = Columns(ccol, ups, loads[1], 2, lon)
    forward.fill(GROUP + 2)
    saves = [chunked(hidden, hid, sem.at[2]), chunked(inner, inn, sem.at[3])]
    edges = []
    for k, rows in enumerate((hidden, inner)):
        for j, (ref, at) in enumerate(((top, 0), (bottom, height - 2))):
            edges.append(
                pltpu.make_async_copy(
                    rows.at[pl.ds(at, 2)], ref.at[pl.ds(2 * k, 2)], edge_sem.at[2 * k + j]
                )
            )
    for at in range(0, height, GROUP):
        reverse.fill(at + GROUP + 2)
        pre = jnp.dot(w1[...], rows_of(fcol, at), preferred_element_type=F32)
        forward.fill(at + 2 * GROUP + 2)
        back = jnp.dot(a2[...], rows_of(ccol, at), preferred_element_type=F32)
        cdf = 0.5 * (1.0 + lax.erf(pre * 0.7071067811865476))
        value = (pre * cdf).astype(BF16)
        rate = cdf + pre * jnp.exp(-0.5 * pre * pre) * 0.3989422804014327
        grad = (back * rate).astype(BF16)
        for s in range(GROUP):
            hidden[at + s] = value[:, s * wide : (s + 1) * wide]
            inner[at + s] = grad[:, s * wide : (s + 1) * wide]
        for save in saves:
            save[at // GROUP].start()
    for copy in edges:
        copy.start()
    sum_terms(one, fcol, inner)
    sum_terms(two, ccol, hidden)
    depth = terms.shape[2] // 2
    place_terms(terms, 0, depth, one, shards, scale, True)
    place_terms(terms, depth, depth, two, shards, scale, False)
    for copy in saves[0] + saves[1] + edges:
        copy.wait()


def interior_body(
    place, source, upstream, hid, inn, own, other,
    out, grad, w2, a1,
    src, ups, mid, cot, hcol, icol, left, right, sem,
):
    height, _, lon = source.shape
    wide = hcol.shape[2]
    work = []
    for k, args in enumerate(
        ((hid, mid, hcol, source, src, w2, left, out), (inn, cot, icol, upstream, ups, a1, right, grad))
    ):
        middle, held, columns, residual, base, weight, result, target = args
        loads = [chunked(middle, held, sem.at[3 * k]), chunked(residual, base, sem.at[3 * k + 1])]
        for pair in zip(*loads):
            for copy in pair:
                copy.start()
        rows = Columns(columns, held, loads[0], 0, lon)
        work.append((rows, loads[1], columns, base, weight, result, target, sem.at[3 * k + 2]))
    load_weight(place, own, other, 1, w2, False)
    load_weight(place, own, other, 0, a1, True)
    saves = []
    for rows, waits, columns, base, weight, result, target, done in work:
        rows.fill(GROUP + 4)
        waits[0].wait()
        for at in range(0, height - 4, GROUP):
            waits[at // GROUP + 1].wait()
            rows.fill(at + 2 * GROUP + 4)
            value = jnp.dot(weight[...], rows_of(columns, at), preferred_element_type=F32)
            for s in range(GROUP):
                part = value[:, s * wide : s * wide + lon]
                row = at + 2 + s
                result[row] = (base[row].astype(F32) + part).astype(BF16)
            span = pl.ds(at + 2, GROUP)
            save = pltpu.make_async_copy(result.at[span], target.at[span], done.at[at // GROUP])
            save.start()
            saves.append(save)
    for save in saves:
        save.wait()


def edge_body(
    source, upstream, hid, inn, above, below, w2, a1, out_in, grad_in,
    out, grad,
    res, mid, columns, result, sem,
):
    del out_in, grad_in
    height, _, lon = source.shape
    wide = columns.shape[3]
    ends = (0, height - 4), (0, height - 2)
    loads, saves = [], []
    for k, (residual, middle, target) in enumerate(((source, hid, out), (upstream, inn, grad))):
        for j in range(2):
            loads.append(
                pltpu.make_async_copy(
                    middle.at[pl.ds(ends[0][j], 4)], mid.at[2 * k + j], sem.at[0, 2 * k + j]
                )
            )
            loads.append(
                pltpu.make_async_copy(
                    residual.at[pl.ds(ends[1][j], 2)], res.at[2 * k + j], sem.at[1, 2 * k + j]
                )
            )
            saves.append(
                pltpu.make_async_copy(
                    result.at[2 * k + j], target.at[pl.ds(ends[1][j], 2)], sem.at[2, 2 * k + j]
                )
            )
    for copy in loads:
        copy.start()
    for k in range(2):
        for r in range(2):
            store_row(columns.at[2 * k], r, above[2 * k + r][:, :lon])
            store_row(columns.at[2 * k + 1], 4 + r, below[2 * k + r][:, :lon])
    for k, weight in enumerate((w2, a1)):
        for j in range(2):
            for copy in loads[4 * k + 2 * j : 4 * k + 2 * j + 2]:
                copy.wait()
            for r in range(4):
                store_row(columns.at[2 * k + j], r + 2 - 2 * j, mid[2 * k + j, r][:, :lon])
        rhs = jnp.concatenate(
            [taps_of(columns.at[2 * k + j], r) for j in range(2) for r in range(2)], axis=1
        )
        value = jnp.dot(weight[...], rhs, preferred_element_type=F32)
        for j in range(2):
            for r in range(2):
                lo = (2 * j + r) * wide
                part = value[:, lo : lo + lon]
                base = res[2 * k + j, r].astype(F32)
                result[2 * k + j, r] = (base + part).astype(BF16)
            saves[2 * k + j].start()
    for copy in saves:
        copy.wait()


def column_body(place, got, mine, *gives):
    def total(f):
        value = got[0, f].astype(F32)
        for i in range(1, got.shape[0]):
            value += got[i, f].astype(F32)
        return value

    mine[...] = total(place[1])
    for d, give in enumerate(gives):
        give[...] = total(place[1] ^ (d + 1)).astype(BF16)


def chunk_body(mine, *refs):
    total = mine[...]
    for piece in refs[:-1]:
        total += piece[...].astype(F32)
    refs[-1][...] = total


def unpack_body(share, depth, chunks, one, two):
    for k, result in enumerate((one, two)):

        def slab(s):
            parts = []
            start = s * share
            while start < (s + 1) * share:
                chunk, inside = divmod(start, depth)
                stop = min((s + 1) * share, (chunk + 1) * depth)
                lo = k * depth + inside
                parts.append(chunks[chunk, lo : lo + stop - start])
                start = stop
            return parts[0] if len(parts) == 1 else jnp.concatenate(parts, axis=0)

        for tap in range(TAPS):
            result[tap] = from_slabs(slab, tap)


def per_device(fields, cotangent, kernel_one, kernel_two):
    _, height, lon, c = fields.shape
    share = kernel_one.shape[3]
    shards = lax.axis_size("fsdp")
    bands = lax.axis_size("lat")
    wide = -(-lon // LANES) * LANES
    scale = 1.0 / (shards * fields.shape[0] * bands * height * lon) ** 0.5
    source = jnp.swapaxes(fields[0], 1, 2)
    upstream = jnp.swapaxes(cotangent[0], 1, 2)
    small = [
        jnp.swapaxes(k.reshape(TAPS, c, share), 1, 2) for k in (kernel_one, kernel_two)
    ]
    place = jnp.stack([lax.axis_index("lat") % 2, lax.axis_index("fsdp")]).astype(jnp.int32)
    forward = [(i, i + 1) for i in range(bands - 1)]
    backward = [(i + 1, i) for i in range(bands - 1)]
    swap = [(i, i ^ 1) for i in range(bands)]

    def edges(top, bottom):
        return lax.ppermute(bottom, "lat", forward), lax.ppermute(top, "lat", backward)

    def partner(value, d):
        return lax.ppermute(value, "fsdp", [(i, i ^ d) for i in range(shards)])

    conv_flops = 2 * TAPS * c * c * height * lon
    groups = height // GROUP
    depth = -(-SLABS * share // (8 * bands)) * 8
    others = range(1, shards)
    half, top, bottom = call(
        pack_body,
        "pack",
        [
            (shape(2 * HALF, share, LANES), VMEM),
            (shape(4, c, lon), ANY),
            (shape(4, c, lon), ANY),
        ],
        [SMEM, VMEM, VMEM, ANY, ANY],
        (place, *small, source, upstream),
        scratch=[pltpu.SemaphoreType.DMA((4,))],
    )
    pieces = [partner(half, d) for d in others]
    above, below = edges(top, bottom)
    (own,) = call(
        stack_body,
        "stack",
        [(shape(shards, 2 * HALF, share, LANES), VMEM)],
        [SMEM] + [VMEM] * shards,
        (place, half, *pieces),
    )
    other = lax.ppermute(own, "lat", swap)

    middle = shape(height, c, wide)
    edge = shape(4, c, wide)
    plain = pltpu.VMEM((height, c, lon), BF16)
    lined = pltpu.VMEM((height, c, wide), BF16)
    columns = pltpu.VMEM((height + 4, 3 * c, wide), BF16)
    matrix = pltpu.VMEM((c, TAPS * c), BF16)
    total = pltpu.VMEM((TAPS * c, c), F32)
    hid, inn, top, bottom, terms = call(
        functools.partial(stage_body, scale, shards),
        "stage",
        [
            (middle, ANY),
            (middle, ANY),
            (edge, ANY),
            (edge, ANY),
            (shape(bands, shards, 2 * depth, LANES), VMEM),
        ],
        [SMEM, ANY, ANY, VMEM, VMEM, VMEM, VMEM],
        (place, source, upstream, above, below, own, other),
        scratch=[plain, plain, columns, columns, matrix, matrix, lined, lined, total, total]
        + [pltpu.SemaphoreType.DMA((4, groups)), pltpu.SemaphoreType.DMA((4,))],
        limit=52,
        flops=4 * conv_flops,
        nbytes=1 << 24,
    )
    above, below = edges(top, bottom)
    got = lax.all_to_all(terms, "lat", 0, 0, tiled=True)
    columns = pltpu.VMEM((height, 3 * c, wide), BF16)
    outs = (shape(height, c, lon), ANY)
    weight = (shape(c, TAPS * c), VMEM)
    out, grad, w2, a1 = call(
        interior_body,
        "interior",
        [outs, outs, weight, weight],
        [SMEM, ANY, ANY, ANY, ANY, VMEM, VMEM],
        (place, source, upstream, hid, inn, own, other),
        scratch=[plain, plain, lined, lined, columns, columns, plain, plain]
        + [pltpu.SemaphoreType.DMA((6, groups))],
        limit=50,
        flops=2 * conv_flops,
        nbytes=1 << 24,
    )
    mine, *gives = call(
        column_body,
        "column",
        [(shape(2 * depth, LANES, dtype=F32), VMEM)]
        + [(shape(2 * depth, LANES), VMEM) for _ in others],
        [SMEM, VMEM],
        (place, got),
    )
    gains = [partner(give, d) for d, give in zip(others, gives)]
    out, grad = pl.pallas_call(
        edge_body,
        name="edge",
        out_shape=[outs[0], outs[0]],
        in_specs=[ANY] * 4 + [VMEM] * 4 + [ANY] * 2,
        out_specs=[ANY, ANY],
        input_output_aliases={8: 0, 9: 1},
        scratch_shapes=[
            pltpu.VMEM((4, 2, c, lon), BF16),
            pltpu.VMEM((4, 4, c, wide), BF16),
            pltpu.VMEM((4, 6, 3 * c, wide), BF16),
            pltpu.VMEM((4, 2, c, lon), BF16),
            pltpu.SemaphoreType.DMA((3, 4)),
        ],
        compiler_params=pltpu.CompilerParams(vmem_limit_bytes=32 << 20),
        cost_estimate=pl.CostEstimate(
            flops=conv_flops // 2, bytes_accessed=1 << 22, transcendentals=0
        ),
    )(source, upstream, hid, inn, above, below, w2, a1, out, grad)
    (chunk,) = call(
        chunk_body,
        "chunk",
        [(shape(2 * depth, LANES, dtype=F32), VMEM)],
        [VMEM] * shards,
        (mine, *gains),
    )
    chunks = lax.all_gather(chunk, "lat", axis=0)
    one, two = call(
        functools.partial(unpack_body, share, depth),
        "unpack",
        [(shape(TAPS, share, c, dtype=F32), VMEM)] * 2,
        [VMEM],
        (chunks,),
    )
    return (
        jnp.swapaxes(out, 1, 2)[None],
        jnp.swapaxes(grad, 1, 2)[None],
        jnp.swapaxes(one, 1, 2).reshape(3, 3, c, share),
        jnp.swapaxes(two, 1, 2).reshape(3, 3, c, share),
    )


def solution(mesh):
    placed = (
        P("fsdp", "lat", None, None),
        P("fsdp", "lat", None, None),
        P(None, None, None, "fsdp"),
        P(None, None, None, "fsdp"),
    )
    return jax.shard_map(
        per_device,
        mesh=mesh,
        in_specs=placed,
        out_specs=placed,
        check_vma=False,
    )
```

time: 530 us -> 137 us (0.26); the launches traced: 521 us -> 137 us
  local copies, waits for them, and re-layouts: 180 us -> 16.1 us
  waiting for transfers between devices: 163 us -> 17.2 us
  matrix products: 70.5 us -> 0 us
  Pallas kernels: 0 us -> 54.9 us
  other arithmetic: 30 us -> 0.08 us
  blocking collectives: 41.3 us -> 13.9 us
  between operations: 15.7 us -> 0.81 us
  starting transfers between devices: 20.4 us -> 33.6 us
    unnamed x3 -> x0, waiting for transfers between devices: 117 us -> none
    conv_general_dilated x14 -> x0, local copies, waits for them, and re-layouts: 98.3 us -> none  [correlate(): lax.conv_general_dilated(padded, kernel, (1, 1), 'VALID', rhs_dilation=(2...]
    pallas_call x0 -> x8, Pallas kernels: none -> 54.9 us  [the longest x7 47.7 us: call(): pl.pallas_call(body, name=name, out_shape=[o for o, _ in outs], in_specs=...]
    psum x1 -> x0, waiting for transfers between devices: 46.3 us -> none  [per_device(): grad_one, grad_two = lax.psum((share_one, share_two), 'lat')]
    conv_general_dilated x4 -> x0, matrix products: 41.3 us -> none  [correlate(): lax.conv_general_dilated(padded, kernel, (1, 1), 'VALID', rhs_dilation=(2...]
    dot_general x18 -> x0, matrix products: 29.2 us -> none  [kernel_terms(): jnp.einsum('nhwc,nhwd->cd', padded[:, 2 * a:2 * a + height, 2 * b:2 * b +...]
    all_gather x2 -> x1, blocking collectives: 41.3 us -> 13.9 us  [per_device(): chunks = lax.all_gather(chunk, 'lat', axis=0)]
    unnamed x87 -> x30, local copies, waits for them, and re-layouts: 37.8 us -> 16.1 us
  transfers between devices with their start and end apart: 10 -> 12, of which waited for: 2 -> 4; matrix products, arithmetic and copies ran while one was open for 23% -> 0% of each run, Pallas kernels for 0% -> 16%
where the time goes in v2:
time: 137 us
  Pallas kernels  54.9 us (40%)
  starting transfers between devices  33.6 us (25%)
  waiting for transfers between devices  17.2 us (13%)
  local copies, waits for them, and re-layouts  16.1 us (12%)
  blocking collectives  13.9 us (10%)
    pallas_call x7, Pallas kernels, call(): pl.pallas_call(body, name=name, out_shape=[o for o, _ in outs], in_specs=...  47.7 us
    unnamed x30, local copies, waits for them, and re-layouts  16.1 us
    ppermute x6, waiting for transfers between devices, partner(): return lax.ppermute(value, 'fsdp', [(i, i ^ d) for i in range(shards)])  14 us
    all_gather x1, blocking collectives, per_device(): chunks = lax.all_gather(chunk, 'lat', axis=0)  13.9 us
    all_to_all x1, starting transfers between devices, per_device(): got = lax.all_to_all(terms, 'lat', 0, 0, tiled=True)  13.8 us
    ppermute x6, starting transfers between devices, partner(): return lax.ppermute(value, 'fsdp', [(i, i ^ d) for i in range(shards)])  10.2 us
    pallas_call x1, Pallas kernels, per_device(): pl.pallas_call(edge_body, name='edge', out_shape=[outs[0], outs[0]], in_s...  7.18 us
    ppermute x2, starting transfers between devices, edges(): lax.ppermute(bottom, 'lat', forward)  7.01 us
  transfers between devices with their start and end apart: 12, of which 4 were waited for; matrix products, arithmetic and copies ran while one was open for 0% of the time, Pallas kernels for 16%

profile of v2, /device:TPU:0, one launch (start us, length us, event | category | flops | bytes accessed | tf_op | source)
XLA Modules:
  0.0 136.6 jit_solution(8535509552492078635)
XLA Ops:
  0.6 0.1 pad_add_fusion.parity.place
  0.7 0.0 copy-start
  0.7 1.7 %copy-done = bf16[1,16,360,192]{2,3,1,0:T(8,128)(2,1)S(1)} copy-done((bf16[1,16,360,192]{2,3,1,0:T(8,128)(2,1)S(1)}, bf16[1,16,360,192]{2,3,1,0:T(8,128)(2,1)}, u32[]{:S(2)}) %copy-start) | copy-done | bytes 2211864
  2.4 0.0 copy-start.2
  2.4 1.7 %copy-done.2 = bf16[1,16,360,192]{2,3,1,0:T(8,128)(2,1)S(1)} copy-done((bf16[1,16,360,192]{2,3,1,0:T(8,128)(2,1)S(1)}, bf16[1,16,360,192]{2,3,1,0:T(8,128)(2,1)}, u32[]{:S(2)}) %copy-start.2) | copy-done | bytes 2211864
  4.0 0.0 copy-start.10
  4.1 0.9 copy-done.10
  5.0 0.0 copy-start.11
  5.0 0.9 copy-done.11
  5.9 0.9 pack.1
  6.8 5.1 %collective-permute-start.4 = (bf16[14,48,128]{2,1,0:T(8,128)(2,1)S(1)}, bf16[14,48,128]{2,1,0:T(8,128)(2,1)S(1)}, u32[]{:S(2)}, u32[]{:S(2)}) collective-permute-start(bf16[14,48,128]{2,1,0:T(8,128)(2,1)S(1)} %get-tuple-element.26.half), channel_id=1, source_target_pairs={{0,24},{8,16},{16,8},{24,0},{1,25},{9,17},{17,9},{25,1},{2,26},{10... | collective-permute-start | bytes 516104 | tf_op jit(solution)/shard_map/ppermute | solution.py:402
  11.9 0.0 collective-permute-start.3
  11.9 0.6 collective-permute-start.2
  12.5 4.7 %collective-permute-done.4.refs_2_ = bf16[14,48,128]{2,1,0:T(8,128)(2,1)S(1)} collective-permute-done((bf16[14,48,128]{2,1,0:T(8,128)(2,1)S(1)}, bf16[14,48,128]{2,1,0:T(8,128)(2,1)S(1)}, u32[]{:S(2)}, u32[]{:S(2)}) %collective-permute-start.4) | collective-permute-done | bytes 172064 | tf_op jit(solution)/shard_map/ppermute | solution.py:402
  17.2 9.4 %collective-permute-done.3.refs_1_ = bf16[14,48,128]{2,1,0:T(8,128)(2,1)S(1)} collective-permute-done((bf16[14,48,128]{2,1,0:T(8,128)(2,1)S(1)}, bf16[14,48,128]{2,1,0:T(8,128)(2,1)S(1)}, u32[]{:S(2)}, u32[]{:S(2)}) %collective-permute-start.3) | collective-permute-done | bytes 172064 | tf_op jit(solution)/shard_map/ppermute | solution.py:402
  26.6 0.0 collective-permute-done.2.refs_0_
  26.6 0.6 stack.13.own
  27.2 0.0 copy-start.8
  27.2 0.1 collective-permute-start.5
  27.3 2.4 %collective-permute-start = (bf16[4,192,360]{2,1,0:T(8,128)(2,1)S(1)}, bf16[4,192,360]{2,1,0:T(8,128)(2,1)S(1)}, u32[]{:S(2)}, u32[]{:S(2)}) collective-permute-start(bf16[4,192,360]{2,1,0:T(8,128)(2,1)S(1)} %get-tuple-element.24), channel_id=1, source_target_pairs={{0,1},{1,2},{2,3},{3,4},{4,5},{5,6},{6,7},{8,9},{9,10},{10,11},{11... | collective-permute-start | bytes 1658888 | tf_op jit(solution)/shard_map/ppermute | solution.py:399
  29.7 1.3 collective-permute-start.1
  31.0 0.3 collective-permute-done.above
  31.3 2.9 %collective-permute-done.1.below = bf16[4,192,360]{2,1,0:T(8,128)(2,1)S(1)} collective-permute-done((bf16[4,192,360]{2,1,0:T(8,128)(2,1)S(1)}, bf16[4,192,360]{2,1,0:T(8,128)(2,1)S(1)}, u32[]{:S(2)}, u32[]{:S(2)}) %collective-permute-start.1) | collective-permute-done | bytes 552992 | tf_op jit(solution)/shard_map/ppermute | solution.py:399
  34.2 0.0 copy-start.14
  34.2 0.0 collective-permute-done.5.other
  34.2 0.0 copy-done.8
  34.2 0.8 copy-done.14
  35.0 0.0 copy-start.12
  35.0 0.8 copy-done.12
  35.9 30.4 %stage.1 = (bf16[16,192,384]{2,1,0:T(8,128)(2,1)}, bf16[16,192,384]{2,1,0:T(8,128)(2,1)}, bf16[4,192,384]{2,1,0:T(8,128)(2,1)}, bf16[4,192,384]{2,1,0:T(8,128)(2,1)}, bf16[8,4,176,128]{3,2,1,0:T(8,128)(2,1)}) custom-call(s32[2]{0:T(128)S(1)} %pad_add_fusion.parity.place, bf16[16,192,360]{2,1,0:T(8,128)(2,1)} %bitcast.27, bf16[16,192,360]{2,1,0:T(8,128)(2,1)} %bitcast.31, ...), custom_call_target="tpu_custom_call" | custom-call | flops 15288238080 | bytes 16777216 | tf_op jit(solution)/shard_map/stage/pallas_call | solution.py:28
  66.3 13.8 %all-to-all-start = ((bf16[8,4,176,128]{3,2,1,0:T(8,128)(2,1)}), bf16[8,4,176,128]{3,2,1,0:T(8,128)(2,1)}, u32[]{:S(2)}, u32[]{:S(2)}) async-start(bf16[8,4,176,128]{3,2,1,0:T(8,128)(2,1)} %get-tuple-element.37), calls=%async_computation | async-start | bytes 2883584 | tf_op jit(solution)/shard_map/all_to_all | solution.py:457
  80.0 4.6 %collective-permute-start.6 = (bf16[4,192,384]{2,1,0:T(8,128)(2,1)}, bf16[4,192,384]{2,1,0:T(8,128)(2,1)}, u32[]{:S(2)}, u32[]{:S(2)}) collective-permute-start(bf16[4,192,384]{2,1,0:T(8,128)(2,1)} %get-tuple-element.29), channel_id=1, source_target_pairs={{0,1},{1,2},{2,3},{3,4},{4,5},{5,6},{6,7},{8,9},{9,10},{10,11},{11... | collective-permute-start | bytes 1769480 | tf_op jit(solution)/shard_map/ppermute | solution.py:399
  84.6 1.3 collective-permute-start.7
  85.9 0.0 copy-start.9
  85.9 1.1 copy-done.9
  87.0 0.0 copy-start.13
  87.0 1.1 copy-done.13
  88.1 0.0 copy-start.1
  88.1 13.3 %interior.1 = (bf16[16,192,360]{2,1,0:T(8,128)(2,1)}, bf16[16,192,360]{2,1,0:T(8,128)(2,1)}, bf16[192,1728]{1,0:T(8,128)(2,1)S(1)}, bf16[192,1728]{1,0:T(8,128)(2,1)S(1)}) custom-call(s32[2]{0:T(128)S(1)} %pad_add_fusion.parity.place, bf16[16,192,360]{2,1,0:T(8,128)(2,1)} %bitcast.28, bf16[16,192,360]{2,1,0:T(8,128)(2,1)} %bitcast.32, ...), custom_call_target="tpu_custom_call" | custom-call | flops 7644119040 | bytes 16777216 | tf_op jit(solution)/shard_map/interior/pallas_call | solution.py:28
  101.4 0.0 copy-start.6
  101.4 0.9 copy-done.6
  102.3 0.0 all-to-all-done.got
  102.3 1.6 %column.1 = (f32[176,128]{1,0:T(8,128)S(1)}, bf16[176,128]{1,0:T(8,128)(2,1)S(1)}, bf16[176,128]{1,0:T(8,128)(2,1)S(1)}, bf16[176,128]{1,0:T(8,128)(2,1)S(1)}) custom-call(s32[2]{0:T(128)S(1)} %pad_add_fusion.parity.place, bf16[8,4,176,128]{3,2,1,0:T(8,128)(2,1)} %all-to-all-done.got), custom_call_target="tpu_custom_call" | custom-call | tf_op jit(solution)/shard_map/column/pallas_call | solution.py:28
  103.9 0.1 collective-permute-start.8
  104.0 3.0 %collective-permute-start.9 = (bf16[176,128]{1,0:T(8,128)(2,1)S(1)}, bf16[176,128]{1,0:T(8,128)(2,1)S(1)}, u32[]{:S(2)}, u32[]{:S(2)}) collective-permute-start(bf16[176,128]{1,0:T(8,128)(2,1)S(1)} %get-tuple-element.40), channel_id=1, source_target_pairs={{0,16},{8,24},{16,0},{24,8},{1,17},{9,25},{17,1},{25,9},{2,18},{10... | collective-permute-start | bytes 135176 | tf_op jit(solution)/shard_map/ppermute | solution.py:402
  107.0 1.3 collective-permute-start.10
  108.3 0.0 collective-permute-done.6.above
  108.3 0.0 collective-permute-done.7.below
  108.3 0.0 copy-done.1
  108.3 0.0 copy-start.3
  108.4 1.7 %copy-done.3 = bf16[1,16,360,192]{2,3,1,0:T(8,128)(2,1)S(1)} copy-done((bf16[1,16,360,192]{2,3,1,0:T(8,128)(2,1)S(1)}, bf16[1,16,360,192]{2,3,1,0:T(8,128)(2,1)}, u32[]{:S(2)}) %copy-start.3) | copy-done | bytes 2211864
  110.0 0.0 copy-start.4
  110.0 1.7 %copy-done.4 = bf16[16,192,384]{2,1,0:T(8,128)(2,1)S(1)} copy-done((bf16[16,192,384]{2,1,0:T(8,128)(2,1)S(1)}, bf16[16,192,384]{2,1,0:T(8,128)(2,1)}, u32[]{:S(2)}) %copy-start.4) | copy-done | bytes 2359320
  111.7 0.0 copy-start.5
  111.7 1.7 %copy-done.5 = bf16[16,192,384]{2,1,0:T(8,128)(2,1)S(1)} copy-done((bf16[16,192,384]{2,1,0:T(8,128)(2,1)S(1)}, bf16[16,192,384]{2,1,0:T(8,128)(2,1)}, u32[]{:S(2)}) %copy-start.5) | copy-done | bytes 2359320
  113.3 0.0 copy-start.7
  113.3 1.1 copy-done.7
  114.4 7.2 %edge.1 = (bf16[16,192,360]{2,1,0:T(8,128)(2,1)}, bf16[16,192,360]{2,1,0:T(8,128)(2,1)}) custom-call(bf16[16,192,360]{2,1,0:T(8,128)(2,1)S(1)} %bitcast.30, bf16[16,192,360]{2,1,0:T(8,128)(2,1)S(1)} %bitcast.34, bf16[16,192,384]{2,1,0:T(8,128)(2,1)S(1)} %copy-done.4, ...), custom_call_target="tpu_custom_call", output_to_operand_aliasing={{0}: (8, {}), {1}: (9, {})} | custom-call | flops 1911029760 | bytes 4194304 | tf_op jit(solution)/shard_map/edge/pallas_call | solution.py:482
  121.6 0.0 collective-permute-done.8.refs_0_
  121.6 0.0 collective-permute-done.9.refs_1_
  121.6 0.0 collective-permute-done.10.refs_2_
  121.7 13.9 %all-gather = f32[1408,128]{1,0:T(8,128)S(1)} all-gather(f32[176,128]{1,0:T(8,128)S(1)} %chunk.1), channel_id=2, replica_groups=mesh['fsdp'=4,'lat'=8] {'lat'}, dimensions={0}, use_global_device_ids=true | all-gather | bytes 811008 | tf_op jit(solution)/shard_map/all_gather | solution.py:508
  135.6 1.0 unpack.1
  (1 shorter events, 0.0 us)
Async XLA Ops:
  0.7 1.7 %copy-start = (bf16[1,16,360,192]{2,3,1,0:T(8,128)(2,1)S(1)}, bf16[1,16,360,192]{2,3,1,0:T(8,128)(2,1)}, u32[]{:S(2)}) copy-start(bf16[1,16,360,192]{2,3,1,0:T(8,128)(2,1)} %param.4) | copy-start | bytes 6635524
  2.4 1.7 %copy-start.2 = (bf16[1,16,360,192]{2,3,1,0:T(8,128)(2,1)S(1)}, bf16[1,16,360,192]{2,3,1,0:T(8,128)(2,1)}, u32[]{:S(2)}) copy-start(bf16[1,16,360,192]{2,3,1,0:T(8,128)(2,1)} %param.5) | copy-start | bytes 6635524
  4.0 0.9 copy-start.10
  5.0 0.9 copy-start.11
  6.8 10.4 %collective-permute-start.4 = (bf16[14,48,128]{2,1,0:T(8,128)(2,1)S(1)}, bf16[14,48,128]{2,1,0:T(8,128)(2,1)S(1)}, u32[]{:S(2)}, u32[]{:S(2)}) collective-permute-start(bf16[14,48,128]{2,1,0:T(8,128)(2,1)S(1)} %get-tuple-element.26.half), channel_id=1, source_target_pairs={{0,24},{8,16},{16,8},{24,0},{1,25},{9,17},{17,9},{25,1},{2,26},{10... | collective-permute-start | bytes 516104 | tf_op jit(solution)/shard_map/ppermute | solution.py:402
  11.9 14.7 %collective-permute-start.3 = (bf16[14,48,128]{2,1,0:T(8,128)(2,1)S(1)}, bf16[14,48,128]{2,1,0:T(8,128)(2,1)S(1)}, u32[]{:S(2)}, u32[]{:S(2)}) collective-permute-start(bf16[14,48,128]{2,1,0:T(8,128)(2,1)S(1)} %get-tuple-element.26.half), channel_id=1, source_target_pairs={{0,16},{8,24},{16,0},{24,8},{1,17},{9,25},{17,1},{25,9},{2,18},{10... | collective-permute-start | bytes 516104 | tf_op jit(solution)/shard_map/ppermute | solution.py:402
  11.9 14.7 %collective-permute-start.2 = (bf16[14,48,128]{2,1,0:T(8,128)(2,1)S(1)}, bf16[14,48,128]{2,1,0:T(8,128)(2,1)S(1)}, u32[]{:S(2)}, u32[]{:S(2)}) collective-permute-start(bf16[14,48,128]{2,1,0:T(8,128)(2,1)S(1)} %get-tuple-element.26.half), channel_id=1, source_target_pairs={{0,8},{8,0},{16,24},{24,16},{1,9},{9,1},{17,25},{25,17},{2,10},{10... | collective-permute-start | bytes 516104 | tf_op jit(solution)/shard_map/ppermute | solution.py:402
  27.2 7.0 %copy-start.8 = (bf16[4,14,48,128]{3,2,1,0:T(8,128)(2,1)}, bf16[4,14,48,128]{3,2,1,0:T(8,128)(2,1)S(1)}, u32[]{:S(2)}) copy-start(bf16[4,14,48,128]{3,2,1,0:T(8,128)(2,1)S(1)} %stack.13.own) | copy-start | bytes 2064388
  27.2 7.0 %collective-permute-start.5 = (bf16[4,14,48,128]{3,2,1,0:T(8,128)(2,1)S(1)}, bf16[4,14,48,128]{3,2,1,0:T(8,128)(2,1)S(1)}, u32[]{:S(2)}, u32[]{:S(2)}) collective-permute-start(bf16[4,14,48,128]{3,2,1,0:T(8,128)(2,1)S(1)} %stack.13.own), channel_id=1, source_target_pairs={{0,1},{1,0},{2,3},{3,2},{4,5},{5,4},{6,7},{7,6},{8,9},{9,8},{10,11... | collective-permute-start | bytes 2064392 | tf_op jit(solution)/shard_map/ppermute | solution.py:429
  27.3 4.0 %collective-permute-start = (bf16[4,192,360]{2,1,0:T(8,128)(2,1)S(1)}, bf16[4,192,360]{2,1,0:T(8,128)(2,1)S(1)}, u32[]{:S(2)}, u32[]{:S(2)}) collective-permute-start(bf16[4,192,360]{2,1,0:T(8,128)(2,1)S(1)} %get-tuple-element.24), channel_id=1, source_target_pairs={{0,1},{1,2},{2,3},{3,4},{4,5},{5,6},{6,7},{8,9},{9,10},{10,11},{11... | collective-permute-start | bytes 1658888 | tf_op jit(solution)/shard_map/ppermute | solution.py:399
  29.7 4.5 %collective-permute-start.1 = (bf16[4,192,360]{2,1,0:T(8,128)(2,1)S(1)}, bf16[4,192,360]{2,1,0:T(8,128)(2,1)S(1)}, u32[]{:S(2)}, u32[]{:S(2)}) collective-permute-start(bf16[4,192,360]{2,1,0:T(8,128)(2,1)S(1)} %get-tuple-element.25), channel_id=1, source_target_pairs={{1,0},{2,1},{3,2},{4,3},{5,4},{6,5},{7,6},{9,8},{10,9},{11,10},{12... | collective-permute-start | bytes 1658888 | tf_op jit(solution)/shard_map/ppermute | solution.py:399
  34.2 0.8 copy-start.14
  35.0 0.8 copy-start.12
  66.3 36.0 %all-to-all-start = ((bf16[8,4,176,128]{3,2,1,0:T(8,128)(2,1)}), bf16[8,4,176,128]{3,2,1,0:T(8,128)(2,1)}, u32[]{:S(2)}, u32[]{:S(2)}) async-start(bf16[8,4,176,128]{3,2,1,0:T(8,128)(2,1)} %get-tuple-element.37), calls=%async_computation | async-start | bytes 2883584 | tf_op jit(solution)/shard_map/all_to_all | solution.py:457
  80.0 28.3 %collective-permute-start.6 = (bf16[4,192,384]{2,1,0:T(8,128)(2,1)}, bf16[4,192,384]{2,1,0:T(8,128)(2,1)}, u32[]{:S(2)}, u32[]{:S(2)}) collective-permute-start(bf16[4,192,384]{2,1,0:T(8,128)(2,1)} %get-tuple-element.29), channel_id=1, source_target_pairs={{0,1},{1,2},{2,3},{3,4},{4,5},{5,6},{6,7},{8,9},{9,10},{10,11},{11... | collective-permute-start | bytes 1769480 | tf_op jit(solution)/shard_map/ppermute | solution.py:399
  84.6 23.7 %collective-permute-start.7 = (bf16[4,192,384]{2,1,0:T(8,128)(2,1)}, bf16[4,192,384]{2,1,0:T(8,128)(2,1)}, u32[]{:S(2)}, u32[]{:S(2)}) collective-permute-start(bf16[4,192,384]{2,1,0:T(8,128)(2,1)} %get-tuple-element.30), channel_id=1, source_target_pairs={{1,0},{2,1},{3,2},{4,3},{5,4},{6,5},{7,6},{9,8},{10,9},{11,10},{12... | collective-permute-start | bytes 1769480 | tf_op jit(solution)/shard_map/ppermute | solution.py:399
  85.9 1.1 copy-start.9
  87.0 1.1 copy-start.13
  88.1 20.2 %copy-start.1 = (bf16[1,16,360,192]{2,3,1,0:T(8,128)(2,1)S(1)}, bf16[1,16,360,192]{2,3,1,0:T(8,128)(2,1)}, u32[]{:S(2)}) copy-start(bf16[1,16,360,192]{2,3,1,0:T(8,128)(2,1)} %param.4) | copy-start | bytes 6635524
  101.4 0.9 copy-start.6
  103.9 17.8 %collective-permute-start.8 = (bf16[176,128]{1,0:T(8,128)(2,1)S(1)}, bf16[176,128]{1,0:T(8,128)(2,1)S(1)}, u32[]{:S(2)}, u32[]{:S(2)}) collective-permute-start(bf16[176,128]{1,0:T(8,128)(2,1)S(1)} %get-tuple-element.39), channel_id=1, source_target_pairs={{0,8},{8,0},{16,24},{24,16},{1,9},{9,1},{17,25},{25,17},{2,10},{10... | collective-permute-start | bytes 135176 | tf_op jit(solution)/shard_map/ppermute | solution.py:402
  104.0 17.7 %collective-permute-start.9 = (bf16[176,128]{1,0:T(8,128)(2,1)S(1)}, bf16[176,128]{1,0:T(8,128)(2,1)S(1)}, u32[]{:S(2)}, u32[]{:S(2)}) collective-permute-start(bf16[176,128]{1,0:T(8,128)(2,1)S(1)} %get-tuple-element.40), channel_id=1, source_target_pairs={{0,16},{8,24},{16,0},{24,8},{1,17},{9,25},{17,1},{25,9},{2,18},{10... | collective-permute-start | bytes 135176 | tf_op jit(solution)/shard_map/ppermute | solution.py:402
  107.0 14.7 %collective-permute-start.10 = (bf16[176,128]{1,0:T(8,128)(2,1)S(1)}, bf16[176,128]{1,0:T(8,128)(2,1)S(1)}, u32[]{:S(2)}, u32[]{:S(2)}) collective-permute-start(bf16[176,128]{1,0:T(8,128)(2,1)S(1)} %get-tuple-element.41), channel_id=1, source_target_pairs={{0,24},{8,16},{16,8},{24,0},{1,25},{9,17},{17,9},{25,1},{2,26},{10... | collective-permute-start | bytes 135176 | tf_op jit(solution)/shard_map/ppermute | solution.py:402
  108.3 1.7 %copy-start.3 = (bf16[1,16,360,192]{2,3,1,0:T(8,128)(2,1)S(1)}, bf16[1,16,360,192]{2,3,1,0:T(8,128)(2,1)}, u32[]{:S(2)}) copy-start(bf16[1,16,360,192]{2,3,1,0:T(8,128)(2,1)} %param.5) | copy-start | bytes 6635524
  110.0 1.7 %copy-start.4 = (bf16[16,192,384]{2,1,0:T(8,128)(2,1)S(1)}, bf16[16,192,384]{2,1,0:T(8,128)(2,1)}, u32[]{:S(2)}) copy-start(bf16[16,192,384]{2,1,0:T(8,128)(2,1)} %get-tuple-element.27.hid) | copy-start | bytes 7077892
  111.7 1.7 %copy-start.5 = (bf16[16,192,384]{2,1,0:T(8,128)(2,1)S(1)}, bf16[16,192,384]{2,1,0:T(8,128)(2,1)}, u32[]{:S(2)}) copy-start(bf16[16,192,384]{2,1,0:T(8,128)(2,1)} %get-tuple-element.28.inn) | copy-start | bytes 7077892
  113.3 1.1 copy-start.7

commit v3 on v2

--- a/solution.py
+++ b/solution.py
@@ -52,9 +52,14 @@
     return jnp.concatenate([slab_of(tap), tail], axis=1)
 
 
-def pack_body(parity, one, two, source, upstream, half, top, bottom, sem):
+def pack_body(
+    parity, first, second, source, upstream, half, top, bottom, one, two, sem
+):
     height = source.shape[0]
-    copies = []
+    copies = [
+        pltpu.make_async_copy(first, one, sem.at[4]),
+        pltpu.make_async_copy(second, two, sem.at[5]),
+    ]
     for base, rows in ((0, source), (2, upstream)):
         for k, (ref, at) in enumerate(((top, 0), (bottom, height - 2))):
             copies.append(
@@ -64,6 +69,8 @@
             )
     for copy in copies:
         copy.start()
+    copies[0].wait()
+    copies[1].wait()
     for side in range(2):
 
         @pl.when(parity[0] == side)
@@ -72,13 +79,13 @@
                 for i in range(HALF):
                     half[k * HALF + i] = to_slab(lambda tap: kernel[tap], side * HALF + i)
 
-    for copy in copies:
+    for copy in copies[2:]:
         copy.wait()
 
 
 def stack_body(place, half, *refs):
-    out = refs[-1]
-    for d, piece in enumerate((half,) + refs[:-1]):
+    *pieces, _, _, out = refs
+    for d, piece in enumerate([half] + pieces):
         out[place[1] ^ d] = piece[...]
 
 
@@ -194,18 +201,31 @@
 
 
 def stage_body(
-    scale, shards, place, source, upstream, above, below, own, other,
+    scale, shards, place, source, upstream, above_in, below_in, own_in, other_in,
     hid, inn, top, bottom, terms,
-    src, ups, fcol, ccol, w1, a2, hidden, inner, one, two, sem, edge_sem,
+    src, ups, fcol, ccol, w1, a2, hidden, inner, one, two, above, below, own, other,
+    sem, edge_sem,
 ):
     height, _, lon = source.shape
     wide = fcol.shape[2]
+    firsts = [
+        pltpu.make_async_copy(a, b, edge_sem.at[4 + k])
+        for k, (a, b) in enumerate(
+            ((own_in, own), (other_in, other), (above_in, above), (below_in, below))
+        )
+    ]
+    for copy in firsts:
+        copy.start()
     loads = [chunked(source, src, sem.at[0]), chunked(upstream, ups, sem.at[1])]
     for pair in zip(*loads):
         for copy in pair:
             copy.start()
+    firsts[0].wait()
+    firsts[1].wait()
     load_weight(place, own, other, 0, w1, False)
     load_weight(place, own, other, 1, a2, True)
+    firsts[2].wait()
+    firsts[3].wait()
     for columns, base in ((fcol, 0), (ccol, 2)):
         for r in range(2):
             store_row(columns, r, above[base + r])
@@ -248,12 +268,18 @@
 
 
 def interior_body(
-    place, source, upstream, hid, inn, own, other,
-    out, grad, w2, a1,
-    src, ups, mid, cot, hcol, icol, left, right, sem,
+    place, source, upstream, hid, inn, own_in, other_in,
+    out, grad, w2_out, a1_out,
+    src, ups, mid, cot, hcol, icol, left, right, w2, a1, own, other, sem, weight_sem,
 ):
     height, _, lon = source.shape
     wide = hcol.shape[2]
+    firsts = [
+        pltpu.make_async_copy(a, b, weight_sem.at[k])
+        for k, (a, b) in enumerate(((own_in, own), (other_in, other)))
+    ]
+    for copy in firsts:
+        copy.start()
     work = []
     for k, args in enumerate(
         ((hid, mid, hcol, source, src, w2, left, out), (inn, cot, icol, upstream, ups, a1, right, grad))
@@ -265,9 +291,17 @@
                 copy.start()
         rows = Columns(columns, held, loads[0], 0, lon)
         work.append((rows, loads[1], columns, base, weight, result, target, sem.at[3 * k + 2]))
+    work[0][0].fill(2 * GROUP)
+    for copy in firsts:
+        copy.wait()
     load_weight(place, own, other, 1, w2, False)
     load_weight(place, own, other, 0, a1, True)
-    saves = []
+    saves = [
+        pltpu.make_async_copy(a, b, weight_sem.at[2 + k])
+        for k, (a, b) in enumerate(((w2, w2_out), (a1, a1_out)))
+    ]
+    for save in saves:
+        save.start()
     for rows, waits, columns, base, weight, result, target, done in work:
         rows.fill(GROUP + 4)
         waits[0].wait()
@@ -288,11 +322,19 @@
 
 
 def edge_body(
-    source, upstream, hid, inn, above, below, w2, a1, out_in, grad_in,
+    source, upstream, hid, inn, above_in, below_in, w2_in, a1_in, out_in, grad_in,
     out, grad,
-    res, mid, columns, result, sem,
+    res, mid, columns, result, above, below, w2, a1, sem,
 ):
     del out_in, grad_in
+    firsts = [
+        pltpu.make_async_copy(a, b, sem.at[3, k])
+        for k, (a, b) in enumerate(
+            ((above_in, above), (below_in, below), (w2_in, w2), (a1_in, a1))
+        )
+    ]
+    for copy in firsts:
+        copy.start()
     height, _, lon = source.shape
     wide = columns.shape[3]
     ends = (0, height - 4), (0, height - 2)
@@ -316,6 +358,8 @@
             )
     for copy in loads:
         copy.start()
+    firsts[0].wait()
+    firsts[1].wait()
     for k in range(2):
         for r in range(2):
             store_row(columns.at[2 * k], r, above[2 * k + r][:, :lon])
@@ -329,6 +373,7 @@
         rhs = jnp.concatenate(
             [taps_of(columns.at[2 * k + j], r) for j in range(2) for r in range(2)], axis=1
         )
+        firsts[2 + k].wait()
         value = jnp.dot(weight[...], rhs, preferred_element_type=F32)
         for j in range(2):
             for r in range(2):
@@ -410,12 +455,13 @@
         "pack",
         [
             (shape(2 * HALF, share, LANES), VMEM),
-            (shape(4, c, lon), ANY),
-            (shape(4, c, lon), ANY),
+            (shape(4, c, lon), VMEM),
+            (shape(4, c, lon), VMEM),
         ],
-        [SMEM, VMEM, VMEM, ANY, ANY],
+        [SMEM, ANY, ANY, ANY, ANY],
         (place, *small, source, upstream),
-        scratch=[pltpu.SemaphoreType.DMA((4,))],
+        scratch=[pltpu.VMEM((TAPS, share, c), BF16)] * 2 + [pltpu.SemaphoreType.DMA((6,))],
+        limit=60,
     )
     pieces = [partner(half, d) for d in others]
     above, below = edges(top, bottom)
@@ -423,8 +469,8 @@
         stack_body,
         "stack",
         [(shape(shards, 2 * HALF, share, LANES), VMEM)],
-        [SMEM] + [VMEM] * shards,
-        (place, half, *pieces),
+        [SMEM] + [VMEM] * shards + [ANY, ANY],
+        (place, half, *pieces, above, below),
     )
     other = lax.ppermute(own, "lat", swap)
 
@@ -435,6 +481,8 @@
     columns = pltpu.VMEM((height + 4, 3 * c, wide), BF16)
     matrix = pltpu.VMEM((c, TAPS * c), BF16)
     total = pltpu.VMEM((TAPS * c, c), F32)
+    halo = pltpu.VMEM((4, c, lon), BF16)
+    gathered = pltpu.VMEM(own.shape, BF16)
     hid, inn, top, bottom, terms = call(
         functools.partial(stage_body, scale, shards),
         "stage",
@@ -445,11 +493,12 @@
             (edge, ANY),
             (shape(bands, shards, 2 * depth, LANES), VMEM),
         ],
-        [SMEM, ANY, ANY, VMEM, VMEM, VMEM, VMEM],
+        [SMEM] + [ANY] * 6,
         (place, source, upstream, above, below, own, other),
         scratch=[plain, plain, columns, columns, matrix, matrix, lined, lined, total, total]
-        + [pltpu.SemaphoreType.DMA((4, groups)), pltpu.SemaphoreType.DMA((4,))],
-        limit=52,
+        + [halo, halo, gathered, gathered]
+        + [pltpu.SemaphoreType.DMA((4, groups)), pltpu.SemaphoreType.DMA((8,))],
+        limit=60,
         flops=4 * conv_flops,
         nbytes=1 << 24,
     )
@@ -457,16 +506,17 @@
     got = lax.all_to_all(terms, "lat", 0, 0, tiled=True)
     columns = pltpu.VMEM((height, 3 * c, wide), BF16)
     outs = (shape(height, c, lon), ANY)
-    weight = (shape(c, TAPS * c), VMEM)
+    weight = (shape(c, TAPS * c), ANY)
     out, grad, w2, a1 = call(
         interior_body,
         "interior",
         [outs, outs, weight, weight],
-        [SMEM, ANY, ANY, ANY, ANY, VMEM, VMEM],
+        [SMEM] + [ANY] * 6,
         (place, source, upstream, hid, inn, own, other),
         scratch=[plain, plain, lined, lined, columns, columns, plain, plain]
-        + [pltpu.SemaphoreType.DMA((6, groups))],
-        limit=50,
+        + [matrix, matrix, gathered, gathered]
+        + [pltpu.SemaphoreType.DMA((6, groups)), pltpu.SemaphoreType.DMA((4,))],
+        limit=60,
         flops=2 * conv_flops,
         nbytes=1 << 24,
     )
@@ -483,7 +533,7 @@
         edge_body,
         name="edge",
         out_shape=[outs[0], outs[0]],
-        in_specs=[ANY] * 4 + [VMEM] * 4 + [ANY] * 2,
+        in_specs=[ANY] * 10,
         out_specs=[ANY, ANY],
         input_output_aliases={8: 0, 9: 1},
         scratch_shapes=[
@@ -491,9 +541,13 @@
             pltpu.VMEM((4, 4, c, wide), BF16),
             pltpu.VMEM((4, 6, 3 * c, wide), BF16),
             pltpu.VMEM((4, 2, c, lon), BF16),
-            pltpu.SemaphoreType.DMA((3, 4)),
+            pltpu.VMEM(edge.shape, BF16),
+            pltpu.VMEM(edge.shape, BF16),
+            matrix,
+            matrix,
+            pltpu.SemaphoreType.DMA((4, 4)),
         ],
-        compiler_params=pltpu.CompilerParams(vmem_limit_bytes=32 << 20),
+        compiler_params=pltpu.CompilerParams(vmem_limit_bytes=60 << 20),
         cost_estimate=pl.CostEstimate(
             flops=conv_flops // 2, bytes_accessed=1 << 22, transcendentals=0
         ),

time: 137 us -> 121 us (0.88)
  local copies, waits for them, and re-layouts: 16.1 us -> 3.1 us
  starting transfers between devices: 33.6 us -> 22.5 us
  Pallas kernels: 54.9 us -> 60.4 us
  blocking collectives: 13.9 us -> 16.5 us
    unnamed x30 -> x20, local copies, waits for them, and re-layouts: 16.1 us -> 3.1 us
    all_to_all x1, starting transfers between devices: 13.8 us -> 4.89 us  [per_device(): got = lax.all_to_all(terms, 'lat', 0, 0, tiled=True)]
    pallas_call x7, Pallas kernels: 47.7 us -> 52.2 us  [call(): pl.pallas_call(body, name=name, out_shape=[o for o, _ in outs], in_specs=...]
    ppermute x2, waiting for transfers between devices: 2.92 us -> 0.01 us  [edges(): lax.ppermute(top, 'lat', backward)]
    all_gather x1, blocking collectives: 13.9 us -> 16.5 us  [per_device(): chunks = lax.all_gather(chunk, 'lat', axis=0)]
    ppermute x2, starting transfers between devices: 7.01 us -> 4.83 us  [edges(): lax.ppermute(bottom, 'lat', forward)]
    ppermute x1, waiting for transfers between devices: 0.01 us -> 1.77 us  [per_device(): other = lax.ppermute(own, 'lat', swap)]
  transfers between devices with their start and end apart: 12 -> 12, of which waited for: 4 -> 4; matrix products, arithmetic and copies ran while one was open for 0% -> 0% of each run, Pallas kernels for 16% -> 20%
where the time goes in v3:
time: 121 us
  Pallas kernels  60.4 us (50%)
  starting transfers between devices  22.5 us (19%)
  waiting for transfers between devices  16.8 us (14%)
  blocking collectives  16.5 us (14%)
  local copies, waits for them, and re-layouts  3.1 us (3%)
    pallas_call x7, Pallas kernels, call(): pl.pallas_call(body, name=name, out_shape=[o for o, _ in outs], in_specs=...  52.2 us
    all_gather x1, blocking collectives, per_device(): chunks = lax.all_gather(chunk, 'lat', axis=0)  16.5 us
    ppermute x6, waiting for transfers between devices, partner(): return lax.ppermute(value, 'fsdp', [(i, i ^ d) for i in range(shards)])  14.6 us
    ppermute x6, starting transfers between devices, partner(): return lax.ppermute(value, 'fsdp', [(i, i ^ d) for i in range(shards)])  9.58 us
    pallas_call x1, Pallas kernels, per_device(): pl.pallas_call(edge_body, name='edge', out_shape=[outs[0], outs[0]], in_s...  8.2 us
    all_to_all x1, starting transfers between devices, per_device(): got = lax.all_to_all(terms, 'lat', 0, 0, tiled=True)  4.89 us
    ppermute x2, starting transfers between devices, edges(): lax.ppermute(bottom, 'lat', forward)  4.83 us
    unnamed x20, local copies, waits for them, and re-layouts  3.1 us
  transfers between devices with their start and end apart: 12, of which 4 were waited for; matrix products, arithmetic and copies ran while one was open for 0% of the time, Pallas kernels for 20%

profile of v3, /device:TPU:0, one launch (start us, length us, event | category | flops | bytes accessed | tf_op | source)
XLA Modules:
  0.0 120.7 jit_solution(10368042468341891382)
XLA Ops:
  0.6 0.6 pad_add_fusion.parity.place
  1.2 0.0 copy-start.4
  1.2 3.4 %pack.1 = (bf16[14,48,128]{2,1,0:T(8,128)(2,1)}, bf16[4,192,360]{2,1,0:T(8,128)(2,1)}, bf16[4,192,360]{2,1,0:T(8,128)(2,1)}) custom-call(s32[2]{0:T(128)} %pad_add_fusion.parity.place, bf16[9,48,192]{2,1,0:T(8,128)(2,1)} %bitcast.38, bf16[9,48,192]{2,1,0:T(8,128)(2,1)} %bitcast.39, bf16[16,192,360]{2,1,0:T(8,128)(2,1)} %bitcast.28, ...), custom_call_target="tpu_custom_call" | custom-call | tf_op jit(solution)/shard_map/pack/pallas_call | solution.py:28
  4.6 2.4 %collective-permute-start = (bf16[4,192,360]{2,1,0:T(8,128)(2,1)}, bf16[4,192,360]{2,1,0:T(8,128)(2,1)S(1)}, u32[]{:S(2)}, u32[]{:S(2)}) collective-permute-start(bf16[4,192,360]{2,1,0:T(8,128)(2,1)} %get-tuple-element.24), channel_id=1, source_target_pairs={{0,1},{1,2},{2,3},{3,4},{4,5},{5,6},{6,7},{8,9},{9,10},{10,11},{11... | collective-permute-start | bytes 1658888 | tf_op jit(solution)/shard_map/ppermute | solution.py:444
  7.0 1.3 %collective-permute-start.1 = (bf16[4,192,360]{2,1,0:T(8,128)(2,1)}, bf16[4,192,360]{2,1,0:T(8,128)(2,1)S(1)}, u32[]{:S(2)}, u32[]{:S(2)}) collective-permute-start(bf16[4,192,360]{2,1,0:T(8,128)(2,1)} %get-tuple-element.25), channel_id=1, source_target_pairs={{1,0},{2,1},{3,2},{4,3},{5,4},{6,5},{7,6},{9,8},{10,9},{11,10},{12... | collective-permute-start | bytes 1658888 | tf_op jit(solution)/shard_map/ppermute | solution.py:444
  8.3 4.5 %collective-permute-start.4 = (bf16[14,48,128]{2,1,0:T(8,128)(2,1)}, bf16[14,48,128]{2,1,0:T(8,128)(2,1)S(1)}, u32[]{:S(2)}, u32[]{:S(2)}) collective-permute-start(bf16[14,48,128]{2,1,0:T(8,128)(2,1)} %get-tuple-element.26.half), channel_id=1, source_target_pairs={{0,24},{8,16},{16,8},{24,0},{1,25},{9,17},{17,9},{25,1},{2,26},{10... | collective-permute-start | bytes 516104 | tf_op jit(solution)/shard_map/ppermute | solution.py:447
  12.8 0.0 collective-permute-start.3
  12.8 0.6 collective-permute-start.2
  13.4 3.2 %collective-permute-done.4.refs_2_ = bf16[14,48,128]{2,1,0:T(8,128)(2,1)S(1)} collective-permute-done((bf16[14,48,128]{2,1,0:T(8,128)(2,1)}, bf16[14,48,128]{2,1,0:T(8,128)(2,1)S(1)}, u32[]{:S(2)}, u32[]{:S(2)}) %collective-permute-start.4) | collective-permute-done | bytes 172064 | tf_op jit(solution)/shard_map/ppermute | solution.py:447
  16.6 11.4 %collective-permute-done.3.refs_1_ = bf16[14,48,128]{2,1,0:T(8,128)(2,1)S(1)} collective-permute-done((bf16[14,48,128]{2,1,0:T(8,128)(2,1)}, bf16[14,48,128]{2,1,0:T(8,128)(2,1)S(1)}, u32[]{:S(2)}, u32[]{:S(2)}) %collective-permute-start.3) | collective-permute-done | bytes 172064 | tf_op jit(solution)/shard_map/ppermute | solution.py:447
  28.0 0.0 collective-permute-done.2.refs_0_
  28.0 0.0 collective-permute-done.refs_3_.above_in
  28.0 0.0 copy-start.1
  28.0 0.0 collective-permute-done.1.refs_4_.below_in
  28.0 0.0 copy-done.4
  28.0 0.0 copy-start.3
  28.1 1.1 copy-done.3
  29.2 0.0 copy-start.2
  29.2 0.6 stack.13.own_in
  29.8 0.0 copy-start
  29.8 0.6 collective-permute-start.5
  30.4 1.8 %collective-permute-done.5.other_in = bf16[4,14,48,128]{3,2,1,0:T(8,128)(2,1)S(1)} collective-permute-done((bf16[4,14,48,128]{3,2,1,0:T(8,128)(2,1)S(1)}, bf16[4,14,48,128]{3,2,1,0:T(8,128)(2,1)S(1)}, u32[]{:S(2)}, u32[]{:S(2)}) %collective-permute-start.5) | collective-permute-done | bytes 688160 | tf_op jit(solution)/shard_map/ppermute | solution.py:475
  32.2 0.0 copy-done.1
  32.2 0.0 copy-done.2
  32.2 0.0 copy-done
  32.2 0.0 copy-start.8
  32.2 0.9 copy-done.8
  33.1 31.1 %stage.1 = (bf16[16,192,384]{2,1,0:T(8,128)(2,1)}, bf16[16,192,384]{2,1,0:T(8,128)(2,1)}, bf16[4,192,384]{2,1,0:T(8,128)(2,1)}, bf16[4,192,384]{2,1,0:T(8,128)(2,1)}, bf16[8,4,176,128]{3,2,1,0:T(8,128)(2,1)}) custom-call(s32[2]{0:T(128)} %pad_add_fusion.parity.place, bf16[16,192,360]{2,1,0:T(8,128)(2,1)} %bitcast.29, bf16[16,192,360]{2,1,0:T(8,128)(2,1)} %bitcast.33, ...), custom_call_target="tpu_custom_call" | custom-call | flops 15288238080 | bytes 16777216 | tf_op jit(solution)/shard_map/stage/pallas_call | solution.py:28
  64.2 0.0 copy-start.9
  64.2 4.9 %all-to-all-start = ((bf16[8,4,176,128]{3,2,1,0:T(8,128)(2,1)}), bf16[8,4,176,128]{3,2,1,0:T(8,128)(2,1)S(1)}, u32[]{:S(2)}, u32[]{:S(2)}) async-start(bf16[8,4,176,128]{3,2,1,0:T(8,128)(2,1)} %get-tuple-element.37), calls=%async_computation | async-start | bytes 2883584 | tf_op jit(solution)/shard_map/all_to_all | solution.py:506
  69.1 2.4 %collective-permute-start.6 = (bf16[4,192,384]{2,1,0:T(8,128)(2,1)}, bf16[4,192,384]{2,1,0:T(8,128)(2,1)S(1)}, u32[]{:S(2)}, u32[]{:S(2)}) collective-permute-start(bf16[4,192,384]{2,1,0:T(8,128)(2,1)} %get-tuple-element.29), channel_id=1, source_target_pairs={{0,1},{1,2},{2,3},{3,4},{4,5},{5,6},{6,7},{8,9},{9,10},{10,11},{11... | collective-permute-start | bytes 1769480 | tf_op jit(solution)/shard_map/ppermute | solution.py:444
  71.5 0.0 copy-done.9
  71.5 1.3 %collective-permute-start.7 = (bf16[4,192,384]{2,1,0:T(8,128)(2,1)S(1)}, bf16[4,192,384]{2,1,0:T(8,128)(2,1)S(1)}, u32[]{:S(2)}, u32[]{:S(2)}) collective-permute-start(bf16[4,192,384]{2,1,0:T(8,128)(2,1)S(1)} %copy-done.9), channel_id=1, source_target_pairs={{1,0},{2,1},{3,2},{4,3},{5,4},{6,5},{7,6},{9,8},{10,9},{11,10},{12... | collective-permute-start | bytes 1769480 | tf_op jit(solution)/shard_map/ppermute | solution.py:444
  72.8 0.0 copy-start.5
  72.9 15.4 %interior.1 = (bf16[16,192,360]{2,1,0:T(8,128)(2,1)}, bf16[16,192,360]{2,1,0:T(8,128)(2,1)}, bf16[192,1728]{1,0:T(8,128)(2,1)}, bf16[192,1728]{1,0:T(8,128)(2,1)}) custom-call(s32[2]{0:T(128)} %pad_add_fusion.parity.place, bf16[16,192,360]{2,1,0:T(8,128)(2,1)} %bitcast.30, bf16[16,192,360]{2,1,0:T(8,128)(2,1)} %bitcast.34, ...), custom_call_target="tpu_custom_call" | custom-call | flops 7644119040 | bytes 16777216 | tf_op jit(solution)/shard_map/interior/pallas_call | solution.py:28
  88.2 0.5 all-to-all-done.got
  88.7 0.0 copy-done.5
  88.7 0.7 column.1
  89.5 0.1 collective-permute-start.8
  89.5 3.0 %collective-permute-start.9 = (bf16[176,128]{1,0:T(8,128)(2,1)S(1)}, bf16[176,128]{1,0:T(8,128)(2,1)S(1)}, u32[]{:S(2)}, u32[]{:S(2)}) collective-permute-start(bf16[176,128]{1,0:T(8,128)(2,1)S(1)} %get-tuple-element.40), channel_id=1, source_target_pairs={{0,16},{8,24},{16,0},{24,8},{1,17},{9,25},{17,1},{25,9},{2,18},{10... | collective-permute-start | bytes 135176 | tf_op jit(solution)/shard_map/ppermute | solution.py:447
  92.6 1.3 %collective-permute-start.10 = (bf16[176,128]{1,0:T(8,128)(2,1)S(1)}, bf16[176,128]{1,0:T(8,128)(2,1)S(1)}, u32[]{:S(2)}, u32[]{:S(2)}) collective-permute-start(bf16[176,128]{1,0:T(8,128)(2,1)S(1)} %get-tuple-element.41), channel_id=1, source_target_pairs={{0,24},{8,16},{16,8},{24,0},{1,25},{9,17},{17,9},{25,1},{2,26},{10... | collective-permute-start | bytes 135176 | tf_op jit(solution)/shard_map/ppermute | solution.py:447
  93.9 0.0 collective-permute-done.6.above_in
  93.9 0.0 copy-start.6
  93.9 0.0 collective-permute-done.7.below_in
  93.9 0.0 copy-start.7
  93.9 0.8 copy-done.6
  94.7 0.2 copy-done.7
  95.0 8.2 %edge.1 = (bf16[16,192,360]{2,1,0:T(8,128)(2,1)}, bf16[16,192,360]{2,1,0:T(8,128)(2,1)}) custom-call(bf16[16,192,360]{2,1,0:T(8,128)(2,1)} %bitcast.31, bf16[16,192,360]{2,1,0:T(8,128)(2,1)} %bitcast.35, bf16[16,192,384]{2,1,0:T(8,128)(2,1)} %get-tuple-element.27.hid, ...), custom_call_target="tpu_custom_call", output_to_operand_aliasing={{0}: (8, {}), {1}: (9, {})} | custom-call | flops 1911029760 | bytes 4194304 | tf_op jit(solution)/shard_map/edge/pallas_call | solution.py:532
  103.2 0.0 collective-permute-done.8.refs_0_
  103.2 0.0 collective-permute-done.9.refs_1_
  103.2 0.0 collective-permute-done.10.refs_2_
  103.2 16.5 %all-gather = f32[1408,128]{1,0:T(8,128)S(1)} all-gather(f32[176,128]{1,0:T(8,128)S(1)} %chunk.1), channel_id=2, replica_groups=mesh['fsdp'=4,'lat'=8] {'lat'}, dimensions={0}, use_global_device_ids=true | all-gather | bytes 811008 | tf_op jit(solution)/shard_map/all_gather | solution.py:562
  119.7 1.0 unpack.1
  (1 shorter events, 0.0 us)
Async XLA Ops:
  1.2 26.8 %copy-start.4 = (s32[2]{0:T(128)S(1)}, s32[2]{0:T(128)}, u32[]{:S(2)}) copy-start(s32[2]{0:T(128)} %pad_add_fusion.parity.place) | copy-start | bytes 28
  4.6 23.4 %collective-permute-start = (bf16[4,192,360]{2,1,0:T(8,128)(2,1)}, bf16[4,192,360]{2,1,0:T(8,128)(2,1)S(1)}, u32[]{:S(2)}, u32[]{:S(2)}) collective-permute-start(bf16[4,192,360]{2,1,0:T(8,128)(2,1)} %get-tuple-element.24), channel_id=1, source_target_pairs={{0,1},{1,2},{2,3},{3,4},{4,5},{5,6},{6,7},{8,9},{9,10},{10,11},{11... | collective-permute-start | bytes 1658888 | tf_op jit(solution)/shard_map/ppermute | solution.py:444
  7.0 21.0 %collective-permute-start.1 = (bf16[4,192,360]{2,1,0:T(8,128)(2,1)}, bf16[4,192,360]{2,1,0:T(8,128)(2,1)S(1)}, u32[]{:S(2)}, u32[]{:S(2)}) collective-permute-start(bf16[4,192,360]{2,1,0:T(8,128)(2,1)} %get-tuple-element.25), channel_id=1, source_target_pairs={{1,0},{2,1},{3,2},{4,3},{5,4},{6,5},{7,6},{9,8},{10,9},{11,10},{12... | collective-permute-start | bytes 1658888 | tf_op jit(solution)/shard_map/ppermute | solution.py:444
  8.3 8.3 %collective-permute-start.4 = (bf16[14,48,128]{2,1,0:T(8,128)(2,1)}, bf16[14,48,128]{2,1,0:T(8,128)(2,1)S(1)}, u32[]{:S(2)}, u32[]{:S(2)}) collective-permute-start(bf16[14,48,128]{2,1,0:T(8,128)(2,1)} %get-tuple-element.26.half), channel_id=1, source_target_pairs={{0,24},{8,16},{16,8},{24,0},{1,25},{9,17},{17,9},{25,1},{2,26},{10... | collective-permute-start | bytes 516104 | tf_op jit(solution)/shard_map/ppermute | solution.py:447
  12.8 15.2 %collective-permute-start.3 = (bf16[14,48,128]{2,1,0:T(8,128)(2,1)}, bf16[14,48,128]{2,1,0:T(8,128)(2,1)S(1)}, u32[]{:S(2)}, u32[]{:S(2)}) collective-permute-start(bf16[14,48,128]{2,1,0:T(8,128)(2,1)} %get-tuple-element.26.half), channel_id=1, source_target_pairs={{0,16},{8,24},{16,0},{24,8},{1,17},{9,25},{17,1},{25,9},{2,18},{10... | collective-permute-start | bytes 516104 | tf_op jit(solution)/shard_map/ppermute | solution.py:447
  12.8 15.2 %collective-permute-start.2 = (bf16[14,48,128]{2,1,0:T(8,128)(2,1)}, bf16[14,48,128]{2,1,0:T(8,128)(2,1)S(1)}, u32[]{:S(2)}, u32[]{:S(2)}) collective-permute-start(bf16[14,48,128]{2,1,0:T(8,128)(2,1)} %get-tuple-element.26.half), channel_id=1, source_target_pairs={{0,8},{8,0},{16,24},{24,16},{1,9},{9,1},{17,25},{25,17},{2,10},{10... | collective-permute-start | bytes 516104 | tf_op jit(solution)/shard_map/ppermute | solution.py:447
  28.0 4.1 %copy-start.1 = (bf16[4,192,360]{2,1,0:T(8,128)(2,1)}, bf16[4,192,360]{2,1,0:T(8,128)(2,1)S(1)}, u32[]{:S(2)}) copy-start(bf16[4,192,360]{2,1,0:T(8,128)(2,1)S(1)} %collective-permute-done.refs_3_.above_in) | copy-start | bytes 1658884
  28.0 1.1 copy-start.3
  29.2 3.0 %copy-start.2 = (bf16[4,192,360]{2,1,0:T(8,128)(2,1)}, bf16[4,192,360]{2,1,0:T(8,128)(2,1)S(1)}, u32[]{:S(2)}) copy-start(bf16[4,192,360]{2,1,0:T(8,128)(2,1)S(1)} %collective-permute-done.1.refs_4_.below_in) | copy-start | bytes 1658884
  29.8 2.4 %copy-start = (bf16[4,14,48,128]{3,2,1,0:T(8,128)(2,1)}, bf16[4,14,48,128]{3,2,1,0:T(8,128)(2,1)S(1)}, u32[]{:S(2)}) copy-start(bf16[4,14,48,128]{3,2,1,0:T(8,128)(2,1)S(1)} %stack.13.own_in) | copy-start | bytes 2064388
  29.8 2.4 %collective-permute-start.5 = (bf16[4,14,48,128]{3,2,1,0:T(8,128)(2,1)S(1)}, bf16[4,14,48,128]{3,2,1,0:T(8,128)(2,1)S(1)}, u32[]{:S(2)}, u32[]{:S(2)}) collective-permute-start(bf16[4,14,48,128]{3,2,1,0:T(8,128)(2,1)S(1)} %stack.13.own_in), channel_id=1, source_target_pairs={{0,1},{1,0},{2,3},{3,2},{4,5},{5,4},{6,7},{7,6},{8,9},{9,8},{10,11... | collective-permute-start | bytes 2064392 | tf_op jit(solution)/shard_map/ppermute | solution.py:475
  32.2 0.9 copy-start.8
  64.2 7.3 %copy-start.9 = (bf16[4,192,384]{2,1,0:T(8,128)(2,1)S(1)}, bf16[4,192,384]{2,1,0:T(8,128)(2,1)}, u32[]{:S(2)}) copy-start(bf16[4,192,384]{2,1,0:T(8,128)(2,1)} %get-tuple-element.30) | copy-start | bytes 1769476
  64.2 24.5 %all-to-all-start = ((bf16[8,4,176,128]{3,2,1,0:T(8,128)(2,1)}), bf16[8,4,176,128]{3,2,1,0:T(8,128)(2,1)S(1)}, u32[]{:S(2)}, u32[]{:S(2)}) async-start(bf16[8,4,176,128]{3,2,1,0:T(8,128)(2,1)} %get-tuple-element.37), calls=%async_computation | async-start | bytes 2883584 | tf_op jit(solution)/shard_map/all_to_all | solution.py:506
  69.1 24.8 %collective-permute-start.6 = (bf16[4,192,384]{2,1,0:T(8,128)(2,1)}, bf16[4,192,384]{2,1,0:T(8,128)(2,1)S(1)}, u32[]{:S(2)}, u32[]{:S(2)}) collective-permute-start(bf16[4,192,384]{2,1,0:T(8,128)(2,1)} %get-tuple-element.29), channel_id=1, source_target_pairs={{0,1},{1,2},{2,3},{3,4},{4,5},{5,6},{6,7},{8,9},{9,10},{10,11},{11... | collective-permute-start | bytes 1769480 | tf_op jit(solution)/shard_map/ppermute | solution.py:444
  71.5 22.4 %collective-permute-start.7 = (bf16[4,192,384]{2,1,0:T(8,128)(2,1)S(1)}, bf16[4,192,384]{2,1,0:T(8,128)(2,1)S(1)}, u32[]{:S(2)}, u32[]{:S(2)}) collective-permute-start(bf16[4,192,384]{2,1,0:T(8,128)(2,1)S(1)} %copy-done.9), channel_id=1, source_target_pairs={{1,0},{2,1},{3,2},{4,3},{5,4},{6,5},{7,6},{9,8},{10,9},{11,10},{12... | collective-permute-start | bytes 1769480 | tf_op jit(solution)/shard_map/ppermute | solution.py:444
  72.8 15.9 %copy-start.5 = (s32[2]{0:T(128)S(1)}, s32[2]{0:T(128)}, u32[]{:S(2)}) copy-start(s32[2]{0:T(128)} %pad_add_fusion.parity.place) | copy-start | bytes 28
  89.5 13.7 %collective-permute-start.8 = (bf16[176,128]{1,0:T(8,128)(2,1)S(1)}, bf16[176,128]{1,0:T(8,128)(2,1)S(1)}, u32[]{:S(2)}, u32[]{:S(2)}) collective-permute-start(bf16[176,128]{1,0:T(8,128)(2,1)S(1)} %get-tuple-element.39), channel_id=1, source_target_pairs={{0,8},{8,0},{16,24},{24,16},{1,9},{9,1},{17,25},{25,17},{2,10},{10... | collective-permute-start | bytes 135176 | tf_op jit(solution)/shard_map/ppermute | solution.py:447
  89.5 13.6 %collective-permute-start.9 = (bf16[176,128]{1,0:T(8,128)(2,1)S(1)}, bf16[176,128]{1,0:T(8,128)(2,1)S(1)}, u32[]{:S(2)}, u32[]{:S(2)}) collective-permute-start(bf16[176,128]{1,0:T(8,128)(2,1)S(1)} %get-tuple-element.40), channel_id=1, source_target_pairs={{0,16},{8,24},{16,0},{24,8},{1,17},{9,25},{17,1},{25,9},{2,18},{10... | collective-permute-start | bytes 135176 | tf_op jit(solution)/shard_map/ppermute | solution.py:447
  92.6 10.6 %collective-permute-start.10 = (bf16[176,128]{1,0:T(8,128)(2,1)S(1)}, bf16[176,128]{1,0:T(8,128)(2,1)S(1)}, u32[]{:S(2)}, u32[]{:S(2)}) collective-permute-start(bf16[176,128]{1,0:T(8,128)(2,1)S(1)} %get-tuple-element.41), channel_id=1, source_target_pairs={{0,24},{8,16},{16,8},{24,0},{1,25},{9,17},{17,9},{25,1},{2,26},{10... | collective-permute-start | bytes 135176 | tf_op jit(solution)/shard_map/ppermute | solution.py:447
  93.9 0.8 copy-start.6
  93.9 1.0 copy-start.7

commit v4 on v2

--- a/solution.py
+++ b/solution.py
@@ -10,14 +10,13 @@
 BF16 = jnp.bfloat16
 F32 = jnp.float32
 VMEM = pl.BlockSpec(memory_space=pltpu.VMEM)
-SMEM = pl.BlockSpec(memory_space=pltpu.SMEM)
 ANY = pl.BlockSpec(memory_space=pltpu.HBM)
 TAPS = 9
 SLABS = TAPS + (TAPS + 1) // 2
 HALF = SLABS // 2
 LANES = 128
 GROUP = 4
-SPAN = 4
+SPAN = 8
 
 
 def shape(*dims, dtype=BF16):
@@ -52,7 +51,28 @@
     return jnp.concatenate([slab_of(tap), tail], axis=1)
 
 
-def pack_body(parity, one, two, source, upstream, half, top, bottom, sem):
+def parity():
+    return lax.rem(lax.axis_index("lat"), 2)
+
+
+def pack_body(first, second, half, rest, one, two, sem):
+    copies = [
+        pltpu.make_async_copy(first, one, sem.at[0]),
+        pltpu.make_async_copy(second, two, sem.at[1]),
+    ]
+    start(copies)
+    wait(copies)
+    mine = parity() == 0
+    for k, kernel in enumerate((one, two)):
+        for i in range(HALF):
+            low = to_slab(lambda tap: kernel[tap], i)
+            high = to_slab(lambda tap: kernel[tap], HALF + i)
+            half[k * HALF + i] = jnp.where(mine, low, high)
+            rest[k * HALF + i] = jnp.where(mine, high, low)
+
+
+def ends_body(after, source, upstream, top, bottom, sem):
+    del after
     height = source.shape[0]
     copies = []
     for base, rows in ((0, source), (2, upstream)):
@@ -62,30 +82,28 @@
                     rows.at[pl.ds(at, 2)], ref.at[pl.ds(base, 2)], sem.at[base + k]
                 )
             )
-    for copy in copies:
-        copy.start()
-    for side in range(2):
-
-        @pl.when(parity[0] == side)
-        def _():
-            for k, kernel in enumerate((one, two)):
-                for i in range(HALF):
-                    half[k * HALF + i] = to_slab(lambda tap: kernel[tap], side * HALF + i)
-
-    for copy in copies:
-        copy.wait()
-
-
-def stack_body(place, half, *refs):
-    out = refs[-1]
-    for d, piece in enumerate((half,) + refs[:-1]):
-        out[place[1] ^ d] = piece[...]
-
-
-def load_weight(place, own, other, which, weight, adjoint):
+    start(copies)
+    wait(copies)
+
+
+def gate_body(*refs):
+    del refs
+
+
+def gathered_copies(pieces, own, swapped, other, sem):
+    me = lax.axis_index("fsdp")
+    count = len(pieces)
+    return [
+        pltpu.make_async_copy(ref, held.at[me ^ d], sem.at[k * count + d])
+        for k, (refs, held) in enumerate(((pieces, own), (swapped, other)))
+        for d, ref in enumerate(refs)
+    ]
+
+
+def load_weight(own, other, which, weight, adjoint):
     c = weight.shape[0]
     base = which * HALF
-    mine = place[0] == 0
+    mine = parity() == 0
     slabs = {}
 
     def slab(s):
@@ -136,18 +154,19 @@
     ]
 
 
-class Columns:
-    def __init__(self, ref, rows, copies, base, lon):
-        self.ref, self.rows, self.copies = ref, rows, copies
-        self.base, self.lon = base, lon
-        self.done = 0
-
-    def fill(self, upto):
-        while self.done < min(upto, self.rows.shape[0]):
-            if self.done % GROUP == 0:
-                self.copies[self.done // GROUP].wait()
-            store_row(self.ref, self.done + self.base, self.rows[self.done][:, : self.lon])
-            self.done += 1
+def start(copies):
+    for copy in copies:
+        copy.start()
+
+
+def wait(copies):
+    for copy in copies:
+        copy.wait()
+
+
+def fill(columns, base, rows, lon, lo, hi):
+    for r in range(lo, min(hi, rows.shape[0])):
+        store_row(columns, r + base, rows[r][:, :lon])
 
 
 def place_terms(out, base, depth, total, shards, scale, flip):
@@ -193,26 +212,33 @@
     lax.fori_loop(0, field.shape[0] // SPAN, work, 0)
 
 
-def stage_body(
-    scale, shards, place, source, upstream, above, below, own, other,
-    hid, inn, top, bottom, terms,
-    src, ups, fcol, ccol, w1, a2, hidden, inner, one, two, sem, edge_sem,
-):
+def stage_body(scale, shards, *refs):
+    source, upstream, above_in, below_in = refs[:4]
+    pieces, swapped = refs[4 : 4 + shards], refs[4 + shards : 4 + 2 * shards]
+    hid, inn, top, bottom, terms = refs[4 + 2 * shards : 9 + 2 * shards]
+    (
+        src, ups, fcol, ccol, w1, a2, hidden, inner, one, two, above, below, own, other,
+        sem, edge_sem, piece_sem,
+    ) = refs[9 + 2 * shards :]
     height, _, lon = source.shape
     wide = fcol.shape[2]
-    loads = [chunked(source, src, sem.at[0]), chunked(upstream, ups, sem.at[1])]
-    for pair in zip(*loads):
-        for copy in pair:
-            copy.start()
-    load_weight(place, own, other, 0, w1, False)
-    load_weight(place, own, other, 1, a2, True)
+    weights = gathered_copies(pieces, own, swapped, other, piece_sem)
+    firsts = [
+        pltpu.make_async_copy(above_in, above, edge_sem.at[4]),
+        pltpu.make_async_copy(below_in, below, edge_sem.at[5]),
+    ]
+    loads = chunked(source, src, sem.at[0]) + chunked(upstream, ups, sem.at[1])
+    start(weights + firsts + loads)
+    wait(weights)
+    load_weight(own, other, 0, w1, False)
+    load_weight(own, other, 1, a2, True)
+    wait(firsts + loads)
     for columns, base in ((fcol, 0), (ccol, 2)):
         for r in range(2):
             store_row(columns, r, above[base + r])
             store_row(columns, height + 2 + r, below[base + r])
-    forward = Columns(fcol, src, loads[0], 2, lon)
-    reverse = Columns(ccol, ups, loads[1], 2, lon)
-    forward.fill(GROUP + 2)
+    fill(fcol, 2, src, lon, 0, GROUP + 2)
+    fill(ccol, 2, ups, lon, 0, GROUP + 2)
     saves = [chunked(hidden, hid, sem.at[2]), chunked(inner, inn, sem.at[3])]
     edges = []
     for k, rows in enumerate((hidden, inner)):
@@ -223,10 +249,10 @@
                 )
             )
     for at in range(0, height, GROUP):
-        reverse.fill(at + GROUP + 2)
         pre = jnp.dot(w1[...], rows_of(fcol, at), preferred_element_type=F32)
-        forward.fill(at + 2 * GROUP + 2)
+        fill(fcol, 2, src, lon, at + GROUP + 2, at + 2 * GROUP + 2)
         back = jnp.dot(a2[...], rows_of(ccol, at), preferred_element_type=F32)
+        fill(ccol, 2, ups, lon, at + GROUP + 2, at + 2 * GROUP + 2)
         cdf = 0.5 * (1.0 + lax.erf(pre * 0.7071067811865476))
         value = (pre * cdf).astype(BF16)
         rate = cdf + pre * jnp.exp(-0.5 * pre * pre) * 0.3989422804014327
@@ -234,65 +260,78 @@
         for s in range(GROUP):
             hidden[at + s] = value[:, s * wide : (s + 1) * wide]
             inner[at + s] = grad[:, s * wide : (s + 1) * wide]
-        for save in saves:
-            save[at // GROUP].start()
-    for copy in edges:
-        copy.start()
+    start(saves[0] + saves[1] + edges)
     sum_terms(one, fcol, inner)
     sum_terms(two, ccol, hidden)
     depth = terms.shape[2] // 2
     place_terms(terms, 0, depth, one, shards, scale, True)
     place_terms(terms, depth, depth, two, shards, scale, False)
-    for copy in saves[0] + saves[1] + edges:
-        copy.wait()
-
-
-def interior_body(
-    place, source, upstream, hid, inn, own, other,
-    out, grad, w2, a1,
-    src, ups, mid, cot, hcol, icol, left, right, sem,
-):
+    wait(saves[0] + saves[1] + edges)
+
+
+def interior_body(shards, *refs):
+    source, upstream, hid, inn = refs[:4]
+    pieces, swapped = refs[4 : 4 + shards], refs[4 + shards : 4 + 2 * shards]
+    out, grad, w2_out, a1_out, token = refs[4 + 2 * shards : 9 + 2 * shards]
+    token[...] = jnp.zeros_like(token)
+    (
+        src, ups, mid, cot, hcol, icol, left, right, w2, a1, own, other,
+        sem, weight_sem, piece_sem,
+    ) = refs[9 + 2 * shards :]
     height, _, lon = source.shape
     wide = hcol.shape[2]
-    work = []
-    for k, args in enumerate(
-        ((hid, mid, hcol, source, src, w2, left, out), (inn, cot, icol, upstream, ups, a1, right, grad))
-    ):
-        middle, held, columns, residual, base, weight, result, target = args
-        loads = [chunked(middle, held, sem.at[3 * k]), chunked(residual, base, sem.at[3 * k + 1])]
-        for pair in zip(*loads):
-            for copy in pair:
-                copy.start()
-        rows = Columns(columns, held, loads[0], 0, lon)
-        work.append((rows, loads[1], columns, base, weight, result, target, sem.at[3 * k + 2]))
-    load_weight(place, own, other, 1, w2, False)
-    load_weight(place, own, other, 0, a1, True)
-    saves = []
-    for rows, waits, columns, base, weight, result, target, done in work:
-        rows.fill(GROUP + 4)
-        waits[0].wait()
+    firsts = gathered_copies(pieces, own, swapped, other, piece_sem)
+    work = (
+        (hid, mid, hcol, source, src, w2, left, out),
+        (inn, cot, icol, upstream, ups, a1, right, grad),
+    )
+    loads = [
+        chunked(item[0], item[1], sem.at[3 * k]) + chunked(item[3], item[4], sem.at[3 * k + 1])
+        for k, item in enumerate(work)
+    ]
+    start(loads[0][:2] + firsts + loads[0][2:] + loads[1])
+    wait(loads[0][:2])
+    fill(hcol, 0, mid, lon, 0, 2 * GROUP)
+    wait(firsts)
+    load_weight(own, other, 1, w2, False)
+    load_weight(own, other, 0, a1, True)
+    wait(loads[0][2:])
+    saves = [
+        pltpu.make_async_copy(a, b, weight_sem.at[k])
+        for k, (a, b) in enumerate(((w2, w2_out), (a1, a1_out)))
+    ]
+    start(saves)
+    inside = pl.ds(2, height - 4)
+    for k, (_, held, columns, _, base, weight, result, target) in enumerate(work):
         for at in range(0, height - 4, GROUP):
-            waits[at // GROUP + 1].wait()
-            rows.fill(at + 2 * GROUP + 4)
             value = jnp.dot(weight[...], rows_of(columns, at), preferred_element_type=F32)
+            fill(columns, 0, held, lon, at + 2 * GROUP, at + 3 * GROUP)
             for s in range(GROUP):
                 part = value[:, s * wide : s * wide + lon]
                 row = at + 2 + s
                 result[row] = (base[row].astype(F32) + part).astype(BF16)
-            span = pl.ds(at + 2, GROUP)
-            save = pltpu.make_async_copy(result.at[span], target.at[span], done.at[at // GROUP])
-            save.start()
-            saves.append(save)
-    for save in saves:
-        save.wait()
+        saves.append(
+            pltpu.make_async_copy(result.at[inside], target.at[inside], sem.at[3 * k + 2, 0])
+        )
+        if k == 0:
+            wait(loads[1])
+            fill(icol, 0, cot, lon, 0, 2 * GROUP)
+        saves[-1].start()
+    wait(saves)
 
 
 def edge_body(
-    source, upstream, hid, inn, above, below, w2, a1, out_in, grad_in,
+    source, upstream, hid, inn, above_in, below_in, w2_in, a1_in, out_in, grad_in,
     out, grad,
-    res, mid, columns, result, sem,
+    res, mid, columns, result, above, below, w2, a1, sem,
 ):
     del out_in, grad_in
+    firsts = [
+        pltpu.make_async_copy(a, b, sem.at[3, k])
+        for k, (a, b) in enumerate(
+            ((above_in, above), (below_in, below), (w2_in, w2), (a1_in, a1))
+        )
+    ]
     height, _, lon = source.shape
     wide = columns.shape[3]
     ends = (0, height - 4), (0, height - 2)
@@ -314,16 +353,15 @@
                     result.at[2 * k + j], target.at[pl.ds(ends[1][j], 2)], sem.at[2, 2 * k + j]
                 )
             )
-    for copy in loads:
-        copy.start()
+    start(firsts[:2] + loads[0:8:2] + firsts[2:] + loads[1:8:2])
+    wait(firsts[:2] + loads[0:8:2])
     for k in range(2):
         for r in range(2):
             store_row(columns.at[2 * k], r, above[2 * k + r][:, :lon])
             store_row(columns.at[2 * k + 1], 4 + r, below[2 * k + r][:, :lon])
+    wait(firsts[2:] + loads[1:8:2])
     for k, weight in enumerate((w2, a1)):
         for j in range(2):
-            for copy in loads[4 * k + 2 * j : 4 * k + 2 * j + 2]:
-                copy.wait()
             for r in range(4):
                 store_row(columns.at[2 * k + j], r + 2 - 2 * j, mid[2 * k + j, r][:, :lon])
         rhs = jnp.concatenate(
@@ -336,28 +374,31 @@
                 part = value[:, lo : lo + lon]
                 base = res[2 * k + j, r].astype(F32)
                 result[2 * k + j, r] = (base + part).astype(BF16)
-            saves[2 * k + j].start()
-    for copy in saves:
-        copy.wait()
-
-
-def column_body(place, got, mine, *gives):
+    start(saves)
+    wait(saves)
+
+
+def column_body(got, after, mine, *gives):
+    del after
+    me = lax.axis_index("fsdp")
+
     def total(f):
         value = got[0, f].astype(F32)
         for i in range(1, got.shape[0]):
             value += got[i, f].astype(F32)
         return value
 
-    mine[...] = total(place[1])
+    mine[...] = total(me)
     for d, give in enumerate(gives):
-        give[...] = total(place[1] ^ (d + 1)).astype(BF16)
+        give[...] = total(me ^ (d + 1)).astype(BF16)
 
 
 def chunk_body(mine, *refs):
     total = mine[...]
     for piece in refs[:-1]:
         total += piece[...].astype(F32)
-    refs[-1][...] = total
+    for band in range(refs[-1].shape[0]):
+        refs[-1][band] = total
 
 
 def unpack_body(share, depth, chunks, one, two):
@@ -390,7 +431,6 @@
     small = [
         jnp.swapaxes(k.reshape(TAPS, c, share), 1, 2) for k in (kernel_one, kernel_two)
     ]
-    place = jnp.stack([lax.axis_index("lat") % 2, lax.axis_index("fsdp")]).astype(jnp.int32)
     forward = [(i, i + 1) for i in range(bands - 1)]
     backward = [(i + 1, i) for i in range(bands - 1)]
     swap = [(i, i ^ 1) for i in range(bands)]
@@ -405,28 +445,38 @@
     groups = height // GROUP
     depth = -(-SLABS * share // (8 * bands)) * 8
     others = range(1, shards)
-    half, top, bottom = call(
+    slabs = shape(2 * HALF, share, LANES)
+    half, rest = call(
         pack_body,
         "pack",
-        [
-            (shape(2 * HALF, share, LANES), VMEM),
-            (shape(4, c, lon), ANY),
-            (shape(4, c, lon), ANY),
-        ],
-        [SMEM, VMEM, VMEM, ANY, ANY],
-        (place, *small, source, upstream),
+        [(slabs, VMEM), (slabs, VMEM)],
+        [ANY, ANY],
+        small,
+        scratch=[pltpu.VMEM((TAPS, share, c), BF16)] * 2 + [pltpu.SemaphoreType.DMA((2,))],
+        limit=60,
+    )
+    pieces = [partner(half, d) for d in others]
+    top, bottom = call(
+        ends_body,
+        "ends",
+        [(shape(4, c, lon), VMEM), (shape(4, c, lon), VMEM)],
+        [ANY, ANY, ANY],
+        (half, source, upstream),
         scratch=[pltpu.SemaphoreType.DMA((4,))],
-    )
-    pieces = [partner(half, d) for d in others]
+        limit=60,
+    )
     above, below = edges(top, bottom)
-    (own,) = call(
-        stack_body,
-        "stack",
-        [(shape(shards, 2 * HALF, share, LANES), VMEM)],
-        [SMEM] + [VMEM] * shards,
-        (place, half, *pieces),
-    )
-    other = lax.ppermute(own, "lat", swap)
+    pieces = pl.pallas_call(
+        gate_body,
+        name="gate",
+        out_shape=[slabs for _ in others],
+        in_specs=[ANY] * (shards + 1),
+        out_specs=[ANY for _ in others],
+        input_output_aliases={i: i for i in range(shards - 1)},
+        compiler_params=pltpu.CompilerParams(vmem_limit_bytes=60 << 20),
+    )(*pieces, above, below)
+    swapped = [lax.ppermute(piece, "lat", swap) for piece in pieces]
+    kernels = (half, *pieces, rest, *swapped)
 
     middle = shape(height, c, wide)
     edge = shape(4, c, wide)
@@ -435,6 +485,9 @@
     columns = pltpu.VMEM((height + 4, 3 * c, wide), BF16)
     matrix = pltpu.VMEM((c, TAPS * c), BF16)
     total = pltpu.VMEM((TAPS * c, c), F32)
+    halo = pltpu.VMEM((4, c, lon), BF16)
+    gathered = pltpu.VMEM((shards, *slabs.shape), BF16)
+    piece_sems = pltpu.SemaphoreType.DMA((2 * shards,))
     hid, inn, top, bottom, terms = call(
         functools.partial(stage_body, scale, shards),
         "stage",
@@ -445,11 +498,12 @@
             (edge, ANY),
             (shape(bands, shards, 2 * depth, LANES), VMEM),
         ],
-        [SMEM, ANY, ANY, VMEM, VMEM, VMEM, VMEM],
-        (place, source, upstream, above, below, own, other),
+        [ANY] * (4 + 2 * shards),
+        (source, upstream, above, below, *kernels),
         scratch=[plain, plain, columns, columns, matrix, matrix, lined, lined, total, total]
-        + [pltpu.SemaphoreType.DMA((4, groups)), pltpu.SemaphoreType.DMA((4,))],
-        limit=52,
+        + [halo, halo, gathered, gathered]
+        + [pltpu.SemaphoreType.DMA((4, groups)), pltpu.SemaphoreType.DMA((6,)), piece_sems],
+        limit=60,
         flops=4 * conv_flops,
         nbytes=1 << 24,
     )
@@ -457,16 +511,17 @@
     got = lax.all_to_all(terms, "lat", 0, 0, tiled=True)
     columns = pltpu.VMEM((height, 3 * c, wide), BF16)
     outs = (shape(height, c, lon), ANY)
-    weight = (shape(c, TAPS * c), VMEM)
-    out, grad, w2, a1 = call(
-        interior_body,
+    weight = (shape(c, TAPS * c), ANY)
+    out, grad, w2, a1, token = call(
+        functools.partial(interior_body, shards),
         "interior",
-        [outs, outs, weight, weight],
-        [SMEM, ANY, ANY, ANY, ANY, VMEM, VMEM],
-        (place, source, upstream, hid, inn, own, other),
+        [outs, outs, weight, weight, (shape(8, LANES, dtype=F32), VMEM)],
+        [ANY] * (4 + 2 * shards),
+        (source, upstream, hid, inn, *kernels),
         scratch=[plain, plain, lined, lined, columns, columns, plain, plain]
-        + [pltpu.SemaphoreType.DMA((6, groups))],
-        limit=50,
+        + [matrix, matrix, gathered, gathered]
+        + [pltpu.SemaphoreType.DMA((6, groups)), pltpu.SemaphoreType.DMA((2,)), piece_sems],
+        limit=60,
         flops=2 * conv_flops,
         nbytes=1 << 24,
     )
@@ -475,15 +530,23 @@
         "column",
         [(shape(2 * depth, LANES, dtype=F32), VMEM)]
         + [(shape(2 * depth, LANES), VMEM) for _ in others],
-        [SMEM, VMEM],
-        (place, got),
+        [VMEM, ANY],
+        (got, token),
     )
     gains = [partner(give, d) for d, give in zip(others, gives)]
+    (chunk,) = call(
+        chunk_body,
+        "chunk",
+        [(shape(bands, 2 * depth, LANES, dtype=F32), VMEM)],
+        [VMEM] * shards,
+        (mine, *gains),
+    )
+    chunks = lax.all_to_all(chunk, "lat", 0, 0, tiled=True)
     out, grad = pl.pallas_call(
         edge_body,
         name="edge",
         out_shape=[outs[0], outs[0]],
-        in_specs=[ANY] * 4 + [VMEM] * 4 + [ANY] * 2,
+        in_specs=[ANY] * 10,
         out_specs=[ANY, ANY],
         input_output_aliases={8: 0, 9: 1},
         scratch_shapes=[
@@ -491,21 +554,17 @@
             pltpu.VMEM((4, 4, c, wide), BF16),
             pltpu.VMEM((4, 6, 3 * c, wide), BF16),
             pltpu.VMEM((4, 2, c, lon), BF16),
-            pltpu.SemaphoreType.DMA((3, 4)),
+            pltpu.VMEM(edge.shape, BF16),
+            pltpu.VMEM(edge.shape, BF16),
+            matrix,
+            matrix,
+            pltpu.SemaphoreType.DMA((4, 4)),
         ],
-        compiler_params=pltpu.CompilerParams(vmem_limit_bytes=32 << 20),
+        compiler_params=pltpu.CompilerParams(vmem_limit_bytes=60 << 20),
         cost_estimate=pl.CostEstimate(
             flops=conv_flops // 2, bytes_accessed=1 << 22, transcendentals=0
         ),
     )(source, upstream, hid, inn, above, below, w2, a1, out, grad)
-    (chunk,) = call(
-        chunk_body,
-        "chunk",
-        [(shape(2 * depth, LANES, dtype=F32), VMEM)],
-        [VMEM] * shards,
-        (mine, *gains),
-    )
-    chunks = lax.all_gather(chunk, "lat", axis=0)
     one, two = call(
         functools.partial(unpack_body, share, depth),
         "unpack",

time: 137 us -> 114 us (0.83)
  blocking collectives: 13.9 us -> 0 us
  local copies, waits for them, and re-layouts: 16.1 us -> 4.12 us
  waiting for transfers between devices: 17.2 us -> 25.9 us
  starting transfers between devices: 33.6 us -> 27.7 us
    all_gather x1 -> x0, blocking collectives: 13.9 us -> none  [per_device(): chunks = lax.all_gather(chunk, 'lat', axis=0)]
    unnamed x30 -> x26, local copies, waits for them, and re-layouts: 16.1 us -> 4.12 us
    all_to_all x1, starting transfers between devices: 13.8 us -> 4.78 us  [per_device(): got = lax.all_to_all(terms, 'lat', 0, 0, tiled=True)]
    all_to_all x0 -> x1, starting transfers between devices: none -> 4.88 us  [per_device(): chunks = lax.all_to_all(chunk, 'lat', 0, 0, tiled=True)]
    ppermute x6, waiting for transfers between devices: 14 us -> 18.9 us  [partner(): return lax.ppermute(value, 'fsdp', [(i, i ^ d) for i in range(shards)])]
    all_to_all x0 -> x1, waiting for transfers between devices: none -> 4.3 us  [per_device(): chunks = lax.all_to_all(chunk, 'lat', 0, 0, tiled=True)]
    ppermute x2, waiting for transfers between devices: 2.92 us -> 0.01 us  [edges(): lax.ppermute(top, 'lat', backward)]
    ppermute x2, starting transfers between devices: 7.01 us -> 4.83 us  [edges(): lax.ppermute(bottom, 'lat', forward)]
  transfers between devices with their start and end apart: 12 -> 15, of which waited for: 4 -> 9; matrix products, arithmetic and copies ran while one was open for 0% -> 0% of each run, Pallas kernels for 16% -> 19%
where the time goes in v4:
time: 114 us
  Pallas kernels  55.2 us (48%)
  starting transfers between devices  27.7 us (24%)
  waiting for transfers between devices  25.9 us (23%)
  local copies, waits for them, and re-layouts  4.12 us (4%)
    pallas_call x7, Pallas kernels, call(): pl.pallas_call(body, name=name, out_shape=[o for o, _ in outs], in_specs=...  48.7 us
    ppermute x6, waiting for transfers between devices, partner(): return lax.ppermute(value, 'fsdp', [(i, i ^ d) for i in range(shards)])  18.9 us
    ppermute x6, starting transfers between devices, partner(): return lax.ppermute(value, 'fsdp', [(i, i ^ d) for i in range(shards)])  9.58 us
    pallas_call x1, Pallas kernels, per_device(): pl.pallas_call(edge_body, name='edge', out_shape=[outs[0], outs[0]], in_s...  6.53 us
    all_to_all x1, starting transfers between devices, per_device(): chunks = lax.all_to_all(chunk, 'lat', 0, 0, tiled=True)  4.88 us
    ppermute x2, starting transfers between devices, edges(): lax.ppermute(bottom, 'lat', forward)  4.83 us
    all_to_all x1, starting transfers between devices, per_device(): got = lax.all_to_all(terms, 'lat', 0, 0, tiled=True)  4.78 us
    all_to_all x1, waiting for transfers between devices, per_device(): chunks = lax.all_to_all(chunk, 'lat', 0, 0, tiled=True)  4.3 us
  transfers between devices with their start and end apart: 15, of which 9 were waited for; matrix products, arithmetic and copies ran while one was open for 0% of the time, Pallas kernels for 19%

profile of v4, /device:TPU:0, one launch (start us, length us, event | category | flops | bytes accessed | tf_op | source)
XLA Modules:
  0.0 113.8 jit_solution(4377114851921776525)
XLA Ops:
  0.6 1.9 %pack.1 = (bf16[14,48,128]{2,1,0:T(8,128)(2,1)}, bf16[14,48,128]{2,1,0:T(8,128)(2,1)}) custom-call(bf16[9,48,192]{2,1,0:T(8,128)(2,1)} %bitcast.34, bf16[9,48,192]{2,1,0:T(8,128)(2,1)} %bitcast.35), custom_call_target="tpu_custom_call" | custom-call | tf_op jit(solution)/shard_map/pack/pallas_call | solution.py:27
  2.5 0.0 copy-start.5
  2.5 2.3 %ends.1 = (bf16[4,192,360]{2,1,0:T(8,128)(2,1)}, bf16[4,192,360]{2,1,0:T(8,128)(2,1)}) custom-call(bf16[14,48,128]{2,1,0:T(8,128)(2,1)} %get-tuple-element.29.after.refs_4_, bf16[16,192,360]{2,1,0:T(8,128)(2,1)} %bitcast.24, bf16[16,192,360]{2,1,0:T(8,128)(2,1)} %bitcast.28), custom_call_target="tpu_custom_call" | custom-call | tf_op jit(solution)/shard_map/ends/pallas_call | solution.py:27
  4.9 2.4 %collective-permute-start = (bf16[4,192,360]{2,1,0:T(8,128)(2,1)}, bf16[4,192,360]{2,1,0:T(8,128)(2,1)S(1)}, u32[]{:S(2)}, u32[]{:S(2)}) collective-permute-start(bf16[4,192,360]{2,1,0:T(8,128)(2,1)} %get-tuple-element.30), channel_id=1, source_target_pairs={{0,1},{1,2},{2,3},{3,4},{4,5},{5,6},{6,7},{8,9},{9,10},{10,11},{11... | collective-permute-start | bytes 1658888 | tf_op jit(solution)/shard_map/ppermute | solution.py:439
  7.3 1.3 %collective-permute-start.1 = (bf16[4,192,360]{2,1,0:T(8,128)(2,1)}, bf16[4,192,360]{2,1,0:T(8,128)(2,1)S(1)}, u32[]{:S(2)}, u32[]{:S(2)}) collective-permute-start(bf16[4,192,360]{2,1,0:T(8,128)(2,1)} %get-tuple-element.31), channel_id=1, source_target_pairs={{1,0},{2,1},{3,2},{4,3},{5,4},{6,5},{7,6},{9,8},{10,9},{11,10},{12... | collective-permute-start | bytes 1658888 | tf_op jit(solution)/shard_map/ppermute | solution.py:439
  8.6 0.0 copy-done.5
  8.6 4.5 %collective-permute-start.4 = (bf16[14,48,128]{2,1,0:T(8,128)(2,1)S(1)}, bf16[14,48,128]{2,1,0:T(8,128)(2,1)S(1)}, u32[]{:S(2)}, u32[]{:S(2)}) collective-permute-start(bf16[14,48,128]{2,1,0:T(8,128)(2,1)S(1)} %copy-done.5), channel_id=1, source_target_pairs={{0,24},{8,16},{16,8},{24,0},{1,25},{9,17},{17,9},{25,1},{2,26},{10... | collective-permute-start | bytes 516104 | tf_op jit(solution)/shard_map/ppermute | solution.py:442
  13.1 0.0 collective-permute-start.3
  13.1 0.6 collective-permute-start.2
  13.7 3.0 %collective-permute-done.4.refs_2_ = bf16[14,48,128]{2,1,0:T(8,128)(2,1)S(1)} collective-permute-done((bf16[14,48,128]{2,1,0:T(8,128)(2,1)S(1)}, bf16[14,48,128]{2,1,0:T(8,128)(2,1)S(1)}, u32[]{:S(2)}, u32[]{:S(2)}) %collective-permute-start.4) | collective-permute-done | bytes 172064 | tf_op jit(solution)/shard_map/ppermute | solution.py:442
  16.7 0.0 copy-start.6
  16.7 11.4 %collective-permute-done.3.refs_1_ = bf16[14,48,128]{2,1,0:T(8,128)(2,1)S(1)} collective-permute-done((bf16[14,48,128]{2,1,0:T(8,128)(2,1)S(1)}, bf16[14,48,128]{2,1,0:T(8,128)(2,1)S(1)}, u32[]{:S(2)}, u32[]{:S(2)}) %collective-permute-start.3) | collective-permute-done | bytes 172064 | tf_op jit(solution)/shard_map/ppermute | solution.py:442
  28.1 0.0 copy-start.7
  28.1 0.0 collective-permute-done.2.refs_0_
  28.1 0.0 copy-start.8
  28.1 0.0 collective-permute-done.refs_3_.refs_2_
  28.1 0.0 copy-start.3
  28.1 0.0 collective-permute-done.1.refs_4_.refs_3_
  28.1 0.0 copy-done.6
  28.1 0.6 copy-done.7
  28.8 0.1 copy-done.8
  28.8 0.2 copy-done.3
  29.0 0.0 copy-start.4
  29.0 0.8 copy-done.4
  29.8 0.5 collective-permute-start.5
  30.4 0.0 collective-permute-start.6
  30.4 0.5 collective-permute-start.7
  30.9 0.7 collective-permute-done.5.refs_9_
  31.6 0.0 copy-start.10
  31.6 0.4 collective-permute-done.6.refs_10_
  32.0 0.0 copy-start.11
  32.0 0.2 collective-permute-done.7.refs_11_
  32.2 0.0 copy-start.12
  32.2 0.1 copy-done.10
  32.3 0.4 copy-done.11
  32.6 0.3 copy-done.12
  32.9 27.9 %stage.1 = (bf16[16,192,384]{2,1,0:T(8,128)(2,1)}, bf16[16,192,384]{2,1,0:T(8,128)(2,1)}, bf16[4,192,384]{2,1,0:T(8,128)(2,1)}, bf16[4,192,384]{2,1,0:T(8,128)(2,1)}, bf16[8,4,176,128]{3,2,1,0:T(8,128)(2,1)}) custom-call(bf16[16,192,360]{2,1,0:T(8,128)(2,1)} %bitcast.25, bf16[16,192,360]{2,1,0:T(8,128)(2,1)} %bitcast.29, bf16[4,192,360]{2,1,0:T(8,128)(2,1)} %copy-done.3, ...), custom_call_target="tpu_custom_call" | custom-call | flops 15288238080 | bytes 16777216 | tf_op jit(solution)/shard_map/stage/pallas_call | solution.py:27
  60.8 0.0 copy-start.9
  60.8 4.8 %all-to-all-start = ((bf16[8,4,176,128]{3,2,1,0:T(8,128)(2,1)}), bf16[8,4,176,128]{3,2,1,0:T(8,128)(2,1)S(1)}, u32[]{:S(2)}, u32[]{:S(2)}) async-start(bf16[8,4,176,128]{3,2,1,0:T(8,128)(2,1)} %get-tuple-element.46), calls=%async_computation | async-start | bytes 2883584 | tf_op jit(solution)/shard_map/all_to_all | solution.py:511
  65.6 2.4 %collective-permute-start.8 = (bf16[4,192,384]{2,1,0:T(8,128)(2,1)}, bf16[4,192,384]{2,1,0:T(8,128)(2,1)S(1)}, u32[]{:S(2)}, u32[]{:S(2)}) collective-permute-start(bf16[4,192,384]{2,1,0:T(8,128)(2,1)} %get-tuple-element.38), channel_id=1, source_target_pairs={{0,1},{1,2},{2,3},{3,4},{4,5},{5,6},{6,7},{8,9},{9,10},{10,11},{11... | collective-permute-start | bytes 1769480 | tf_op jit(solution)/shard_map/ppermute | solution.py:439
  68.0 0.0 copy-done.9
  68.0 1.3 %collective-permute-start.9 = (bf16[4,192,384]{2,1,0:T(8,128)(2,1)S(1)}, bf16[4,192,384]{2,1,0:T(8,128)(2,1)S(1)}, u32[]{:S(2)}, u32[]{:S(2)}) collective-permute-start(bf16[4,192,384]{2,1,0:T(8,128)(2,1)S(1)} %copy-done.9), channel_id=1, source_target_pairs={{1,0},{2,1},{3,2},{4,3},{5,4},{6,5},{7,6},{9,8},{10,9},{11,10},{12... | collective-permute-start | bytes 1769480 | tf_op jit(solution)/shard_map/ppermute | solution.py:439
  69.3 14.5 %interior.1 = (bf16[16,192,360]{2,1,0:T(8,128)(2,1)}, bf16[16,192,360]{2,1,0:T(8,128)(2,1)}, bf16[192,1728]{1,0:T(8,128)(2,1)}, bf16[192,1728]{1,0:T(8,128)(2,1)}, f32[8,128]{1,0:T(8,128)}) custom-call(bf16[16,192,360]{2,1,0:T(8,128)(2,1)} %bitcast.26, bf16[16,192,360]{2,1,0:T(8,128)(2,1)} %bitcast.30, bf16[16,192,384]{2,1,0:T(8,128)(2,1)} %get-tuple-element.36.refs_2_.hid, ...), custom_call_target="tpu_custom_call" | custom-call | flops 7644119040 | bytes 16777216 | tf_op jit(solution)/shard_map/interior/pallas_call | solution.py:27
  83.8 1.4 %all-to-all-done.got = bf16[8,4,176,128]{3,2,1,0:T(8,128)(2,1)S(1)} async-done(((bf16[8,4,176,128]{3,2,1,0:T(8,128)(2,1)}), bf16[8,4,176,128]{3,2,1,0:T(8,128)(2,1)S(1)}, u32[]{:S(2)}, u32[]{:S(2)}) %all-to-all-start) | async-done | bytes 1441824 | tf_op jit(solution)/shard_map/all_to_all | solution.py:511
  85.2 0.0 copy-start
  85.2 0.7 copy-done
  85.9 0.2 column.1
  86.1 0.1 collective-permute-start.10
  86.2 3.0 %collective-permute-start.11 = (bf16[176,128]{1,0:T(8,128)(2,1)S(1)}, bf16[176,128]{1,0:T(8,128)(2,1)S(1)}, u32[]{:S(2)}, u32[]{:S(2)}) collective-permute-start(bf16[176,128]{1,0:T(8,128)(2,1)S(1)} %get-tuple-element.50), channel_id=1, source_target_pairs={{0,16},{8,24},{16,0},{24,8},{1,17},{9,25},{17,1},{25,9},{2,18},{10... | collective-permute-start | bytes 135176 | tf_op jit(solution)/shard_map/ppermute | solution.py:442
  89.2 1.3 %collective-permute-start.12 = (bf16[176,128]{1,0:T(8,128)(2,1)S(1)}, bf16[176,128]{1,0:T(8,128)(2,1)S(1)}, u32[]{:S(2)}, u32[]{:S(2)}) collective-permute-start(bf16[176,128]{1,0:T(8,128)(2,1)S(1)} %get-tuple-element.51), channel_id=1, source_target_pairs={{0,24},{8,16},{16,8},{24,0},{1,25},{9,17},{17,9},{25,1},{2,26},{10... | collective-permute-start | bytes 135176 | tf_op jit(solution)/shard_map/ppermute | solution.py:442
  90.5 0.0 collective-permute-done.10.refs_0_
  90.6 1.1 collective-permute-done.11.refs_1_
  91.6 3.4 %collective-permute-done.12.refs_2_ = bf16[176,128]{1,0:T(8,128)(2,1)S(1)} collective-permute-done((bf16[176,128]{1,0:T(8,128)(2,1)S(1)}, bf16[176,128]{1,0:T(8,128)(2,1)S(1)}, u32[]{:S(2)}, u32[]{:S(2)}) %collective-permute-start.12) | collective-permute-done | bytes 45088 | tf_op jit(solution)/shard_map/ppermute | solution.py:442
  95.1 1.0 chunk.1
  96.0 4.9 %all-to-all-start.1 = ((f32[8,176,128]{2,1,0:T(8,128)}), f32[8,176,128]{2,1,0:T(8,128)S(1)}, u32[]{:S(2)}, u32[]{:S(2)}) async-start(f32[8,176,128]{2,1,0:T(8,128)} %chunk.1), calls=%async_computation.1 | async-start | bytes 1441792 | tf_op jit(solution)/shard_map/all_to_all | solution.py:544
  100.9 0.0 collective-permute-done.8.above_in
  100.9 0.0 copy-start.1
  100.9 0.0 collective-permute-done.9.below_in
  100.9 0.0 copy-start.2
  100.9 0.8 copy-done.1
  101.7 0.2 copy-done.2
  102.0 6.5 %edge.1 = (bf16[16,192,360]{2,1,0:T(8,128)(2,1)}, bf16[16,192,360]{2,1,0:T(8,128)(2,1)}) custom-call(bf16[16,192,360]{2,1,0:T(8,128)(2,1)} %bitcast.27, bf16[16,192,360]{2,1,0:T(8,128)(2,1)} %bitcast.31, bf16[16,192,384]{2,1,0:T(8,128)(2,1)} %get-tuple-element.36.refs_2_.hid, ...), custom_call_target="tpu_custom_call", output_to_operand_aliasing={{0}: (8, {}), {1}: (9, {})} | custom-call | flops 1911029760 | bytes 4194304 | tf_op jit(solution)/shard_map/edge/pallas_call | solution.py:545
  108.5 4.3 %all-to-all-done.1.chunks = f32[8,176,128]{2,1,0:T(8,128)S(1)} async-done(((f32[8,176,128]{2,1,0:T(8,128)}), f32[8,176,128]{2,1,0:T(8,128)S(1)}, u32[]{:S(2)}, u32[]{:S(2)}) %all-to-all-start.1) | async-done | bytes 720928 | tf_op jit(solution)/shard_map/all_to_all | solution.py:544
  112.8 1.0 unpack.1
  (1 shorter events, 0.0 us)
Async XLA Ops:
  2.5 6.0 %copy-start.5 = (bf16[14,48,128]{2,1,0:T(8,128)(2,1)S(1)}, bf16[14,48,128]{2,1,0:T(8,128)(2,1)}, u32[]{:S(2)}) copy-start(bf16[14,48,128]{2,1,0:T(8,128)(2,1)} %get-tuple-element.29.after.refs_4_) | copy-start | bytes 516100
  4.9 23.2 %collective-permute-start = (bf16[4,192,360]{2,1,0:T(8,128)(2,1)}, bf16[4,192,360]{2,1,0:T(8,128)(2,1)S(1)}, u32[]{:S(2)}, u32[]{:S(2)}) collective-permute-start(bf16[4,192,360]{2,1,0:T(8,128)(2,1)} %get-tuple-element.30), channel_id=1, source_target_pairs={{0,1},{1,2},{2,3},{3,4},{4,5},{5,6},{6,7},{8,9},{9,10},{10,11},{11... | collective-permute-start | bytes 1658888 | tf_op jit(solution)/shard_map/ppermute | solution.py:439
  7.3 20.8 %collective-permute-start.1 = (bf16[4,192,360]{2,1,0:T(8,128)(2,1)}, bf16[4,192,360]{2,1,0:T(8,128)(2,1)S(1)}, u32[]{:S(2)}, u32[]{:S(2)}) collective-permute-start(bf16[4,192,360]{2,1,0:T(8,128)(2,1)} %get-tuple-element.31), channel_id=1, source_target_pairs={{1,0},{2,1},{3,2},{4,3},{5,4},{6,5},{7,6},{9,8},{10,9},{11,10},{12... | collective-permute-start | bytes 1658888 | tf_op jit(solution)/shard_map/ppermute | solution.py:439
  8.6 8.1 %collective-permute-start.4 = (bf16[14,48,128]{2,1,0:T(8,128)(2,1)S(1)}, bf16[14,48,128]{2,1,0:T(8,128)(2,1)S(1)}, u32[]{:S(2)}, u32[]{:S(2)}) collective-permute-start(bf16[14,48,128]{2,1,0:T(8,128)(2,1)S(1)} %copy-done.5), channel_id=1, source_target_pairs={{0,24},{8,16},{16,8},{24,0},{1,25},{9,17},{17,9},{25,1},{2,26},{10... | collective-permute-start | bytes 516104 | tf_op jit(solution)/shard_map/ppermute | solution.py:442
  13.1 15.0 %collective-permute-start.3 = (bf16[14,48,128]{2,1,0:T(8,128)(2,1)S(1)}, bf16[14,48,128]{2,1,0:T(8,128)(2,1)S(1)}, u32[]{:S(2)}, u32[]{:S(2)}) collective-permute-start(bf16[14,48,128]{2,1,0:T(8,128)(2,1)S(1)} %copy-done.5), channel_id=1, source_target_pairs={{0,16},{8,24},{16,0},{24,8},{1,17},{9,25},{17,1},{25,9},{2,18},{10... | collective-permute-start | bytes 516104 | tf_op jit(solution)/shard_map/ppermute | solution.py:442
  13.1 15.0 %collective-permute-start.2 = (bf16[14,48,128]{2,1,0:T(8,128)(2,1)S(1)}, bf16[14,48,128]{2,1,0:T(8,128)(2,1)S(1)}, u32[]{:S(2)}, u32[]{:S(2)}) collective-permute-start(bf16[14,48,128]{2,1,0:T(8,128)(2,1)S(1)} %copy-done.5), channel_id=1, source_target_pairs={{0,8},{8,0},{16,24},{24,16},{1,9},{9,1},{17,25},{25,17},{2,10},{10... | collective-permute-start | bytes 516104 | tf_op jit(solution)/shard_map/ppermute | solution.py:442
  16.7 11.4 %copy-start.6 = (bf16[14,48,128]{2,1,0:T(8,128)(2,1)}, bf16[14,48,128]{2,1,0:T(8,128)(2,1)S(1)}, u32[]{:S(2)}) copy-start(bf16[14,48,128]{2,1,0:T(8,128)(2,1)S(1)} %collective-permute-done.4.refs_2_) | copy-start | bytes 516100
  28.1 0.7 copy-start.7
  28.1 0.8 copy-start.8
  28.1 0.9 copy-start.3
  29.0 0.8 copy-start.4
  29.8 1.8 %collective-permute-start.5 = (bf16[14,48,128]{2,1,0:T(8,128)(2,1)}, bf16[14,48,128]{2,1,0:T(8,128)(2,1)S(1)}, u32[]{:S(2)}, u32[]{:S(2)}) collective-permute-start(bf16[14,48,128]{2,1,0:T(8,128)(2,1)} %get-tuple-element.32.refs_5_), channel_id=1, source_target_pairs={{0,1},{1,0},{2,3},{3,2},{4,5},{5,4},{6,7},{7,6},{8,9},{9,8},{10,11... | collective-permute-start | bytes 516104 | tf_op jit(solution)/shard_map/ppermute | solution.py:478
  30.4 1.6 %collective-permute-start.6 = (bf16[14,48,128]{2,1,0:T(8,128)(2,1)}, bf16[14,48,128]{2,1,0:T(8,128)(2,1)S(1)}, u32[]{:S(2)}, u32[]{:S(2)}) collective-permute-start(bf16[14,48,128]{2,1,0:T(8,128)(2,1)} %get-tuple-element.33.refs_6_), channel_id=1, source_target_pairs={{0,1},{1,0},{2,3},{3,2},{4,5},{5,4},{6,7},{7,6},{8,9},{9,8},{10,11... | collective-permute-start | bytes 516104 | tf_op jit(solution)/shard_map/ppermute | solution.py:478
  30.4 1.9 %collective-permute-start.7 = (bf16[14,48,128]{2,1,0:T(8,128)(2,1)}, bf16[14,48,128]{2,1,0:T(8,128)(2,1)S(1)}, u32[]{:S(2)}, u32[]{:S(2)}) collective-permute-start(bf16[14,48,128]{2,1,0:T(8,128)(2,1)} %get-tuple-element.34.refs_7_), channel_id=1, source_target_pairs={{0,1},{1,0},{2,3},{3,2},{4,5},{5,4},{6,7},{7,6},{8,9},{9,8},{10,11... | collective-permute-start | bytes 516104 | tf_op jit(solution)/shard_map/ppermute | solution.py:478
  31.6 0.7 copy-start.10
  32.0 0.7 copy-start.11
  32.2 0.7 copy-start.12
  60.8 7.2 %copy-start.9 = (bf16[4,192,384]{2,1,0:T(8,128)(2,1)S(1)}, bf16[4,192,384]{2,1,0:T(8,128)(2,1)}, u32[]{:S(2)}) copy-start(bf16[4,192,384]{2,1,0:T(8,128)(2,1)} %get-tuple-element.39) | copy-start | bytes 1769476
  60.8 24.4 %all-to-all-start = ((bf16[8,4,176,128]{3,2,1,0:T(8,128)(2,1)}), bf16[8,4,176,128]{3,2,1,0:T(8,128)(2,1)S(1)}, u32[]{:S(2)}, u32[]{:S(2)}) async-start(bf16[8,4,176,128]{3,2,1,0:T(8,128)(2,1)} %get-tuple-element.46), calls=%async_computation | async-start | bytes 2883584 | tf_op jit(solution)/shard_map/all_to_all | solution.py:511
  65.6 35.3 %collective-permute-start.8 = (bf16[4,192,384]{2,1,0:T(8,128)(2,1)}, bf16[4,192,384]{2,1,0:T(8,128)(2,1)S(1)}, u32[]{:S(2)}, u32[]{:S(2)}) collective-permute-start(bf16[4,192,384]{2,1,0:T(8,128)(2,1)} %get-tuple-element.38), channel_id=1, source_target_pairs={{0,1},{1,2},{2,3},{3,4},{4,5},{5,6},{6,7},{8,9},{9,10},{10,11},{11... | collective-permute-start | bytes 1769480 | tf_op jit(solution)/shard_map/ppermute | solution.py:439
  68.0 32.9 %collective-permute-start.9 = (bf16[4,192,384]{2,1,0:T(8,128)(2,1)S(1)}, bf16[4,192,384]{2,1,0:T(8,128)(2,1)S(1)}, u32[]{:S(2)}, u32[]{:S(2)}) collective-permute-start(bf16[4,192,384]{2,1,0:T(8,128)(2,1)S(1)} %copy-done.9), channel_id=1, source_target_pairs={{1,0},{2,1},{3,2},{4,3},{5,4},{6,5},{7,6},{9,8},{10,9},{11,10},{12... | collective-permute-start | bytes 1769480 | tf_op jit(solution)/shard_map/ppermute | solution.py:439
  85.2 0.7 copy-start
  86.1 4.5 %collective-permute-start.10 = (bf16[176,128]{1,0:T(8,128)(2,1)S(1)}, bf16[176,128]{1,0:T(8,128)(2,1)S(1)}, u32[]{:S(2)}, u32[]{:S(2)}) collective-permute-start(bf16[176,128]{1,0:T(8,128)(2,1)S(1)} %get-tuple-element.49), channel_id=1, source_target_pairs={{0,8},{8,0},{16,24},{24,16},{1,9},{9,1},{17,25},{25,17},{2,10},{10... | collective-permute-start | bytes 135176 | tf_op jit(solution)/shard_map/ppermute | solution.py:442
  86.2 5.5 %collective-permute-start.11 = (bf16[176,128]{1,0:T(8,128)(2,1)S(1)}, bf16[176,128]{1,0:T(8,128)(2,1)S(1)}, u32[]{:S(2)}, u32[]{:S(2)}) collective-permute-start(bf16[176,128]{1,0:T(8,128)(2,1)S(1)} %get-tuple-element.50), channel_id=1, source_target_pairs={{0,16},{8,24},{16,0},{24,8},{1,17},{9,25},{17,1},{25,9},{2,18},{10... | collective-permute-start | bytes 135176 | tf_op jit(solution)/shard_map/ppermute | solution.py:442
  89.2 5.8 %collective-permute-start.12 = (bf16[176,128]{1,0:T(8,128)(2,1)S(1)}, bf16[176,128]{1,0:T(8,128)(2,1)S(1)}, u32[]{:S(2)}, u32[]{:S(2)}) collective-permute-start(bf16[176,128]{1,0:T(8,128)(2,1)S(1)} %get-tuple-element.51), channel_id=1, source_target_pairs={{0,24},{8,16},{16,8},{24,0},{1,25},{9,17},{17,9},{25,1},{2,26},{10... | collective-permute-start | bytes 135176 | tf_op jit(solution)/shard_map/ppermute | solution.py:442
  96.0 16.8 %all-to-all-start.1 = ((f32[8,176,128]{2,1,0:T(8,128)}), f32[8,176,128]{2,1,0:T(8,128)S(1)}, u32[]{:S(2)}, u32[]{:S(2)}) async-start(f32[8,176,128]{2,1,0:T(8,128)} %chunk.1), calls=%async_computation.1 | async-start | bytes 1441792 | tf_op jit(solution)/shard_map/all_to_all | solution.py:544
  100.9 0.8 copy-start.1
  100.9 1.0 copy-start.2

commit v5 on v4

--- a/solution.py
+++ b/solution.py
@@ -17,6 +17,7 @@
 LANES = 128
 GROUP = 4
 SPAN = 8
+SWEEP = 8
 
 
 def shape(*dims, dtype=BF16):
@@ -237,8 +238,8 @@
         for r in range(2):
             store_row(columns, r, above[base + r])
             store_row(columns, height + 2 + r, below[base + r])
-    fill(fcol, 2, src, lon, 0, GROUP + 2)
-    fill(ccol, 2, ups, lon, 0, GROUP + 2)
+    fill(fcol, 2, src, lon, 0, SWEEP + 2)
+    fill(ccol, 2, ups, lon, 0, SWEEP + 2)
     saves = [chunked(hidden, hid, sem.at[2]), chunked(inner, inn, sem.at[3])]
     edges = []
     for k, rows in enumerate((hidden, inner)):
@@ -248,16 +249,16 @@
                     rows.at[pl.ds(at, 2)], ref.at[pl.ds(2 * k, 2)], edge_sem.at[2 * k + j]
                 )
             )
-    for at in range(0, height, GROUP):
-        pre = jnp.dot(w1[...], rows_of(fcol, at), preferred_element_type=F32)
-        fill(fcol, 2, src, lon, at + GROUP + 2, at + 2 * GROUP + 2)
-        back = jnp.dot(a2[...], rows_of(ccol, at), preferred_element_type=F32)
-        fill(ccol, 2, ups, lon, at + GROUP + 2, at + 2 * GROUP + 2)
+    for at in range(0, height, SWEEP):
+        pre = jnp.dot(w1[...], rows_of(fcol, at, SWEEP), preferred_element_type=F32)
+        fill(fcol, 2, src, lon, at + SWEEP + 2, at + 2 * SWEEP + 2)
+        back = jnp.dot(a2[...], rows_of(ccol, at, SWEEP), preferred_element_type=F32)
+        fill(ccol, 2, ups, lon, at + SWEEP + 2, at + 2 * SWEEP + 2)
         cdf = 0.5 * (1.0 + lax.erf(pre * 0.7071067811865476))
         value = (pre * cdf).astype(BF16)
         rate = cdf + pre * jnp.exp(-0.5 * pre * pre) * 0.3989422804014327
         grad = (back * rate).astype(BF16)
-        for s in range(GROUP):
+        for s in range(SWEEP):
             hidden[at + s] = value[:, s * wide : (s + 1) * wide]
             inner[at + s] = grad[:, s * wide : (s + 1) * wide]
     start(saves[0] + saves[1] + edges)
@@ -470,10 +471,10 @@
         gate_body,
         name="gate",
         out_shape=[slabs for _ in others],
-        in_specs=[ANY] * (shards + 1),
-        out_specs=[ANY for _ in others],
+        in_specs=[VMEM] * (shards + 1),
+        out_specs=[VMEM for _ in others],
         input_output_aliases={i: i for i in range(shards - 1)},
-        compiler_params=pltpu.CompilerParams(vmem_limit_bytes=60 << 20),
+        compiler_params=pltpu.CompilerParams(vmem_limit_bytes=16 << 20),
     )(*pieces, above, below)
     swapped = [lax.ppermute(piece, "lat", swap) for piece in pieces]
     kernels = (half, *pieces, rest, *swapped)
@@ -530,7 +531,7 @@
         "column",
         [(shape(2 * depth, LANES, dtype=F32), VMEM)]
         + [(shape(2 * depth, LANES), VMEM) for _ in others],
-        [VMEM, ANY],
+        [VMEM, VMEM],
         (got, token),
     )
     gains = [partner(give, d) for d, give in zip(others, gives)]

time: 114 us -> 112 us (0.982)
  local copies, waits for them, and re-layouts: 4.12 us -> 2.37 us
    unnamed x26, local copies, waits for them, and re-layouts: 4.12 us -> 2.37 us
  transfers between devices with their start and end apart: 15 -> 15, of which waited for: 9 -> 9; matrix products, arithmetic and copies ran while one was open for 0% -> 0% of each run, Pallas kernels for 19% -> 20%
where the time goes in v5:
time: 112 us
  Pallas kernels  55.3 us (49%)
  starting transfers between devices  27.8 us (25%)
  waiting for transfers between devices  25.7 us (23%)
  local copies, waits for them, and re-layouts  2.37 us (2%)
    pallas_call x7, Pallas kernels, call(): pl.pallas_call(body, name=name, out_shape=[o for o, _ in outs], in_specs=...  48.7 us
    ppermute x6, waiting for transfers between devices, partner(): return lax.ppermute(value, 'fsdp', [(i, i ^ d) for i in range(shards)])  18.9 us
    ppermute x6, starting transfers between devices, partner(): return lax.ppermute(value, 'fsdp', [(i, i ^ d) for i in range(shards)])  9.58 us
    pallas_call x1, Pallas kernels, per_device(): pl.pallas_call(edge_body, name='edge', out_shape=[outs[0], outs[0]], in_s...  6.53 us
    all_to_all x1, starting transfers between devices, per_device(): chunks = lax.all_to_all(chunk, 'lat', 0, 0, tiled=True)  4.88 us
    ppermute x2, starting transfers between devices, edges(): lax.ppermute(bottom, 'lat', forward)  4.83 us
    all_to_all x1, starting transfers between devices, per_device(): got = lax.all_to_all(terms, 'lat', 0, 0, tiled=True)  4.78 us
    all_to_all x1, waiting for transfers between devices, per_device(): chunks = lax.all_to_all(chunk, 'lat', 0, 0, tiled=True)  4.3 us
  transfers between devices with their start and end apart: 15, of which 9 were waited for; matrix products, arithmetic and copies ran while one was open for 0% of the time, Pallas kernels for 20%

profile of v5, /device:TPU:0, one launch (start us, length us, event | category | flops | bytes accessed | tf_op | source)
XLA Modules:
  0.0 112.0 jit_solution(6089534359093090516)
XLA Ops:
  0.6 1.9 %pack.1 = (bf16[14,48,128]{2,1,0:T(8,128)(2,1)}, bf16[14,48,128]{2,1,0:T(8,128)(2,1)}) custom-call(bf16[9,48,192]{2,1,0:T(8,128)(2,1)} %bitcast.34, bf16[9,48,192]{2,1,0:T(8,128)(2,1)} %bitcast.35), custom_call_target="tpu_custom_call" | custom-call | tf_op jit(solution)/shard_map/pack/pallas_call | solution.py:28
  2.5 0.0 copy-start.8
  2.5 2.3 %ends.1 = (bf16[4,192,360]{2,1,0:T(8,128)(2,1)}, bf16[4,192,360]{2,1,0:T(8,128)(2,1)}) custom-call(bf16[14,48,128]{2,1,0:T(8,128)(2,1)} %get-tuple-element.29.after.refs_4_, bf16[16,192,360]{2,1,0:T(8,128)(2,1)} %bitcast.24, bf16[16,192,360]{2,1,0:T(8,128)(2,1)} %bitcast.28), custom_call_target="tpu_custom_call" | custom-call | tf_op jit(solution)/shard_map/ends/pallas_call | solution.py:28
  4.9 2.4 %collective-permute-start = (bf16[4,192,360]{2,1,0:T(8,128)(2,1)}, bf16[4,192,360]{2,1,0:T(8,128)(2,1)S(1)}, u32[]{:S(2)}, u32[]{:S(2)}) collective-permute-start(bf16[4,192,360]{2,1,0:T(8,128)(2,1)} %get-tuple-element.30), channel_id=1, source_target_pairs={{0,1},{1,2},{2,3},{3,4},{4,5},{5,6},{6,7},{8,9},{9,10},{10,11},{11... | collective-permute-start | bytes 1658888 | tf_op jit(solution)/shard_map/ppermute | solution.py:440
  7.3 1.3 %collective-permute-start.1 = (bf16[4,192,360]{2,1,0:T(8,128)(2,1)}, bf16[4,192,360]{2,1,0:T(8,128)(2,1)S(1)}, u32[]{:S(2)}, u32[]{:S(2)}) collective-permute-start(bf16[4,192,360]{2,1,0:T(8,128)(2,1)} %get-tuple-element.31), channel_id=1, source_target_pairs={{1,0},{2,1},{3,2},{4,3},{5,4},{6,5},{7,6},{9,8},{10,9},{11,10},{12... | collective-permute-start | bytes 1658888 | tf_op jit(solution)/shard_map/ppermute | solution.py:440
  8.6 0.0 copy-done.8
  8.6 4.5 %collective-permute-start.4 = (bf16[14,48,128]{2,1,0:T(8,128)(2,1)S(1)}, bf16[14,48,128]{2,1,0:T(8,128)(2,1)S(1)}, u32[]{:S(2)}, u32[]{:S(2)}) collective-permute-start(bf16[14,48,128]{2,1,0:T(8,128)(2,1)S(1)} %copy-done.8), channel_id=1, source_target_pairs={{0,24},{8,16},{16,8},{24,0},{1,25},{9,17},{17,9},{25,1},{2,26},{10... | collective-permute-start | bytes 516104 | tf_op jit(solution)/shard_map/ppermute | solution.py:443
  13.1 0.0 collective-permute-start.3
  13.1 0.6 collective-permute-start.2
  13.7 3.0 %collective-permute-done.4.refs_2_ = bf16[14,48,128]{2,1,0:T(8,128)(2,1)S(1)} collective-permute-done((bf16[14,48,128]{2,1,0:T(8,128)(2,1)S(1)}, bf16[14,48,128]{2,1,0:T(8,128)(2,1)S(1)}, u32[]{:S(2)}, u32[]{:S(2)}) %collective-permute-start.4) | collective-permute-done | bytes 172064 | tf_op jit(solution)/shard_map/ppermute | solution.py:443
  16.7 11.4 %collective-permute-done.3.refs_1_ = bf16[14,48,128]{2,1,0:T(8,128)(2,1)S(1)} collective-permute-done((bf16[14,48,128]{2,1,0:T(8,128)(2,1)S(1)}, bf16[14,48,128]{2,1,0:T(8,128)(2,1)S(1)}, u32[]{:S(2)}, u32[]{:S(2)}) %collective-permute-start.3) | collective-permute-done | bytes 172064 | tf_op jit(solution)/shard_map/ppermute | solution.py:443
  28.1 0.0 collective-permute-done.2.refs_0_
  28.1 0.0 collective-permute-done.refs_3_.refs_2_
  28.1 0.0 copy-start
  28.1 0.0 collective-permute-done.1.refs_4_.refs_3_
  28.1 0.0 copy-start.1
  28.1 0.0 copy-start.2
  28.1 0.0 copy-start.3
  28.1 0.0 copy-start.4
  28.1 0.6 collective-permute-start.5
  28.8 0.1 collective-permute-start.6
  28.8 0.4 collective-permute-start.7
  29.3 0.5 collective-permute-done.5.refs_9_
  29.8 0.0 copy-start.10
  29.8 0.4 collective-permute-done.6.refs_10_
  30.2 0.0 copy-start.11
  30.2 0.2 collective-permute-done.7.refs_11_
  30.4 0.0 copy-start.12
  30.4 0.0 copy-done
  30.4 0.0 copy-done.1
  30.4 0.0 copy-done.2
  30.4 0.0 copy-done.3
  30.4 0.0 copy-done.4
  30.4 0.0 copy-done.10
  30.5 0.4 copy-done.11
  30.8 0.2 copy-done.12
  31.1 27.9 %stage.1 = (bf16[16,192,384]{2,1,0:T(8,128)(2,1)}, bf16[16,192,384]{2,1,0:T(8,128)(2,1)}, bf16[4,192,384]{2,1,0:T(8,128)(2,1)}, bf16[4,192,384]{2,1,0:T(8,128)(2,1)}, bf16[8,4,176,128]{3,2,1,0:T(8,128)(2,1)}) custom-call(bf16[16,192,360]{2,1,0:T(8,128)(2,1)} %bitcast.25, bf16[16,192,360]{2,1,0:T(8,128)(2,1)} %bitcast.29, bf16[4,192,360]{2,1,0:T(8,128)(2,1)} %copy-done, ...), custom_call_target="tpu_custom_call" | custom-call | flops 15288238080 | bytes 16777216 | tf_op jit(solution)/shard_map/stage/pallas_call | solution.py:28
  59.0 0.0 copy-start.9
  59.0 4.8 %all-to-all-start = ((bf16[8,4,176,128]{3,2,1,0:T(8,128)(2,1)}), bf16[8,4,176,128]{3,2,1,0:T(8,128)(2,1)S(1)}, u32[]{:S(2)}, u32[]{:S(2)}) async-start(bf16[8,4,176,128]{3,2,1,0:T(8,128)(2,1)} %get-tuple-element.46), calls=%async_computation | async-start | bytes 2883584 | tf_op jit(solution)/shard_map/all_to_all | solution.py:512
  63.8 2.4 %collective-permute-start.8 = (bf16[4,192,384]{2,1,0:T(8,128)(2,1)}, bf16[4,192,384]{2,1,0:T(8,128)(2,1)S(1)}, u32[]{:S(2)}, u32[]{:S(2)}) collective-permute-start(bf16[4,192,384]{2,1,0:T(8,128)(2,1)} %get-tuple-element.38), channel_id=1, source_target_pairs={{0,1},{1,2},{2,3},{3,4},{4,5},{5,6},{6,7},{8,9},{9,10},{10,11},{11... | collective-permute-start | bytes 1769480 | tf_op jit(solution)/shard_map/ppermute | solution.py:440
  66.2 0.0 copy-done.9
  66.2 1.3 %collective-permute-start.9 = (bf16[4,192,384]{2,1,0:T(8,128)(2,1)S(1)}, bf16[4,192,384]{2,1,0:T(8,128)(2,1)S(1)}, u32[]{:S(2)}, u32[]{:S(2)}) collective-permute-start(bf16[4,192,384]{2,1,0:T(8,128)(2,1)S(1)} %copy-done.9), channel_id=1, source_target_pairs={{1,0},{2,1},{3,2},{4,3},{5,4},{6,5},{7,6},{9,8},{10,9},{11,10},{12... | collective-permute-start | bytes 1769480 | tf_op jit(solution)/shard_map/ppermute | solution.py:440
  67.5 14.5 %interior.1 = (bf16[16,192,360]{2,1,0:T(8,128)(2,1)}, bf16[16,192,360]{2,1,0:T(8,128)(2,1)}, bf16[192,1728]{1,0:T(8,128)(2,1)}, bf16[192,1728]{1,0:T(8,128)(2,1)}, f32[8,128]{1,0:T(8,128)}) custom-call(bf16[16,192,360]{2,1,0:T(8,128)(2,1)} %bitcast.26, bf16[16,192,360]{2,1,0:T(8,128)(2,1)} %bitcast.30, bf16[16,192,384]{2,1,0:T(8,128)(2,1)} %get-tuple-element.36.refs_2_.hid, ...), custom_call_target="tpu_custom_call" | custom-call | flops 7644119040 | bytes 16777216 | tf_op jit(solution)/shard_map/interior/pallas_call | solution.py:28
  82.0 1.4 %all-to-all-done.got = bf16[8,4,176,128]{3,2,1,0:T(8,128)(2,1)S(1)} async-done(((bf16[8,4,176,128]{3,2,1,0:T(8,128)(2,1)}), bf16[8,4,176,128]{3,2,1,0:T(8,128)(2,1)S(1)}, u32[]{:S(2)}, u32[]{:S(2)}) %all-to-all-start) | async-done | bytes 1441824 | tf_op jit(solution)/shard_map/all_to_all | solution.py:512
  83.4 0.0 copy-start.5
  83.4 0.7 copy-done.5
  84.1 0.2 column.1
  84.3 0.1 collective-permute-start.10
  84.4 3.0 %collective-permute-start.11 = (bf16[176,128]{1,0:T(8,128)(2,1)S(1)}, bf16[176,128]{1,0:T(8,128)(2,1)S(1)}, u32[]{:S(2)}, u32[]{:S(2)}) collective-permute-start(bf16[176,128]{1,0:T(8,128)(2,1)S(1)} %get-tuple-element.50), channel_id=1, source_target_pairs={{0,16},{8,24},{16,0},{24,8},{1,17},{9,25},{17,1},{25,9},{2,18},{10... | collective-permute-start | bytes 135176 | tf_op jit(solution)/shard_map/ppermute | solution.py:443
  87.4 1.3 %collective-permute-start.12 = (bf16[176,128]{1,0:T(8,128)(2,1)S(1)}, bf16[176,128]{1,0:T(8,128)(2,1)S(1)}, u32[]{:S(2)}, u32[]{:S(2)}) collective-permute-start(bf16[176,128]{1,0:T(8,128)(2,1)S(1)} %get-tuple-element.51), channel_id=1, source_target_pairs={{0,24},{8,16},{16,8},{24,0},{1,25},{9,17},{17,9},{25,1},{2,26},{10... | collective-permute-start | bytes 135176 | tf_op jit(solution)/shard_map/ppermute | solution.py:443
  88.7 0.0 collective-permute-done.10.refs_0_
  88.8 1.1 collective-permute-done.11.refs_1_
  89.8 3.4 %collective-permute-done.12.refs_2_ = bf16[176,128]{1,0:T(8,128)(2,1)S(1)} collective-permute-done((bf16[176,128]{1,0:T(8,128)(2,1)S(1)}, bf16[176,128]{1,0:T(8,128)(2,1)S(1)}, u32[]{:S(2)}, u32[]{:S(2)}) %collective-permute-start.12) | collective-permute-done | bytes 45088 | tf_op jit(solution)/shard_map/ppermute | solution.py:443
  93.2 1.0 chunk.1
  94.2 4.9 %all-to-all-start.1 = ((f32[8,176,128]{2,1,0:T(8,128)}), f32[8,176,128]{2,1,0:T(8,128)S(1)}, u32[]{:S(2)}, u32[]{:S(2)}) async-start(f32[8,176,128]{2,1,0:T(8,128)} %chunk.1), calls=%async_computation.1 | async-start | bytes 1441792 | tf_op jit(solution)/shard_map/all_to_all | solution.py:545
  99.1 0.0 collective-permute-done.8.above_in
  99.1 0.0 copy-start.6
  99.1 0.0 collective-permute-done.9.below_in
  99.1 0.0 copy-start.7
  99.1 0.8 copy-done.6
  99.9 0.2 copy-done.7
  100.1 6.5 %edge.1 = (bf16[16,192,360]{2,1,0:T(8,128)(2,1)}, bf16[16,192,360]{2,1,0:T(8,128)(2,1)}) custom-call(bf16[16,192,360]{2,1,0:T(8,128)(2,1)} %bitcast.27, bf16[16,192,360]{2,1,0:T(8,128)(2,1)} %bitcast.31, bf16[16,192,384]{2,1,0:T(8,128)(2,1)} %get-tuple-element.36.refs_2_.hid, ...), custom_call_target="tpu_custom_call", output_to_operand_aliasing={{0}: (8, {}), {1}: (9, {})} | custom-call | flops 1911029760 | bytes 4194304 | tf_op jit(solution)/shard_map/edge/pallas_call | solution.py:546
  106.7 4.3 %all-to-all-done.1.chunks = f32[8,176,128]{2,1,0:T(8,128)S(1)} async-done(((f32[8,176,128]{2,1,0:T(8,128)}), f32[8,176,128]{2,1,0:T(8,128)S(1)}, u32[]{:S(2)}, u32[]{:S(2)}) %all-to-all-start.1) | async-done | bytes 720928 | tf_op jit(solution)/shard_map/all_to_all | solution.py:545
  111.0 1.0 unpack.1
  (1 shorter events, 0.0 us)
Async XLA Ops:
  2.5 6.0 %copy-start.8 = (bf16[14,48,128]{2,1,0:T(8,128)(2,1)S(1)}, bf16[14,48,128]{2,1,0:T(8,128)(2,1)}, u32[]{:S(2)}) copy-start(bf16[14,48,128]{2,1,0:T(8,128)(2,1)} %get-tuple-element.29.after.refs_4_) | copy-start | bytes 516100
  4.9 23.2 %collective-permute-start = (bf16[4,192,360]{2,1,0:T(8,128)(2,1)}, bf16[4,192,360]{2,1,0:T(8,128)(2,1)S(1)}, u32[]{:S(2)}, u32[]{:S(2)}) collective-permute-start(bf16[4,192,360]{2,1,0:T(8,128)(2,1)} %get-tuple-element.30), channel_id=1, source_target_pairs={{0,1},{1,2},{2,3},{3,4},{4,5},{5,6},{6,7},{8,9},{9,10},{10,11},{11... | collective-permute-start | bytes 1658888 | tf_op jit(solution)/shard_map/ppermute | solution.py:440
  7.3 20.8 %collective-permute-start.1 = (bf16[4,192,360]{2,1,0:T(8,128)(2,1)}, bf16[4,192,360]{2,1,0:T(8,128)(2,1)S(1)}, u32[]{:S(2)}, u32[]{:S(2)}) collective-permute-start(bf16[4,192,360]{2,1,0:T(8,128)(2,1)} %get-tuple-element.31), channel_id=1, source_target_pairs={{1,0},{2,1},{3,2},{4,3},{5,4},{6,5},{7,6},{9,8},{10,9},{11,10},{12... | collective-permute-start | bytes 1658888 | tf_op jit(solution)/shard_map/ppermute | solution.py:440
  8.6 8.1 %collective-permute-start.4 = (bf16[14,48,128]{2,1,0:T(8,128)(2,1)S(1)}, bf16[14,48,128]{2,1,0:T(8,128)(2,1)S(1)}, u32[]{:S(2)}, u32[]{:S(2)}) collective-permute-start(bf16[14,48,128]{2,1,0:T(8,128)(2,1)S(1)} %copy-done.8), channel_id=1, source_target_pairs={{0,24},{8,16},{16,8},{24,0},{1,25},{9,17},{17,9},{25,1},{2,26},{10... | collective-permute-start | bytes 516104 | tf_op jit(solution)/shard_map/ppermute | solution.py:443
  13.1 15.0 %collective-permute-start.3 = (bf16[14,48,128]{2,1,0:T(8,128)(2,1)S(1)}, bf16[14,48,128]{2,1,0:T(8,128)(2,1)S(1)}, u32[]{:S(2)}, u32[]{:S(2)}) collective-permute-start(bf16[14,48,128]{2,1,0:T(8,128)(2,1)S(1)} %copy-done.8), channel_id=1, source_target_pairs={{0,16},{8,24},{16,0},{24,8},{1,17},{9,25},{17,1},{25,9},{2,18},{10... | collective-permute-start | bytes 516104 | tf_op jit(solution)/shard_map/ppermute | solution.py:443
  13.1 15.0 %collective-permute-start.2 = (bf16[14,48,128]{2,1,0:T(8,128)(2,1)S(1)}, bf16[14,48,128]{2,1,0:T(8,128)(2,1)S(1)}, u32[]{:S(2)}, u32[]{:S(2)}) collective-permute-start(bf16[14,48,128]{2,1,0:T(8,128)(2,1)S(1)} %copy-done.8), channel_id=1, source_target_pairs={{0,8},{8,0},{16,24},{24,16},{1,9},{9,1},{17,25},{25,17},{2,10},{10... | collective-permute-start | bytes 516104 | tf_op jit(solution)/shard_map/ppermute | solution.py:443
  28.1 2.3 %copy-start = (bf16[4,192,360]{2,1,0:T(8,128)(2,1)}, bf16[4,192,360]{2,1,0:T(8,128)(2,1)S(1)}, u32[]{:S(2)}) copy-start(bf16[4,192,360]{2,1,0:T(8,128)(2,1)S(1)} %collective-permute-done.refs_3_.refs_2_) | copy-start | bytes 1658884
  28.1 2.3 %copy-start.1 = (bf16[4,192,360]{2,1,0:T(8,128)(2,1)}, bf16[4,192,360]{2,1,0:T(8,128)(2,1)S(1)}, u32[]{:S(2)}) copy-start(bf16[4,192,360]{2,1,0:T(8,128)(2,1)S(1)} %collective-permute-done.1.refs_4_.refs_3_) | copy-start | bytes 1658884
  28.1 2.3 %copy-start.2 = (bf16[14,48,128]{2,1,0:T(8,128)(2,1)}, bf16[14,48,128]{2,1,0:T(8,128)(2,1)S(1)}, u32[]{:S(2)}) copy-start(bf16[14,48,128]{2,1,0:T(8,128)(2,1)S(1)} %get-tuple-element.34.refs_7_) | copy-start | bytes 516100
  28.1 2.3 %copy-start.3 = (bf16[14,48,128]{2,1,0:T(8,128)(2,1)}, bf16[14,48,128]{2,1,0:T(8,128)(2,1)S(1)}, u32[]{:S(2)}) copy-start(bf16[14,48,128]{2,1,0:T(8,128)(2,1)S(1)} %get-tuple-element.33.refs_6_) | copy-start | bytes 516100
  28.1 2.3 %copy-start.4 = (bf16[14,48,128]{2,1,0:T(8,128)(2,1)}, bf16[14,48,128]{2,1,0:T(8,128)(2,1)S(1)}, u32[]{:S(2)}) copy-start(bf16[14,48,128]{2,1,0:T(8,128)(2,1)S(1)} %get-tuple-element.32.refs_5_) | copy-start | bytes 516100
  28.1 1.6 %collective-permute-start.5 = (bf16[14,48,128]{2,1,0:T(8,128)(2,1)S(1)}, bf16[14,48,128]{2,1,0:T(8,128)(2,1)S(1)}, u32[]{:S(2)}, u32[]{:S(2)}) collective-permute-start(bf16[14,48,128]{2,1,0:T(8,128)(2,1)S(1)} %get-tuple-element.32.refs_5_), channel_id=1, source_target_pairs={{0,1},{1,0},{2,3},{3,2},{4,5},{5,4},{6,7},{7,6},{8,9},{9,8},{10,11... | collective-permute-start | bytes 516104 | tf_op jit(solution)/shard_map/ppermute | solution.py:479
  28.8 1.4 %collective-permute-start.6 = (bf16[14,48,128]{2,1,0:T(8,128)(2,1)S(1)}, bf16[14,48,128]{2,1,0:T(8,128)(2,1)S(1)}, u32[]{:S(2)}, u32[]{:S(2)}) collective-permute-start(bf16[14,48,128]{2,1,0:T(8,128)(2,1)S(1)} %get-tuple-element.33.refs_6_), channel_id=1, source_target_pairs={{0,1},{1,0},{2,3},{3,2},{4,5},{5,4},{6,7},{7,6},{8,9},{9,8},{10,11... | collective-permute-start | bytes 516104 | tf_op jit(solution)/shard_map/ppermute | solution.py:479
  28.8 1.6 %collective-permute-start.7 = (bf16[14,48,128]{2,1,0:T(8,128)(2,1)S(1)}, bf16[14,48,128]{2,1,0:T(8,128)(2,1)S(1)}, u32[]{:S(2)}, u32[]{:S(2)}) collective-permute-start(bf16[14,48,128]{2,1,0:T(8,128)(2,1)S(1)} %get-tuple-element.34.refs_7_), channel_id=1, source_target_pairs={{0,1},{1,0},{2,3},{3,2},{4,5},{5,4},{6,7},{7,6},{8,9},{9,8},{10,11... | collective-permute-start | bytes 516104 | tf_op jit(solution)/shard_map/ppermute | solution.py:479
  29.8 0.7 copy-start.10
  30.2 0.7 copy-start.11
  30.4 0.7 copy-start.12
  59.0 7.2 %copy-start.9 = (bf16[4,192,384]{2,1,0:T(8,128)(2,1)S(1)}, bf16[4,192,384]{2,1,0:T(8,128)(2,1)}, u32[]{:S(2)}) copy-start(bf16[4,192,384]{2,1,0:T(8,128)(2,1)} %get-tuple-element.39) | copy-start | bytes 1769476
  59.0 24.4 %all-to-all-start = ((bf16[8,4,176,128]{3,2,1,0:T(8,128)(2,1)}), bf16[8,4,176,128]{3,2,1,0:T(8,128)(2,1)S(1)}, u32[]{:S(2)}, u32[]{:S(2)}) async-start(bf16[8,4,176,128]{3,2,1,0:T(8,128)(2,1)} %get-tuple-element.46), calls=%async_computation | async-start | bytes 2883584 | tf_op jit(solution)/shard_map/all_to_all | solution.py:512
  63.8 35.3 %collective-permute-start.8 = (bf16[4,192,384]{2,1,0:T(8,128)(2,1)}, bf16[4,192,384]{2,1,0:T(8,128)(2,1)S(1)}, u32[]{:S(2)}, u32[]{:S(2)}) collective-permute-start(bf16[4,192,384]{2,1,0:T(8,128)(2,1)} %get-tuple-element.38), channel_id=1, source_target_pairs={{0,1},{1,2},{2,3},{3,4},{4,5},{5,6},{6,7},{8,9},{9,10},{10,11},{11... | collective-permute-start | bytes 1769480 | tf_op jit(solution)/shard_map/ppermute | solution.py:440
  66.2 32.9 %collective-permute-start.9 = (bf16[4,192,384]{2,1,0:T(8,128)(2,1)S(1)}, bf16[4,192,384]{2,1,0:T(8,128)(2,1)S(1)}, u32[]{:S(2)}, u32[]{:S(2)}) collective-permute-start(bf16[4,192,384]{2,1,0:T(8,128)(2,1)S(1)} %copy-done.9), channel_id=1, source_target_pairs={{1,0},{2,1},{3,2},{4,3},{5,4},{6,5},{7,6},{9,8},{10,9},{11,10},{12... | collective-permute-start | bytes 1769480 | tf_op jit(solution)/shard_map/ppermute | solution.py:440
  83.4 0.7 copy-start.5
  84.3 4.5 %collective-permute-start.10 = (bf16[176,128]{1,0:T(8,128)(2,1)S(1)}, bf16[176,128]{1,0:T(8,128)(2,1)S(1)}, u32[]{:S(2)}, u32[]{:S(2)}) collective-permute-start(bf16[176,128]{1,0:T(8,128)(2,1)S(1)} %get-tuple-element.49), channel_id=1, source_target_pairs={{0,8},{8,0},{16,24},{24,16},{1,9},{9,1},{17,25},{25,17},{2,10},{10... | collective-permute-start | bytes 135176 | tf_op jit(solution)/shard_map/ppermute | solution.py:443
  84.4 5.5 %collective-permute-start.11 = (bf16[176,128]{1,0:T(8,128)(2,1)S(1)}, bf16[176,128]{1,0:T(8,128)(2,1)S(1)}, u32[]{:S(2)}, u32[]{:S(2)}) collective-permute-start(bf16[176,128]{1,0:T(8,128)(2,1)S(1)} %get-tuple-element.50), channel_id=1, source_target_pairs={{0,16},{8,24},{16,0},{24,8},{1,17},{9,25},{17,1},{25,9},{2,18},{10... | collective-permute-start | bytes 135176 | tf_op jit(solution)/shard_map/ppermute | solution.py:443
  87.4 5.8 %collective-permute-start.12 = (bf16[176,128]{1,0:T(8,128)(2,1)S(1)}, bf16[176,128]{1,0:T(8,128)(2,1)S(1)}, u32[]{:S(2)}, u32[]{:S(2)}) collective-permute-start(bf16[176,128]{1,0:T(8,128)(2,1)S(1)} %get-tuple-element.51), channel_id=1, source_target_pairs={{0,24},{8,16},{16,8},{24,0},{1,25},{9,17},{17,9},{25,1},{2,26},{10... | collective-permute-start | bytes 135176 | tf_op jit(solution)/shard_map/ppermute | solution.py:443
  94.2 16.8 %all-to-all-start.1 = ((f32[8,176,128]{2,1,0:T(8,128)}), f32[8,176,128]{2,1,0:T(8,128)S(1)}, u32[]{:S(2)}, u32[]{:S(2)}) async-start(f32[8,176,128]{2,1,0:T(8,128)} %chunk.1), calls=%async_computation.1 | async-start | bytes 1441792 | tf_op jit(solution)/shard_map/all_to_all | solution.py:545
  99.1 0.8 copy-start.6
  99.1 1.0 copy-start.7

commit v6 on v5

--- a/solution.py
+++ b/solution.py
@@ -56,26 +56,12 @@
     return lax.rem(lax.axis_index("lat"), 2)
 
 
-def pack_body(first, second, half, rest, one, two, sem):
+def pack_body(first, second, source, upstream, half, rest, top, bottom, one, two, sem):
+    height = source.shape[0]
     copies = [
-        pltpu.make_async_copy(first, one, sem.at[0]),
-        pltpu.make_async_copy(second, two, sem.at[1]),
-    ]
-    start(copies)
-    wait(copies)
-    mine = parity() == 0
-    for k, kernel in enumerate((one, two)):
-        for i in range(HALF):
-            low = to_slab(lambda tap: kernel[tap], i)
-            high = to_slab(lambda tap: kernel[tap], HALF + i)
-            half[k * HALF + i] = jnp.where(mine, low, high)
-            rest[k * HALF + i] = jnp.where(mine, high, low)
-
-
-def ends_body(after, source, upstream, top, bottom, sem):
-    del after
-    height = source.shape[0]
-    copies = []
+        pltpu.make_async_copy(first, one, sem.at[4]),
+        pltpu.make_async_copy(second, two, sem.at[5]),
+    ]
     for base, rows in ((0, source), (2, upstream)):
         for k, (ref, at) in enumerate(((top, 0), (bottom, height - 2))):
             copies.append(
@@ -84,7 +70,15 @@
                 )
             )
     start(copies)
-    wait(copies)
+    wait(copies[:2])
+    mine = parity() == 0
+    for k, kernel in enumerate((one, two)):
+        for i in range(HALF):
+            low = to_slab(lambda tap: kernel[tap], i)
+            high = to_slab(lambda tap: kernel[tap], HALF + i)
+            half[k * HALF + i] = jnp.where(mine, low, high)
+            rest[k * HALF + i] = jnp.where(mine, high, low)
+    wait(copies[2:])
 
 
 def gate_body(*refs):
@@ -303,11 +297,14 @@
     ]
     start(saves)
     inside = pl.ds(2, height - 4)
+    stride = (height - 4) // 2
     for k, (_, held, columns, _, base, weight, result, target) in enumerate(work):
-        for at in range(0, height - 4, GROUP):
-            value = jnp.dot(weight[...], rows_of(columns, at), preferred_element_type=F32)
-            fill(columns, 0, held, lon, at + 2 * GROUP, at + 3 * GROUP)
-            for s in range(GROUP):
+        for at in range(0, height - 4, stride):
+            if at == 0:
+                fill(columns, 0, held, lon, 2 * GROUP, stride + 4)
+            value = jnp.dot(weight[...], rows_of(columns, at, stride), preferred_element_type=F32)
+            fill(columns, 0, held, lon, at + stride + 4, at + 2 * stride + 4)
+            for s in range(stride):
                 part = value[:, s * wide : s * wide + lon]
                 row = at + 2 + s
                 result[row] = (base[row].astype(F32) + part).astype(BF16)
@@ -447,25 +444,21 @@
     depth = -(-SLABS * share // (8 * bands)) * 8
     others = range(1, shards)
     slabs = shape(2 * HALF, share, LANES)
-    half, rest = call(
+    half, rest, top, bottom = call(
         pack_body,
         "pack",
-        [(slabs, VMEM), (slabs, VMEM)],
-        [ANY, ANY],
-        small,
-        scratch=[pltpu.VMEM((TAPS, share, c), BF16)] * 2 + [pltpu.SemaphoreType.DMA((2,))],
+        [
+            (slabs, VMEM),
+            (slabs, VMEM),
+            (shape(4, c, lon), VMEM),
+            (shape(4, c, lon), VMEM),
+        ],
+        [ANY] * 4,
+        (*small, source, upstream),
+        scratch=[pltpu.VMEM((TAPS, share, c), BF16)] * 2 + [pltpu.SemaphoreType.DMA((6,))],
         limit=60,
     )
     pieces = [partner(half, d) for d in others]
-    top, bottom = call(
-        ends_body,
-        "ends",
-        [(shape(4, c, lon), VMEM), (shape(4, c, lon), VMEM)],
-        [ANY, ANY, ANY],
-        (half, source, upstream),
-        scratch=[pltpu.SemaphoreType.DMA((4,))],
-        limit=60,
-    )
     above, below = edges(top, bottom)
     pieces = pl.pallas_call(
         gate_body,

time: 112 us -> 111 us (level)
  Pallas kernels: 55.3 us -> 53.6 us
    pallas_call x7 -> x6, Pallas kernels: 48.7 us -> 47.1 us  [call(): pl.pallas_call(body, name=name, out_shape=[o for o, _ in outs], in_specs=...]
    unnamed x26 -> x24, local copies, waits for them, and re-layouts: 2.37 us -> 2.39 us
  transfers between devices with their start and end apart: 15 -> 15, of which waited for: 9 -> 10; matrix products, arithmetic and copies ran while one was open for 0% -> 0% of each run, Pallas kernels for 20% -> 20%
where the time goes in v6:
time: 111 us
  Pallas kernels  53.6 us (48%)
  starting transfers between devices  27.7 us (25%)
  waiting for transfers between devices  25.9 us (23%)
  local copies, waits for them, and re-layouts  2.39 us (2%)
    pallas_call x6, Pallas kernels, call(): pl.pallas_call(body, name=name, out_shape=[o for o, _ in outs], in_specs=...  47.1 us
    ppermute x6, waiting for transfers between devices, partner(): return lax.ppermute(value, 'fsdp', [(i, i ^ d) for i in range(shards)])  19.1 us
    ppermute x6, starting transfers between devices, partner(): return lax.ppermute(value, 'fsdp', [(i, i ^ d) for i in range(shards)])  9.58 us
    pallas_call x1, Pallas kernels, per_device(): pl.pallas_call(edge_body, name='edge', out_shape=[outs[0], outs[0]], in_s...  6.53 us
    all_to_all x1, starting transfers between devices, per_device(): chunks = lax.all_to_all(chunk, 'lat', 0, 0, tiled=True)  4.86 us
    ppermute x2, starting transfers between devices, edges(): lax.ppermute(bottom, 'lat', forward)  4.83 us
    all_to_all x1, starting transfers between devices, per_device(): got = lax.all_to_all(terms, 'lat', 0, 0, tiled=True)  4.78 us
    all_to_all x1, waiting for transfers between devices, per_device(): chunks = lax.all_to_all(chunk, 'lat', 0, 0, tiled=True)  4.28 us
  transfers between devices with their start and end apart: 15, of which 10 were waited for; matrix products, arithmetic and copies ran while one was open for 0% of the time, Pallas kernels for 20%

profile of v6, /device:TPU:0, one launch (start us, length us, event | category | flops | bytes accessed | tf_op | source)
XLA Modules:
  0.0 110.5 jit_solution(11330229083771094206)
XLA Ops:
  0.6 2.6 %pack.1 = (bf16[14,48,128]{2,1,0:T(8,128)(2,1)}, bf16[14,48,128]{2,1,0:T(8,128)(2,1)}, bf16[4,192,360]{2,1,0:T(8,128)(2,1)}, bf16[4,192,360]{2,1,0:T(8,128)(2,1)}) custom-call(bf16[9,48,192]{2,1,0:T(8,128)(2,1)} %bitcast.34, bf16[9,48,192]{2,1,0:T(8,128)(2,1)} %bitcast.35, bf16[16,192,360]{2,1,0:T(8,128)(2,1)} %bitcast.24, bf16[16,192,360]{2,1,0:T(8,128)(2,1)} %bitcast.28), custom_call_target="tpu_custom_call" | custom-call | tf_op jit(solution)/shard_map/pack/pallas_call | solution.py:28
  3.3 2.4 %collective-permute-start = (bf16[4,192,360]{2,1,0:T(8,128)(2,1)}, bf16[4,192,360]{2,1,0:T(8,128)(2,1)S(1)}, u32[]{:S(2)}, u32[]{:S(2)}) collective-permute-start(bf16[4,192,360]{2,1,0:T(8,128)(2,1)} %get-tuple-element.29), channel_id=1, source_target_pairs={{0,1},{1,2},{2,3},{3,4},{4,5},{5,6},{6,7},{8,9},{9,10},{10,11},{11... | collective-permute-start | bytes 1658888 | tf_op jit(solution)/shard_map/ppermute | solution.py:437
  5.7 1.3 %collective-permute-start.1 = (bf16[4,192,360]{2,1,0:T(8,128)(2,1)}, bf16[4,192,360]{2,1,0:T(8,128)(2,1)S(1)}, u32[]{:S(2)}, u32[]{:S(2)}) collective-permute-start(bf16[4,192,360]{2,1,0:T(8,128)(2,1)} %get-tuple-element.30), channel_id=1, source_target_pairs={{1,0},{2,1},{3,2},{4,3},{5,4},{6,5},{7,6},{9,8},{10,9},{11,10},{12... | collective-permute-start | bytes 1658888 | tf_op jit(solution)/shard_map/ppermute | solution.py:437
  7.0 4.5 %collective-permute-start.4 = (bf16[14,48,128]{2,1,0:T(8,128)(2,1)}, bf16[14,48,128]{2,1,0:T(8,128)(2,1)S(1)}, u32[]{:S(2)}, u32[]{:S(2)}) collective-permute-start(bf16[14,48,128]{2,1,0:T(8,128)(2,1)} %get-tuple-element.31.refs_4_), channel_id=1, source_target_pairs={{0,24},{8,16},{16,8},{24,0},{1,25},{9,17},{17,9},{25,1},{2,26},{10... | collective-permute-start | bytes 516104 | tf_op jit(solution)/shard_map/ppermute | solution.py:440
  11.5 0.0 collective-permute-start.3
  11.5 0.6 collective-permute-start.2
  12.1 3.2 %collective-permute-done.4.refs_2_ = bf16[14,48,128]{2,1,0:T(8,128)(2,1)S(1)} collective-permute-done((bf16[14,48,128]{2,1,0:T(8,128)(2,1)}, bf16[14,48,128]{2,1,0:T(8,128)(2,1)S(1)}, u32[]{:S(2)}, u32[]{:S(2)}) %collective-permute-start.4) | collective-permute-done | bytes 172064 | tf_op jit(solution)/shard_map/ppermute | solution.py:440
  15.3 11.4 %collective-permute-done.3.refs_1_ = bf16[14,48,128]{2,1,0:T(8,128)(2,1)S(1)} collective-permute-done((bf16[14,48,128]{2,1,0:T(8,128)(2,1)}, bf16[14,48,128]{2,1,0:T(8,128)(2,1)S(1)}, u32[]{:S(2)}, u32[]{:S(2)}) %collective-permute-start.3) | collective-permute-done | bytes 172064 | tf_op jit(solution)/shard_map/ppermute | solution.py:440
  26.7 0.0 collective-permute-done.2.refs_0_
  26.7 0.0 collective-permute-done.refs_3_.refs_2_
  26.7 0.0 copy-start
  26.7 0.0 collective-permute-done.1.refs_4_.refs_3_
  26.7 0.0 copy-start.1
  26.7 0.0 copy-start.2
  26.7 0.0 copy-start.3
  26.7 0.0 copy-start.4
  26.7 0.6 collective-permute-start.5
  27.4 0.1 collective-permute-start.6
  27.4 0.4 collective-permute-start.7
  27.9 0.5 collective-permute-done.5.refs_9_
  28.4 0.0 copy-start.9
  28.4 0.4 collective-permute-done.6.refs_10_
  28.8 0.0 copy-start.10
  28.8 0.2 collective-permute-done.7.refs_11_
  29.0 0.0 copy-start.11
  29.0 0.0 copy-done
  29.0 0.0 copy-done.1
  29.0 0.0 copy-done.2
  29.0 0.0 copy-done.3
  29.0 0.0 copy-done.4
  29.0 0.0 copy-done.9
  29.1 0.4 copy-done.10
  29.4 0.2 copy-done.11
  29.7 27.9 %stage.1 = (bf16[16,192,384]{2,1,0:T(8,128)(2,1)}, bf16[16,192,384]{2,1,0:T(8,128)(2,1)}, bf16[4,192,384]{2,1,0:T(8,128)(2,1)}, bf16[4,192,384]{2,1,0:T(8,128)(2,1)}, bf16[8,4,176,128]{3,2,1,0:T(8,128)(2,1)}) custom-call(bf16[16,192,360]{2,1,0:T(8,128)(2,1)} %bitcast.25, bf16[16,192,360]{2,1,0:T(8,128)(2,1)} %bitcast.29, bf16[4,192,360]{2,1,0:T(8,128)(2,1)} %copy-done, ...), custom_call_target="tpu_custom_call" | custom-call | flops 15288238080 | bytes 16777216 | tf_op jit(solution)/shard_map/stage/pallas_call | solution.py:28
  57.6 0.0 copy-start.8
  57.6 4.8 %all-to-all-start = ((bf16[8,4,176,128]{3,2,1,0:T(8,128)(2,1)}), bf16[8,4,176,128]{3,2,1,0:T(8,128)(2,1)S(1)}, u32[]{:S(2)}, u32[]{:S(2)}) async-start(bf16[8,4,176,128]{3,2,1,0:T(8,128)(2,1)} %get-tuple-element.46), calls=%async_computation | async-start | bytes 2883584 | tf_op jit(solution)/shard_map/all_to_all | solution.py:505
  62.4 2.4 %collective-permute-start.8 = (bf16[4,192,384]{2,1,0:T(8,128)(2,1)}, bf16[4,192,384]{2,1,0:T(8,128)(2,1)S(1)}, u32[]{:S(2)}, u32[]{:S(2)}) collective-permute-start(bf16[4,192,384]{2,1,0:T(8,128)(2,1)} %get-tuple-element.38), channel_id=1, source_target_pairs={{0,1},{1,2},{2,3},{3,4},{4,5},{5,6},{6,7},{8,9},{9,10},{10,11},{11... | collective-permute-start | bytes 1769480 | tf_op jit(solution)/shard_map/ppermute | solution.py:437
  64.8 0.0 copy-done.8
  64.8 1.3 %collective-permute-start.9 = (bf16[4,192,384]{2,1,0:T(8,128)(2,1)S(1)}, bf16[4,192,384]{2,1,0:T(8,128)(2,1)S(1)}, u32[]{:S(2)}, u32[]{:S(2)}) collective-permute-start(bf16[4,192,384]{2,1,0:T(8,128)(2,1)S(1)} %copy-done.8), channel_id=1, source_target_pairs={{1,0},{2,1},{3,2},{4,3},{5,4},{6,5},{7,6},{9,8},{10,9},{11,10},{12... | collective-permute-start | bytes 1769480 | tf_op jit(solution)/shard_map/ppermute | solution.py:437
  66.1 14.4 %interior.1 = (bf16[16,192,360]{2,1,0:T(8,128)(2,1)}, bf16[16,192,360]{2,1,0:T(8,128)(2,1)}, bf16[192,1728]{1,0:T(8,128)(2,1)}, bf16[192,1728]{1,0:T(8,128)(2,1)}, f32[8,128]{1,0:T(8,128)}) custom-call(bf16[16,192,360]{2,1,0:T(8,128)(2,1)} %bitcast.26, bf16[16,192,360]{2,1,0:T(8,128)(2,1)} %bitcast.30, bf16[16,192,384]{2,1,0:T(8,128)(2,1)} %get-tuple-element.36.refs_2_.hid, ...), custom_call_target="tpu_custom_call" | custom-call | flops 7644119040 | bytes 16777216 | tf_op jit(solution)/shard_map/interior/pallas_call | solution.py:28
  80.6 1.4 %all-to-all-done.got = bf16[8,4,176,128]{3,2,1,0:T(8,128)(2,1)S(1)} async-done(((bf16[8,4,176,128]{3,2,1,0:T(8,128)(2,1)}), bf16[8,4,176,128]{3,2,1,0:T(8,128)(2,1)S(1)}, u32[]{:S(2)}, u32[]{:S(2)}) %all-to-all-start) | async-done | bytes 1441824 | tf_op jit(solution)/shard_map/all_to_all | solution.py:505
  82.0 0.0 copy-start.5
  82.0 0.7 copy-done.5
  82.7 0.2 column.1
  82.9 0.1 collective-permute-start.10
  82.9 3.0 %collective-permute-start.11 = (bf16[176,128]{1,0:T(8,128)(2,1)S(1)}, bf16[176,128]{1,0:T(8,128)(2,1)S(1)}, u32[]{:S(2)}, u32[]{:S(2)}) collective-permute-start(bf16[176,128]{1,0:T(8,128)(2,1)S(1)} %get-tuple-element.50), channel_id=1, source_target_pairs={{0,16},{8,24},{16,0},{24,8},{1,17},{9,25},{17,1},{25,9},{2,18},{10... | collective-permute-start | bytes 135176 | tf_op jit(solution)/shard_map/ppermute | solution.py:440
  86.0 1.3 %collective-permute-start.12 = (bf16[176,128]{1,0:T(8,128)(2,1)S(1)}, bf16[176,128]{1,0:T(8,128)(2,1)S(1)}, u32[]{:S(2)}, u32[]{:S(2)}) collective-permute-start(bf16[176,128]{1,0:T(8,128)(2,1)S(1)} %get-tuple-element.51), channel_id=1, source_target_pairs={{0,24},{8,16},{16,8},{24,0},{1,25},{9,17},{17,9},{25,1},{2,26},{10... | collective-permute-start | bytes 135176 | tf_op jit(solution)/shard_map/ppermute | solution.py:440
  87.3 0.1 collective-permute-done.10.refs_0_
  87.4 1.1 collective-permute-done.11.refs_1_
  88.5 3.4 %collective-permute-done.12.refs_2_ = bf16[176,128]{1,0:T(8,128)(2,1)S(1)} collective-permute-done((bf16[176,128]{1,0:T(8,128)(2,1)S(1)}, bf16[176,128]{1,0:T(8,128)(2,1)S(1)}, u32[]{:S(2)}, u32[]{:S(2)}) %collective-permute-start.12) | collective-permute-done | bytes 45088 | tf_op jit(solution)/shard_map/ppermute | solution.py:440
  91.8 0.9 chunk.1
  92.8 4.9 %all-to-all-start.1 = ((f32[8,176,128]{2,1,0:T(8,128)}), f32[8,176,128]{2,1,0:T(8,128)S(1)}, u32[]{:S(2)}, u32[]{:S(2)}) async-start(f32[8,176,128]{2,1,0:T(8,128)} %chunk.1), calls=%async_computation.1 | async-start | bytes 1441792 | tf_op jit(solution)/shard_map/all_to_all | solution.py:538
  97.6 0.0 collective-permute-done.8.above_in
  97.6 0.0 copy-start.6
  97.7 0.0 collective-permute-done.9.below_in
  97.7 0.0 copy-start.7
  97.7 0.8 copy-done.6
  98.5 0.3 copy-done.7
  98.7 6.5 %edge.1 = (bf16[16,192,360]{2,1,0:T(8,128)(2,1)}, bf16[16,192,360]{2,1,0:T(8,128)(2,1)}) custom-call(bf16[16,192,360]{2,1,0:T(8,128)(2,1)} %bitcast.27, bf16[16,192,360]{2,1,0:T(8,128)(2,1)} %bitcast.31, bf16[16,192,384]{2,1,0:T(8,128)(2,1)} %get-tuple-element.36.refs_2_.hid, ...), custom_call_target="tpu_custom_call", output_to_operand_aliasing={{0}: (8, {}), {1}: (9, {})} | custom-call | flops 1911029760 | bytes 4194304 | tf_op jit(solution)/shard_map/edge/pallas_call | solution.py:539
  105.3 4.3 %all-to-all-done.1.chunks = f32[8,176,128]{2,1,0:T(8,128)S(1)} async-done(((f32[8,176,128]{2,1,0:T(8,128)}), f32[8,176,128]{2,1,0:T(8,128)S(1)}, u32[]{:S(2)}, u32[]{:S(2)}) %all-to-all-start.1) | async-done | bytes 720928 | tf_op jit(solution)/shard_map/all_to_all | solution.py:538
  109.5 1.0 unpack.1
  (1 shorter events, 0.0 us)
Async XLA Ops:
  3.3 23.4 %collective-permute-start = (bf16[4,192,360]{2,1,0:T(8,128)(2,1)}, bf16[4,192,360]{2,1,0:T(8,128)(2,1)S(1)}, u32[]{:S(2)}, u32[]{:S(2)}) collective-permute-start(bf16[4,192,360]{2,1,0:T(8,128)(2,1)} %get-tuple-element.29), channel_id=1, source_target_pairs={{0,1},{1,2},{2,3},{3,4},{4,5},{5,6},{6,7},{8,9},{9,10},{10,11},{11... | collective-permute-start | bytes 1658888 | tf_op jit(solution)/shard_map/ppermute | solution.py:437
  5.7 21.0 %collective-permute-start.1 = (bf16[4,192,360]{2,1,0:T(8,128)(2,1)}, bf16[4,192,360]{2,1,0:T(8,128)(2,1)S(1)}, u32[]{:S(2)}, u32[]{:S(2)}) collective-permute-start(bf16[4,192,360]{2,1,0:T(8,128)(2,1)} %get-tuple-element.30), channel_id=1, source_target_pairs={{1,0},{2,1},{3,2},{4,3},{5,4},{6,5},{7,6},{9,8},{10,9},{11,10},{12... | collective-permute-start | bytes 1658888 | tf_op jit(solution)/shard_map/ppermute | solution.py:437
  7.0 8.3 %collective-permute-start.4 = (bf16[14,48,128]{2,1,0:T(8,128)(2,1)}, bf16[14,48,128]{2,1,0:T(8,128)(2,1)S(1)}, u32[]{:S(2)}, u32[]{:S(2)}) collective-permute-start(bf16[14,48,128]{2,1,0:T(8,128)(2,1)} %get-tuple-element.31.refs_4_), channel_id=1, source_target_pairs={{0,24},{8,16},{16,8},{24,0},{1,25},{9,17},{17,9},{25,1},{2,26},{10... | collective-permute-start | bytes 516104 | tf_op jit(solution)/shard_map/ppermute | solution.py:440
  11.5 15.2 %collective-permute-start.3 = (bf16[14,48,128]{2,1,0:T(8,128)(2,1)}, bf16[14,48,128]{2,1,0:T(8,128)(2,1)S(1)}, u32[]{:S(2)}, u32[]{:S(2)}) collective-permute-start(bf16[14,48,128]{2,1,0:T(8,128)(2,1)} %get-tuple-element.31.refs_4_), channel_id=1, source_target_pairs={{0,16},{8,24},{16,0},{24,8},{1,17},{9,25},{17,1},{25,9},{2,18},{10... | collective-permute-start | bytes 516104 | tf_op jit(solution)/shard_map/ppermute | solution.py:440
  11.5 15.2 %collective-permute-start.2 = (bf16[14,48,128]{2,1,0:T(8,128)(2,1)}, bf16[14,48,128]{2,1,0:T(8,128)(2,1)S(1)}, u32[]{:S(2)}, u32[]{:S(2)}) collective-permute-start(bf16[14,48,128]{2,1,0:T(8,128)(2,1)} %get-tuple-element.31.refs_4_), channel_id=1, source_target_pairs={{0,8},{8,0},{16,24},{24,16},{1,9},{9,1},{17,25},{25,17},{2,10},{10... | collective-permute-start | bytes 516104 | tf_op jit(solution)/shard_map/ppermute | solution.py:440
  26.7 2.3 %copy-start = (bf16[4,192,360]{2,1,0:T(8,128)(2,1)}, bf16[4,192,360]{2,1,0:T(8,128)(2,1)S(1)}, u32[]{:S(2)}) copy-start(bf16[4,192,360]{2,1,0:T(8,128)(2,1)S(1)} %collective-permute-done.refs_3_.refs_2_) | copy-start | bytes 1658884
  26.7 2.3 %copy-start.1 = (bf16[4,192,360]{2,1,0:T(8,128)(2,1)}, bf16[4,192,360]{2,1,0:T(8,128)(2,1)S(1)}, u32[]{:S(2)}) copy-start(bf16[4,192,360]{2,1,0:T(8,128)(2,1)S(1)} %collective-permute-done.1.refs_4_.refs_3_) | copy-start | bytes 1658884
  26.7 2.3 %copy-start.2 = (bf16[14,48,128]{2,1,0:T(8,128)(2,1)}, bf16[14,48,128]{2,1,0:T(8,128)(2,1)S(1)}, u32[]{:S(2)}) copy-start(bf16[14,48,128]{2,1,0:T(8,128)(2,1)S(1)} %get-tuple-element.34.refs_7_) | copy-start | bytes 516100
  26.7 2.3 %copy-start.3 = (bf16[14,48,128]{2,1,0:T(8,128)(2,1)}, bf16[14,48,128]{2,1,0:T(8,128)(2,1)S(1)}, u32[]{:S(2)}) copy-start(bf16[14,48,128]{2,1,0:T(8,128)(2,1)S(1)} %get-tuple-element.33.refs_6_) | copy-start | bytes 516100
  26.7 2.3 %copy-start.4 = (bf16[14,48,128]{2,1,0:T(8,128)(2,1)}, bf16[14,48,128]{2,1,0:T(8,128)(2,1)S(1)}, u32[]{:S(2)}) copy-start(bf16[14,48,128]{2,1,0:T(8,128)(2,1)S(1)} %get-tuple-element.32.refs_5_) | copy-start | bytes 516100
  26.7 1.6 %collective-permute-start.5 = (bf16[14,48,128]{2,1,0:T(8,128)(2,1)S(1)}, bf16[14,48,128]{2,1,0:T(8,128)(2,1)S(1)}, u32[]{:S(2)}, u32[]{:S(2)}) collective-permute-start(bf16[14,48,128]{2,1,0:T(8,128)(2,1)S(1)} %get-tuple-element.32.refs_5_), channel_id=1, source_target_pairs={{0,1},{1,0},{2,3},{3,2},{4,5},{5,4},{6,7},{7,6},{8,9},{9,8},{10,11... | collective-permute-start | bytes 516104 | tf_op jit(solution)/shard_map/ppermute | solution.py:472
  27.4 1.4 %collective-permute-start.6 = (bf16[14,48,128]{2,1,0:T(8,128)(2,1)S(1)}, bf16[14,48,128]{2,1,0:T(8,128)(2,1)S(1)}, u32[]{:S(2)}, u32[]{:S(2)}) collective-permute-start(bf16[14,48,128]{2,1,0:T(8,128)(2,1)S(1)} %get-tuple-element.33.refs_6_), channel_id=1, source_target_pairs={{0,1},{1,0},{2,3},{3,2},{4,5},{5,4},{6,7},{7,6},{8,9},{9,8},{10,11... | collective-permute-start | bytes 516104 | tf_op jit(solution)/shard_map/ppermute | solution.py:472
  27.4 1.6 %collective-permute-start.7 = (bf16[14,48,128]{2,1,0:T(8,128)(2,1)S(1)}, bf16[14,48,128]{2,1,0:T(8,128)(2,1)S(1)}, u32[]{:S(2)}, u32[]{:S(2)}) collective-permute-start(bf16[14,48,128]{2,1,0:T(8,128)(2,1)S(1)} %get-tuple-element.34.refs_7_), channel_id=1, source_target_pairs={{0,1},{1,0},{2,3},{3,2},{4,5},{5,4},{6,7},{7,6},{8,9},{9,8},{10,11... | collective-permute-start | bytes 516104 | tf_op jit(solution)/shard_map/ppermute | solution.py:472
  28.4 0.7 copy-start.9
  28.8 0.7 copy-start.10
  29.0 0.7 copy-start.11
  57.6 7.2 %copy-start.8 = (bf16[4,192,384]{2,1,0:T(8,128)(2,1)S(1)}, bf16[4,192,384]{2,1,0:T(8,128)(2,1)}, u32[]{:S(2)}) copy-start(bf16[4,192,384]{2,1,0:T(8,128)(2,1)} %get-tuple-element.39) | copy-start | bytes 1769476
  57.6 24.4 %all-to-all-start = ((bf16[8,4,176,128]{3,2,1,0:T(8,128)(2,1)}), bf16[8,4,176,128]{3,2,1,0:T(8,128)(2,1)S(1)}, u32[]{:S(2)}, u32[]{:S(2)}) async-start(bf16[8,4,176,128]{3,2,1,0:T(8,128)(2,1)} %get-tuple-element.46), calls=%async_computation | async-start | bytes 2883584 | tf_op jit(solution)/shard_map/all_to_all | solution.py:505
  62.4 35.3 %collective-permute-start.8 = (bf16[4,192,384]{2,1,0:T(8,128)(2,1)}, bf16[4,192,384]{2,1,0:T(8,128)(2,1)S(1)}, u32[]{:S(2)}, u32[]{:S(2)}) collective-permute-start(bf16[4,192,384]{2,1,0:T(8,128)(2,1)} %get-tuple-element.38), channel_id=1, source_target_pairs={{0,1},{1,2},{2,3},{3,4},{4,5},{5,6},{6,7},{8,9},{9,10},{10,11},{11... | collective-permute-start | bytes 1769480 | tf_op jit(solution)/shard_map/ppermute | solution.py:437
  64.8 32.8 %collective-permute-start.9 = (bf16[4,192,384]{2,1,0:T(8,128)(2,1)S(1)}, bf16[4,192,384]{2,1,0:T(8,128)(2,1)S(1)}, u32[]{:S(2)}, u32[]{:S(2)}) collective-permute-start(bf16[4,192,384]{2,1,0:T(8,128)(2,1)S(1)} %copy-done.8), channel_id=1, source_target_pairs={{1,0},{2,1},{3,2},{4,3},{5,4},{6,5},{7,6},{9,8},{10,9},{11,10},{12... | collective-permute-start | bytes 1769480 | tf_op jit(solution)/shard_map/ppermute | solution.py:437
  82.0 0.7 copy-start.5
  82.9 4.5 %collective-permute-start.10 = (bf16[176,128]{1,0:T(8,128)(2,1)S(1)}, bf16[176,128]{1,0:T(8,128)(2,1)S(1)}, u32[]{:S(2)}, u32[]{:S(2)}) collective-permute-start(bf16[176,128]{1,0:T(8,128)(2,1)S(1)} %get-tuple-element.49), channel_id=1, source_target_pairs={{0,8},{8,0},{16,24},{24,16},{1,9},{9,1},{17,25},{25,17},{2,10},{10... | collective-permute-start | bytes 135176 | tf_op jit(solution)/shard_map/ppermute | solution.py:440
  82.9 5.5 %collective-permute-start.11 = (bf16[176,128]{1,0:T(8,128)(2,1)S(1)}, bf16[176,128]{1,0:T(8,128)(2,1)S(1)}, u32[]{:S(2)}, u32[]{:S(2)}) collective-permute-start(bf16[176,128]{1,0:T(8,128)(2,1)S(1)} %get-tuple-element.50), channel_id=1, source_target_pairs={{0,16},{8,24},{16,0},{24,8},{1,17},{9,25},{17,1},{25,9},{2,18},{10... | collective-permute-start | bytes 135176 | tf_op jit(solution)/shard_map/ppermute | solution.py:440
  86.0 5.8 %collective-permute-start.12 = (bf16[176,128]{1,0:T(8,128)(2,1)S(1)}, bf16[176,128]{1,0:T(8,128)(2,1)S(1)}, u32[]{:S(2)}, u32[]{:S(2)}) collective-permute-start(bf16[176,128]{1,0:T(8,128)(2,1)S(1)} %get-tuple-element.51), channel_id=1, source_target_pairs={{0,24},{8,16},{16,8},{24,0},{1,25},{9,17},{17,9},{25,1},{2,26},{10... | collective-permute-start | bytes 135176 | tf_op jit(solution)/shard_map/ppermute | solution.py:440
  92.8 16.8 %all-to-all-start.1 = ((f32[8,176,128]{2,1,0:T(8,128)}), f32[8,176,128]{2,1,0:T(8,128)S(1)}, u32[]{:S(2)}, u32[]{:S(2)}) async-start(f32[8,176,128]{2,1,0:T(8,128)} %chunk.1), calls=%async_computation.1 | async-start | bytes 1441792 | tf_op jit(solution)/shard_map/all_to_all | solution.py:538
  97.6 0.8 copy-start.6
  97.7 1.1 copy-start.7
